TPU v7x, 32 devices: a whole 2x2x4 slice. The times are simulated.
32 devices in a mesh: orbit: 8 (over y, x, core), tile: 4 (over z).
Axes of the slice: x: 2, y: 2, z: 4, core: 2. Of those that a mesh axis runs over, the one named last changes fastest.
Arguments:
- tokens: bfloat16 [32, 256, 1280], P('orbit', 'tile'), may hold values from -6 to 6
- cotangent: bfloat16 [32, 256, 1280], P('orbit', 'tile'), may hold values from -60 to 60
- w_query: bfloat16 [1280, 1280], replicated, may hold values from -0.15625 to 0.15625
- w_key: bfloat16 [1280, 1280], replicated, may hold values from -0.15625 to 0.15625
- w_value: bfloat16 [1280, 1280], replicated, may hold values from -0.15625 to 0.15625
- conv_taps: float32 [3, 1280], replicated, may hold values from 0.3 to 1
- conv_bias: float32 [1280], replicated, may hold values from -2 to 2
Outputs:
- grad_tokens: bfloat16 [32, 256, 1280], P('orbit', 'tile')
All inputs are finite; a program needn't handle non-finite values.
Results may differ from a plain program's by a relative error of at most 0.009.
The roundings to bfloat16 on the way count: a program that leaves them out, or rounds other values in their place, can miss the bound.
Values may be sent and summed in bfloat16 or wider, within the bound.
No kernel may reach another device: no remote copies, remote signals or barrier semaphores. Data moves between devices by JAX's collectives and lax.ppermute only.
A program may use at most 64 MiB of HBM per device.

v0:
```python
import functools
import math

import jax
import jax.numpy as jnp
from jax import lax
from jax.experimental import pallas as pl
from jax.experimental.pallas import tpu as pltpu
from jax.sharding import PartitionSpec as P


HEAD_DIM = 64
LANES = 128
BLOCK = 256
NT = (((1,), (1,)), ((), ()))
TN = (((0,), (0,)), ((), ()))


def iota(shape, dim):
    return lax.broadcasted_iota(jnp.int32, shape, dim)


def reorder_matrix(frames, toks, to_token_major):
    rows = frames * toks
    out_row = iota((rows, rows), 0)
    in_row = iota((rows, rows), 1)
    if to_token_major:
        source = (out_row % frames) * toks + out_row // frames
    else:
        source = (out_row % toks) * frames + out_row // toks
    return (in_row == source).astype(jnp.float32).astype(jnp.bfloat16)


def half_masks(rows):
    low = (iota((rows, LANES), 1) < HEAD_DIM).astype(jnp.float32)
    return low.astype(jnp.bfloat16), (1.0 - low).astype(jnp.bfloat16)


def split_pair(block, masks):
    return jnp.concatenate([block * masks[0], block * masks[1]], axis=0)


def compact(full, frames):
    token_of = iota((frames, LANES), 1) // frames
    kept = full[:frames]
    for tok in range(1, LANES // frames):
        kept = jnp.where(token_of == tok, full[tok * frames:(tok + 1) * frames], kept)
    return kept


def expand(kept, token_masks):
    return jnp.concatenate([kept * mask for mask in token_masks], axis=0)


def pack_kernel(me_ref, tokens_ref, cotangent_ref, *refs, peers):
    outs = refs[:peers // 2]
    energy_ref, held_ref, sems = refs[peers // 2:]
    me = me_ref[0]
    frame_rows = held_ref.shape[0]
    frame_copies = [
        pltpu.make_async_copy(cotangent_ref.at[frame], held_ref.at[frame], sems.at[peers + frame])
        for frame in range(frame_rows)
    ]
    copies = [
        pltpu.make_async_copy(
            tokens_ref.at[:, me ^ mask], outs[mask // 2].at[mask % 2], sems.at[mask]
        )
        for mask in range(peers)
    ]
    for copy in frame_copies + copies:
        copy.start()
    for frame in range(frame_rows):
        frame_copies[frame].wait()
        total = jnp.zeros(held_ref.shape[2:], jnp.float32)
        for group in range(peers):
            grad = held_ref[frame, group].astype(jnp.float32)
            total += grad * grad
        energy_ref[frame:frame + 1, :] = jnp.broadcast_to(
            jnp.sum(total, keepdims=True), (1, LANES)
        )
    for copy in copies:
        copy.wait()


def scale_kernel(me_ref, energy_ref, other_ref, cotangent_ref, *outs, peers, count):
    me = me_ref[0]
    factor = lax.rsqrt((energy_ref[...] + other_ref[...]) / count + 1e-06)
    frame_rows = cotangent_ref.shape[0]
    for mask in range(peers):
        for frame in range(frame_rows):
            grad = cotangent_ref[frame, me ^ mask].astype(jnp.float32)
            outs[mask // 2][mask % 2, frame] = (
                grad * factor[frame:frame + 1, :1]
            ).astype(jnp.bfloat16)


def load_kernel(*refs):
    count = len(refs) // 2
    sems = refs[-1]
    copies = [pltpu.make_async_copy(refs[i], refs[count + i], sems.at[i]) for i in range(count)]
    for copy in copies:
        copy.start()
    for copy in copies:
        copy.wait()


def place_kernel(me_ref, *refs, peers):
    blocks = refs[:peers]
    out_ref, sems = refs[peers:]
    me = me_ref[0]
    copies = [
        pltpu.make_async_copy(blocks[mask], out_ref.at[:, me ^ mask], sems.at[mask])
        for mask in range(peers)
    ]
    for copy in copies:
        copy.start()
    for copy in copies:
        copy.wait()


def block_of(blocks, mask):
    block = blocks[mask][...]
    return block[0] if mask % 2 == 0 else block


def forward_kernel(me_ref, taps_ref, bias_ref, wq_ref, wk_ref, wv_ref, *refs, frames, toks, peers):
    blocks = refs[:peers]
    q_ref, k_ref, v_ref, prob_ref, source_ref, hidden_ref = refs[peers:]
    rows, channels = hidden_ref.shape
    part = rows // peers
    me = me_ref[0]
    for mask in range(peers):
        start = pl.multiple_of((me ^ mask) * part, part)
        source_ref[pl.ds(start, part), :] = block_of(blocks, mask).astype(jnp.float32)
    order = reorder_matrix(frames, toks, True)
    for col in range(0, channels, BLOCK):
        cols = slice(col, col + BLOCK)
        source = source_ref[:, cols]
        mixed = (
            taps_ref[0:1, cols] * pltpu.roll(source, toks, 0)
            + taps_ref[1:2, cols] * source
            + taps_ref[2:3, cols] * pltpu.roll(source, rows - toks, 0)
        )
        hidden = (source + mixed + bias_ref[cols].reshape(1, BLOCK)).astype(jnp.bfloat16)
        hidden_ref[:, cols] = jnp.dot(
            order, hidden, preferred_element_type=jnp.float32
        ).astype(jnp.bfloat16)

    masks = half_masks(LANES)
    inv_root = 1.0 / math.sqrt(HEAD_DIM)
    for col in range(0, channels, BLOCK):
        block = slice(col, col + BLOCK)
        for weight_ref, out_ref in ((wq_ref, q_ref), (wk_ref, k_ref), (wv_ref, v_ref)):
            out_ref[:, block] = jnp.dot(
                hidden_ref[...], weight_ref[:, block], preferred_element_type=jnp.float32
            ).astype(jnp.bfloat16)
        for start in range(col, col + BLOCK, LANES):
            cols = slice(start, start + LANES)
            for row in range(0, rows, LANES):
                here = slice(row, row + LANES)
                full = lax.dot_general(
                    split_pair(k_ref[here, cols], masks), q_ref[here, cols],
                    NT, preferred_element_type=jnp.float32,
                )
                for head in range(2):
                    scores = compact(full[head * LANES:(head + 1) * LANES], frames) * inv_root
                    expo = jnp.exp(scores - jnp.max(scores, axis=0, keepdims=True))
                    inverse = 1.0 / jnp.sum(expo, axis=0, keepdims=True)
                    prob_ref[start // HEAD_DIM + head, :, here] = expo * inverse


def backward_kernel(me_ref, taps_ref, wq_ref, wk_ref, wv_ref, q_ref, k_ref, v_ref, prob_ref,
                    *refs, frames, toks, peers):
    blocks = refs[:peers]
    outs = refs[peers:2 * peers]
    grad_ref, left_ref, result_ref = refs[2 * peers:]
    rows, channels = grad_ref.shape
    part = rows // peers
    me = me_ref[0]
    for mask in range(peers):
        start = pl.multiple_of((me ^ mask) * part, part)
        result_ref[pl.ds(start, part), :] = block_of(blocks, mask)
    order = reorder_matrix(frames, toks, True)
    for col in range(0, channels, BLOCK):
        cols = slice(col, col + BLOCK)
        grad_ref[:, cols] = jnp.dot(
            order, result_ref[:, cols], preferred_element_type=jnp.float32
        ).astype(jnp.bfloat16)

    masks = half_masks(LANES)
    token_of = iota((frames, LANES), 1) // frames
    token_masks = [
        (token_of == tok).astype(jnp.float32).astype(jnp.bfloat16) for tok in range(LANES // frames)
    ]
    inv_root = 1.0 / math.sqrt(HEAD_DIM)
    for start in range(0, channels, LANES):
        cols = slice(start, start + LANES)
        for row in range(0, rows, LANES):
            here = slice(row, row + LANES)
            g_pair = grad_ref[here, cols]
            full = lax.dot_general(
                split_pair(v_ref[here, cols], masks), g_pair, NT, preferred_element_type=jnp.float32
            )
            prob_wide, score_wide = [], []
            for head in range(2):
                prob = prob_ref[start // HEAD_DIM + head, :, here]
                prob_low = prob.astype(jnp.bfloat16)
                grad_prob = compact(full[head * LANES:(head + 1) * LANES], frames)
                delta = jnp.sum(prob_low.astype(jnp.float32) * grad_prob, axis=0, keepdims=True)
                d_scores = (prob * (grad_prob - delta)).astype(jnp.bfloat16)
                prob_wide.append(expand(prob_low, token_masks))
                score_wide.append(expand(d_scores, token_masks))
            left_ref[0, here, cols] = (lax.dot_general(
                jnp.concatenate(score_wide, axis=0), split_pair(k_ref[here, cols], masks),
                TN, preferred_element_type=jnp.float32,
            ) * inv_root).astype(jnp.bfloat16)
            left_ref[1, here, cols] = (jnp.dot(
                jnp.concatenate(score_wide, axis=1), split_pair(q_ref[here, cols], masks),
                preferred_element_type=jnp.float32,
            ) * inv_root).astype(jnp.bfloat16)
            left_ref[2, here, cols] = jnp.dot(
                jnp.concatenate(prob_wide, axis=1), split_pair(g_pair, masks),
                preferred_element_type=jnp.float32,
            ).astype(jnp.bfloat16)

    order = reorder_matrix(frames, toks, False)
    for col in range(0, channels, BLOCK):
        cols = slice(col, col + BLOCK)
        total = sum(
            lax.dot_general(left_ref[index], weight_ref[cols, :], NT, preferred_element_type=jnp.float32)
            for index, weight_ref in enumerate((wq_ref, wk_ref, wv_ref))
        )
        source = jnp.dot(order, total.astype(jnp.bfloat16), preferred_element_type=jnp.float32)
        result_ref[:, cols] = (
            source
            + taps_ref[0:1, cols] * pltpu.roll(source, rows - toks, 0)
            + taps_ref[1:2, cols] * source
            + taps_ref[2:3, cols] * pltpu.roll(source, toks, 0)
        ).astype(jnp.bfloat16)
    for mask in range(peers):
        start = pl.multiple_of((me ^ mask) * part, part)
        outs[mask][...] = result_ref[pl.ds(start, part), :]


def swap(value, axis, mask):
    return lax.ppermute(value, axis, [(i, i ^ mask) for i in range(lax.axis_size(axis))])


def grant(mebibytes):
    return pltpu.CompilerParams(vmem_limit_bytes=mebibytes << 20)


def on_chip(value):
    return pltpu.with_memory_space_constraint(value, pltpu.VMEM)


def off_chip(value):
    return pltpu.with_memory_space_constraint(value, pltpu.HBM)


def far_first(peers):
    return sorted(range(1, peers), key=lambda mask: (-bin(mask >> 1).count("1"), -mask))


def gather_tokens(sent):
    peers = lax.axis_size("orbit")
    _, frame_rows, toks, channels = sent[0].shape
    parts = [sent[0]] + [None] * (peers // 2 - 1)
    for mask in far_first(peers):
        if mask % 2 == 0:
            parts[mask // 2] = swap(sent[mask // 2], "orbit", mask)
    blocks = []
    for chip in range(peers // 2):
        pair = parts[chip].reshape(2, frame_rows * toks, channels)
        mine = pair[1]
        blocks += [pair, swap(mine, "orbit", 1)]
    return blocks


def spread_frames(blocks):
    peers = len(blocks)
    received = [blocks[0]] + [None] * (peers - 1)
    for mask in far_first(peers):
        received[mask] = swap(blocks[mask], "orbit", mask)
    return received


def tile_sum(value):
    mask = 1
    other = jnp.zeros_like(value)
    while mask < lax.axis_size("tile"):
        value = value + other if mask > 1 else value
        other = swap(value, "tile", mask)
        mask *= 2
    return value, other


def body(tokens, cotangent, w_query, w_key, w_value, conv_taps, conv_bias):
    frame_rows, tile_rows, channels = tokens.shape
    peers = lax.axis_size("orbit")
    me = lax.axis_index("orbit")
    frames = frame_rows * peers
    toks = tile_rows // peers
    rows = frames * toks
    part = frame_rows * toks
    spatial_all = tile_rows * lax.axis_size("tile")
    heads = channels // HEAD_DIM
    me_arg = me.astype(jnp.int32).reshape(1)
    smem = pl.BlockSpec(memory_space=pltpu.SMEM)
    vmem = pl.BlockSpec(memory_space=pltpu.VMEM)
    hbm = pl.BlockSpec(memory_space=pltpu.HBM)
    low = functools.partial(pltpu.VMEM, dtype=jnp.bfloat16)
    sent_shape = low((2, frame_rows, toks, channels))
    split = (frame_rows, peers, toks, channels)

    *sent_tokens, energy, held = pl.pallas_call(
        functools.partial(pack_kernel, peers=peers),
        in_specs=[smem, hbm, hbm],
        out_specs=[vmem] * (peers // 2 + 2),
        out_shape=[sent_shape] * (peers // 2)
        + [pltpu.VMEM((frame_rows, LANES), jnp.float32), low(split)],
        scratch_shapes=[pltpu.SemaphoreType.DMA((peers + frame_rows,))],
        compiler_params=grant(8),
        name="pack",
    )(me_arg, off_chip(tokens.reshape(split)), off_chip(cotangent.reshape(split)))
    energy_here, energy_there = tile_sum(energy)
    token_blocks = gather_tokens(sent_tokens)
    sent_grads = pl.pallas_call(
        functools.partial(scale_kernel, peers=peers, count=spatial_all * channels),
        in_specs=[smem, vmem, vmem, vmem],
        out_specs=[vmem] * (peers // 2),
        out_shape=[sent_shape] * (peers // 2),
        compiler_params=grant(8),
        name="scale",
    )(me_arg, on_chip(energy_here), on_chip(energy_there), on_chip(held))
    grad_blocks = gather_tokens(sent_grads)

    parameters = (conv_taps, conv_bias, w_query, w_key, w_value)
    conv_taps, conv_bias, *weights = map(on_chip, pl.pallas_call(
        load_kernel,
        in_specs=[hbm] * len(parameters),
        out_specs=[vmem] * len(parameters),
        out_shape=[pltpu.VMEM(value.shape, value.dtype) for value in parameters],
        scratch_shapes=[pltpu.SemaphoreType.DMA((len(parameters),))],
        compiler_params=grant(4),
        name="load",
    )(*map(off_chip, parameters)))
    sizes = dict(frames=frames, toks=toks, peers=peers)
    query, key, value, prob = pl.pallas_call(
        functools.partial(forward_kernel, **sizes),
        in_specs=[smem] + [vmem] * (5 + peers),
        out_specs=[vmem] * 4,
        out_shape=[low((rows, channels))] * 3 + [pltpu.VMEM((heads, frames, rows), jnp.float32)],
        scratch_shapes=[
            pltpu.VMEM((rows, channels), jnp.float32), pltpu.VMEM((rows, channels), jnp.bfloat16)
        ],
        compiler_params=grant(20),
        name="forward",
    )(me_arg, conv_taps, conv_bias, *weights, *map(on_chip, token_blocks))
    results = pl.pallas_call(
        functools.partial(backward_kernel, **sizes),
        in_specs=[smem] + [vmem] * (8 + peers),
        out_specs=[vmem] * peers,
        out_shape=[low((part, channels))] * peers,
        scratch_shapes=[
            pltpu.VMEM((rows, channels), jnp.bfloat16),
            pltpu.VMEM((3, rows, channels), jnp.bfloat16),
            pltpu.VMEM((rows, channels), jnp.bfloat16),
        ],
        compiler_params=grant(20),
        name="backward",
    )(me_arg, conv_taps, *weights, *map(on_chip, (query, key, value, prob)), *map(on_chip, grad_blocks))
    received = [block.reshape(frame_rows, toks, channels) for block in spread_frames(results)]
    output = pl.pallas_call(
        functools.partial(place_kernel, peers=peers),
        in_specs=[smem] + [vmem] * peers,
        out_specs=hbm,
        out_shape=jax.ShapeDtypeStruct(split, jnp.bfloat16),
        scratch_shapes=[pltpu.SemaphoreType.DMA((peers,))],
        compiler_params=grant(4),
        name="place",
    )(me_arg, *map(on_chip, received))
    return output.reshape(frame_rows, tile_rows, channels)


def solution(mesh):
    in_specs = (P("orbit", "tile", None), P("orbit", "tile", None), P(), P(), P(), P(), P())
    out_specs = P("orbit", "tile", None)
    return jax.shard_map(body, mesh=mesh, in_specs=in_specs, out_specs=out_specs, check_vma=False)
```

profile of v0, /device:TPU:0, one launch (start us, length us, event | category | flops | bytes accessed | tf_op | source)
XLA Modules:
  0.0 55.5 jit_solution(10328954007531259278)
XLA Ops:
  0.0 1.6 %pack.1 = (bf16[2,4,8,1280]{3,2,1,0:T(8,128)(2,1)S(1)}, bf16[2,4,8,1280]{3,2,1,0:T(8,128)(2,1)S(1)}, bf16[2,4,8,1280]{3,2,1,0:T(8,128)(2,1)S(1)}, bf16[2,4,8,128...) custom-call(s32[1]{0:T(128)} %bitcast.me_ref, bf16[4,8,8,1280]{3,2,1,0:T(8,128)(2,1)} %bitcast.52, ...), custom_call_target="tpu_custom_call" | custom-call | tf_op jit(solution)/shard_map/pack/pallas_call | solution.py:316
  1.6 3.1 %collective-permute-start.7 = (f32[4,128]{1,0:T(4,128)S(1)}, f32[4,128]{1,0:T(4,128)S(1)}, u32[]{:S(2)}, u32[]{:S(2)}) collective-permute-start(f32[4,128]{1,0:T(4,128)S(1)} %get-tuple-element.45), channel_id=1, source_target_pairs={{0,1},{1,0},{2,3},{3,2},{4,5},{5,4},{6,7},{7,6},{8,9},{9,8},{10,11... | collective-permute-start | bytes 6152 | tf_op jit(solution)/shard_map/ppermute | solution.py:246
  4.7 1.5 %collective-permute-start.1 = (bf16[2,4,8,1280]{3,2,1,0:T(8,128)(2,1)S(1)}, bf16[2,4,8,1280]{3,2,1,0:T(8,128)(2,1)S(1)}, u32[]{:S(2)}, u32[]{:S(2)}) collective-permute-start(bf16[2,4,8,1280]{3,2,1,0:T(8,128)(2,1)S(1)} %get-tuple-element.38), channel_id=1, source_target_pairs={{0,8},{4,12},{8,0},{12,4},{16,24},{20,28},{24,16},{28,20},{1,9},{5... | collective-permute-start | bytes 491528 | tf_op jit(solution)/shard_map/ppermute | solution.py:246
  6.2 1.5 %collective-permute-start.3 = (bf16[2,4,8,1280]{3,2,1,0:T(8,128)(2,1)S(1)}, bf16[2,4,8,1280]{3,2,1,0:T(8,128)(2,1)S(1)}, u32[]{:S(2)}, u32[]{:S(2)}) collective-permute-start(bf16[2,4,8,1280]{3,2,1,0:T(8,128)(2,1)S(1)} %get-tuple-element.39), channel_id=1, source_target_pairs={{0,16},{4,20},{8,24},{12,28},{16,0},{20,4},{24,8},{28,12},{1,17},{... | collective-permute-start | bytes 491528 | tf_op jit(solution)/shard_map/ppermute | solution.py:246
  7.7 0.5 collective-permute-start.5
  8.2 2.6 %collective-permute-start.8 = (f32[4,128]{1,0:T(4,128)S(1)}, f32[4,128]{1,0:T(4,128)S(1)}, u32[]{:S(2)}, u32[]{:S(2)}) collective-permute-start(f32[4,128]{1,0:T(4,128)S(1)} %add.3.energy_ref), channel_id=1, source_target_pairs={{0,2},{1,3},{2,0},{3,1},{4,6},{5,7},{6,4},{7,5},{8,10},{9,11},{10,... | collective-permute-start | bytes 6152 | tf_op jit(solution)/shard_map/ppermute | solution.py:246
  10.8 1.9 %collective-permute-done.8.other_ref = f32[4,128]{1,0:T(4,128)S(1)} collective-permute-done((f32[4,128]{1,0:T(4,128)S(1)}, f32[4,128]{1,0:T(4,128)S(1)}, u32[]{:S(2)}, u32[]{:S(2)}) %collective-permute-start.8) | collective-permute-done | bytes 2080 | tf_op jit(solution)/shard_map/ppermute | solution.py:246
  12.7 0.2 scale.1
  12.9 1.6 %collective-permute-start.10 = (bf16[2,4,8,1280]{3,2,1,0:T(8,128)(2,1)S(1)}, bf16[2,4,8,1280]{3,2,1,0:T(8,128)(2,1)S(1)}, u32[]{:S(2)}, u32[]{:S(2)}) collective-permute-start(bf16[2,4,8,1280]{3,2,1,0:T(8,128)(2,1)S(1)} %get-tuple-element.48), channel_id=1, source_target_pairs={{0,8},{4,12},{8,0},{12,4},{16,24},{20,28},{24,16},{28,20},{1,9},{5... | collective-permute-start | bytes 491528 | tf_op jit(solution)/shard_map/ppermute | solution.py:246
  14.4 1.6 %collective-permute-start.12 = (bf16[2,4,8,1280]{3,2,1,0:T(8,128)(2,1)S(1)}, bf16[2,4,8,1280]{3,2,1,0:T(8,128)(2,1)S(1)}, u32[]{:S(2)}, u32[]{:S(2)}) collective-permute-start(bf16[2,4,8,1280]{3,2,1,0:T(8,128)(2,1)S(1)} %get-tuple-element.49), channel_id=1, source_target_pairs={{0,16},{4,20},{8,24},{12,28},{16,0},{20,4},{24,8},{28,12},{1,17},{... | collective-permute-start | bytes 491528 | tf_op jit(solution)/shard_map/ppermute | solution.py:246
  16.0 0.6 %collective-permute-start.14 = (bf16[2,4,8,1280]{3,2,1,0:T(8,128)(2,1)S(1)}, bf16[2,4,8,1280]{3,2,1,0:T(8,128)(2,1)S(1)}, u32[]{:S(2)}, u32[]{:S(2)}) collective-permute-start(bf16[2,4,8,1280]{3,2,1,0:T(8,128)(2,1)S(1)} %get-tuple-element.50), channel_id=1, source_target_pairs={{0,24},{4,28},{8,16},{12,20},{16,8},{20,12},{24,0},{28,4},{1,25},{... | collective-permute-start | bytes 491528 | tf_op jit(solution)/shard_map/ppermute | solution.py:246
  16.6 0.1 collective-permute-start.9
  16.7 3.1 %collective-permute-done.10 = bf16[2,4,8,1280]{3,2,1,0:T(8,128)(2,1)S(1)} collective-permute-done((bf16[2,4,8,1280]{3,2,1,0:T(8,128)(2,1)S(1)}, bf16[2,4,8,1280]{3,2,1,0:T(8,128)(2,1)S(1)}, u32[]{:S(2)}, u32[]{:S(2)}) %collective-permute-start.10) | collective-permute-done | bytes 163872 | tf_op jit(solution)/shard_map/ppermute | solution.py:246
  19.8 3.3 %collective-permute-done.12 = bf16[2,4,8,1280]{3,2,1,0:T(8,128)(2,1)S(1)} collective-permute-done((bf16[2,4,8,1280]{3,2,1,0:T(8,128)(2,1)S(1)}, bf16[2,4,8,1280]{3,2,1,0:T(8,128)(2,1)S(1)}, u32[]{:S(2)}, u32[]{:S(2)}) %collective-permute-start.12) | collective-permute-done | bytes 163872 | tf_op jit(solution)/shard_map/ppermute | solution.py:246
  23.1 0.6 %collective-permute-start.6 = (bf16[32,1280]{1,0:T(8,128)(2,1)S(1)}, bf16[32,1280]{1,0:T(8,128)(2,1)S(1)}, u32[]{:S(2)}, u32[]{:S(2)}) collective-permute-start(bf16[32,1280]{1,0:T(8,128)(2,1)S(1)} %slice_bitcast_fusion.3), channel_id=1, source_target_pairs={{0,4},{4,0},{8,12},{12,8},{16,20},{20,16},{24,28},{28,24},{1,5},{5... | collective-permute-start | bytes 245768 | tf_op jit(solution)/shard_map/ppermute | solution.py:246
  23.7 0.1 collective-permute-start.11
  23.8 0.5 collective-permute-start.13
  24.3 0.1 collective-permute-done.4.refs_5_
  24.4 0.2 collective-permute-start.15
  24.5 3.9 %load.1 = (f32[3,1280]{1,0:T(4,128)S(1)}, f32[1280]{0:T(1024)S(1)}, bf16[1280,1280]{1,0:T(8,128)(2,1)S(1)}, bf16[1280,1280]{1,0:T(8,128)(2,1)S(1)}, bf16[1280,1280]{1,0:T(8,128)(2,1)S(1)}) custom-call(f32[3,1280]{1,0:T(4,128)} %refs_0_.1, f32[1280]{0:T(1024)} %refs_1_.1, bf16[1280,1280]{1,0:T(8,128)(2,1)} %refs_2_.1, bf16[1280,1280]{1,0:T(8,128)(2,1)} %refs_3_.1, ...), custom_call_target="tpu_custom_call" | custom-call | tf_op jit(solution)/shard_map/load/pallas_call | solution.py:339
  28.5 4.0 %forward.1 = (bf16[256,1280]{1,0:T(8,128)(2,1)S(1)}, bf16[256,1280]{1,0:T(8,128)(2,1)S(1)}, bf16[256,1280]{1,0:T(8,128)(2,1)S(1)}, f32[20,32,256]{2,1,0:T(8,128)S(1)}) custom-call(s32[1]{0:T(128)} %bitcast.me_ref, f32[3,1280]{1,0:T(4,128)S(1)} %get-tuple-element.32.taps_ref, f32[1280]{0:T(1024)S(1)} %get-tuple-element.36.bias_ref, ...), custom_call_target="tpu_custom_call" | custom-call | tf_op jit(solution)/shard_map/forward/pallas_call | solution.py:349
  32.5 10.2 %backward.1 = (bf16[32,1280]{1,0:T(8,128)(2,1)S(1)}, bf16[32,1280]{1,0:T(8,128)(2,1)S(1)}, bf16[32,1280]{1,0:T(8,128)(2,1)S(1)}, bf16[32,1280]{1,0:T(8,128)(2,1)...) custom-call(s32[1]{0:T(128)} %bitcast.me_ref, ...), custom_call_target="tpu_custom_call" | custom-call | tf_op jit(solution)/shard_map/backward/pallas_call | solution.py:360
  42.8 0.4 collective-permute-start.16
  43.2 1.5 %collective-permute-start.18 = (bf16[32,1280]{1,0:T(8,128)(2,1)S(1)}, bf16[32,1280]{1,0:T(8,128)(2,1)S(1)}, u32[]{:S(2)}, u32[]{:S(2)}) collective-permute-start(bf16[32,1280]{1,0:T(8,128)(2,1)S(1)} %get-tuple-element.54), channel_id=1, source_target_pairs={{0,12},{4,8},{8,4},{12,0},{16,28},{20,24},{24,20},{28,16},{1,13},{... | collective-permute-start | bytes 245768 | tf_op jit(solution)/shard_map/ppermute | solution.py:246
  44.7 1.0 %collective-permute-start.19 = (bf16[32,1280]{1,0:T(8,128)(2,1)S(1)}, bf16[32,1280]{1,0:T(8,128)(2,1)S(1)}, u32[]{:S(2)}, u32[]{:S(2)}) collective-permute-start(bf16[32,1280]{1,0:T(8,128)(2,1)S(1)} %get-tuple-element.55), channel_id=1, source_target_pairs={{0,16},{4,20},{8,24},{12,28},{16,0},{20,4},{24,8},{28,12},{1,17},{... | collective-permute-start | bytes 245768 | tf_op jit(solution)/shard_map/ppermute | solution.py:246
  45.7 1.0 %collective-permute-start.20 = (bf16[32,1280]{1,0:T(8,128)(2,1)S(1)}, bf16[32,1280]{1,0:T(8,128)(2,1)S(1)}, u32[]{:S(2)}, u32[]{:S(2)}) collective-permute-start(bf16[32,1280]{1,0:T(8,128)(2,1)S(1)} %get-tuple-element.56), channel_id=1, source_target_pairs={{0,20},{4,16},{8,28},{12,24},{16,4},{20,0},{24,12},{28,8},{1,21},{... | collective-permute-start | bytes 245768 | tf_op jit(solution)/shard_map/ppermute | solution.py:246
  46.7 0.8 %collective-permute-start.21 = (bf16[32,1280]{1,0:T(8,128)(2,1)S(1)}, bf16[32,1280]{1,0:T(8,128)(2,1)S(1)}, u32[]{:S(2)}, u32[]{:S(2)}) collective-permute-start(bf16[32,1280]{1,0:T(8,128)(2,1)S(1)} %get-tuple-element.57), channel_id=1, source_target_pairs={{0,24},{4,28},{8,16},{12,20},{16,8},{20,12},{24,0},{28,4},{1,25},{... | collective-permute-start | bytes 245768 | tf_op jit(solution)/shard_map/ppermute | solution.py:246
  47.5 1.0 %collective-permute-done.17 = bf16[32,1280]{1,0:T(8,128)(2,1)S(1)} collective-permute-done((bf16[32,1280]{1,0:T(8,128)(2,1)S(1)}, bf16[32,1280]{1,0:T(8,128)(2,1)S(1)}, u32[]{:S(2)}, u32[]{:S(2)}) %collective-permute-start.17) | collective-permute-done | bytes 81952 | tf_op jit(solution)/shard_map/ppermute | solution.py:246
  48.5 0.6 %collective-permute-start.22 = (bf16[32,1280]{1,0:T(8,128)(2,1)S(1)}, bf16[32,1280]{1,0:T(8,128)(2,1)S(1)}, u32[]{:S(2)}, u32[]{:S(2)}) collective-permute-start(bf16[32,1280]{1,0:T(8,128)(2,1)S(1)} %get-tuple-element.58), channel_id=1, source_target_pairs={{0,28},{4,24},{8,20},{12,16},{16,12},{20,8},{24,4},{28,0},{1,29},{... | collective-permute-start | bytes 245768 | tf_op jit(solution)/shard_map/ppermute | solution.py:246
  49.1 0.9 %collective-permute-done.19 = bf16[32,1280]{1,0:T(8,128)(2,1)S(1)} collective-permute-done((bf16[32,1280]{1,0:T(8,128)(2,1)S(1)}, bf16[32,1280]{1,0:T(8,128)(2,1)S(1)}, u32[]{:S(2)}, u32[]{:S(2)}) %collective-permute-start.19) | collective-permute-done | bytes 81952 | tf_op jit(solution)/shard_map/ppermute | solution.py:246
  50.0 4.6 %collective-permute-done.20 = bf16[32,1280]{1,0:T(8,128)(2,1)S(1)} collective-permute-done((bf16[32,1280]{1,0:T(8,128)(2,1)S(1)}, bf16[32,1280]{1,0:T(8,128)(2,1)S(1)}, u32[]{:S(2)}, u32[]{:S(2)}) %collective-permute-start.20) | collective-permute-done | bytes 81952 | tf_op jit(solution)/shard_map/ppermute | solution.py:246
  54.6 0.9 %place.1 = bf16[4,8,8,1280]{3,2,1,0:T(8,128)(2,1)} custom-call(s32[1]{0:T(128)} %bitcast.me_ref, bf16[4,8,1280]{2,1,0:T(8,128)(2,1)S(1)} %bitcast.44, bf16[4,8,1280]{2,1,0:T(8,128)(2,1)S(1)} %bitcast.45, bf16[4,8,1280]{2,1,0:T(8,128)(2,1)S(1)} %bitcast.46, bf16[4,8,1280]{2,1,0:T(8,128)(2,1)S(1)} %bitcast.47, bf16[4,8,1280]{2,1,0:T(8,128)(2,1)S(1)} %bitcast.48, ...), custom_call_target="tpu_custom_call" | custom-call | tf_op jit(solution)/shard_map/place/pallas_call | solution.py:374
  (29 shorter events, 0.1 us)
Async XLA Ops:
  1.6 6.6 %collective-permute-start.7 = (f32[4,128]{1,0:T(4,128)S(1)}, f32[4,128]{1,0:T(4,128)S(1)}, u32[]{:S(2)}, u32[]{:S(2)}) collective-permute-start(f32[4,128]{1,0:T(4,128)S(1)} %get-tuple-element.45), channel_id=1, source_target_pairs={{0,1},{1,0},{2,3},{3,2},{4,5},{5,4},{6,7},{7,6},{8,9},{9,8},{10,11... | collective-permute-start | bytes 6152 | tf_op jit(solution)/shard_map/ppermute | solution.py:246
  4.7 9.7 %collective-permute-start.1 = (bf16[2,4,8,1280]{3,2,1,0:T(8,128)(2,1)S(1)}, bf16[2,4,8,1280]{3,2,1,0:T(8,128)(2,1)S(1)}, u32[]{:S(2)}, u32[]{:S(2)}) collective-permute-start(bf16[2,4,8,1280]{3,2,1,0:T(8,128)(2,1)S(1)} %get-tuple-element.38), channel_id=1, source_target_pairs={{0,8},{4,12},{8,0},{12,4},{16,24},{20,28},{24,16},{28,20},{1,9},{5... | collective-permute-start | bytes 491528 | tf_op jit(solution)/shard_map/ppermute | solution.py:246
  6.2 9.8 %collective-permute-start.3 = (bf16[2,4,8,1280]{3,2,1,0:T(8,128)(2,1)S(1)}, bf16[2,4,8,1280]{3,2,1,0:T(8,128)(2,1)S(1)}, u32[]{:S(2)}, u32[]{:S(2)}) collective-permute-start(bf16[2,4,8,1280]{3,2,1,0:T(8,128)(2,1)S(1)} %get-tuple-element.39), channel_id=1, source_target_pairs={{0,16},{4,20},{8,24},{12,28},{16,0},{20,4},{24,8},{28,12},{1,17},{... | collective-permute-start | bytes 491528 | tf_op jit(solution)/shard_map/ppermute | solution.py:246
  7.7 8.9 %collective-permute-start.5 = (bf16[2,4,8,1280]{3,2,1,0:T(8,128)(2,1)S(1)}, bf16[2,4,8,1280]{3,2,1,0:T(8,128)(2,1)S(1)}, u32[]{:S(2)}, u32[]{:S(2)}) collective-permute-start(bf16[2,4,8,1280]{3,2,1,0:T(8,128)(2,1)S(1)} %get-tuple-element.40), channel_id=1, source_target_pairs={{0,24},{4,28},{8,16},{12,20},{16,8},{20,12},{24,0},{28,4},{1,25},{... | collective-permute-start | bytes 491528 | tf_op jit(solution)/shard_map/ppermute | solution.py:246
  8.2 4.5 %collective-permute-start.8 = (f32[4,128]{1,0:T(4,128)S(1)}, f32[4,128]{1,0:T(4,128)S(1)}, u32[]{:S(2)}, u32[]{:S(2)}) collective-permute-start(f32[4,128]{1,0:T(4,128)S(1)} %add.3.energy_ref), channel_id=1, source_target_pairs={{0,2},{1,3},{2,0},{3,1},{4,6},{5,7},{6,4},{7,5},{8,10},{9,11},{10,... | collective-permute-start | bytes 6152 | tf_op jit(solution)/shard_map/ppermute | solution.py:246
  10.8 12.9 %collective-permute-start = (bf16[32,1280]{1,0:T(8,128)(2,1)S(1)}, bf16[32,1280]{1,0:T(8,128)(2,1)S(1)}, u32[]{:S(2)}, u32[]{:S(2)}) collective-permute-start(bf16[32,1280]{1,0:T(8,128)(2,1)S(1)} %slice_bitcast_fusion.7), channel_id=1, source_target_pairs={{0,4},{4,0},{8,12},{12,8},{16,20},{20,16},{24,28},{28,24},{1,5},{5... | collective-permute-start | bytes 245768 | tf_op jit(solution)/shard_map/ppermute | solution.py:246
  12.9 6.9 %collective-permute-start.10 = (bf16[2,4,8,1280]{3,2,1,0:T(8,128)(2,1)S(1)}, bf16[2,4,8,1280]{3,2,1,0:T(8,128)(2,1)S(1)}, u32[]{:S(2)}, u32[]{:S(2)}) collective-permute-start(bf16[2,4,8,1280]{3,2,1,0:T(8,128)(2,1)S(1)} %get-tuple-element.48), channel_id=1, source_target_pairs={{0,8},{4,12},{8,0},{12,4},{16,24},{20,28},{24,16},{28,20},{1,9},{5... | collective-permute-start | bytes 491528 | tf_op jit(solution)/shard_map/ppermute | solution.py:246
  14.4 8.7 %collective-permute-start.12 = (bf16[2,4,8,1280]{3,2,1,0:T(8,128)(2,1)S(1)}, bf16[2,4,8,1280]{3,2,1,0:T(8,128)(2,1)S(1)}, u32[]{:S(2)}, u32[]{:S(2)}) collective-permute-start(bf16[2,4,8,1280]{3,2,1,0:T(8,128)(2,1)S(1)} %get-tuple-element.49), channel_id=1, source_target_pairs={{0,16},{4,20},{8,24},{12,28},{16,0},{20,4},{24,8},{28,12},{1,17},{... | collective-permute-start | bytes 491528 | tf_op jit(solution)/shard_map/ppermute | solution.py:246
  16.0 7.1 %collective-permute-start.14 = (bf16[2,4,8,1280]{3,2,1,0:T(8,128)(2,1)S(1)}, bf16[2,4,8,1280]{3,2,1,0:T(8,128)(2,1)S(1)}, u32[]{:S(2)}, u32[]{:S(2)}) collective-permute-start(bf16[2,4,8,1280]{3,2,1,0:T(8,128)(2,1)S(1)} %get-tuple-element.50), channel_id=1, source_target_pairs={{0,24},{4,28},{8,16},{12,20},{16,8},{20,12},{24,0},{28,4},{1,25},{... | collective-permute-start | bytes 491528 | tf_op jit(solution)/shard_map/ppermute | solution.py:246
  16.6 15.9 %collective-permute-start.9 = (bf16[32,1280]{1,0:T(8,128)(2,1)S(1)}, bf16[32,1280]{1,0:T(8,128)(2,1)S(1)}, u32[]{:S(2)}, u32[]{:S(2)}) collective-permute-start(bf16[32,1280]{1,0:T(8,128)(2,1)S(1)} %slice_bitcast_fusion.6), channel_id=1, source_target_pairs={{0,4},{4,0},{8,12},{12,8},{16,20},{20,16},{24,28},{28,24},{1,5},{5... | collective-permute-start | bytes 245768 | tf_op jit(solution)/shard_map/ppermute | solution.py:246
  19.8 4.0 %collective-permute-start.2 = (bf16[32,1280]{1,0:T(8,128)(2,1)S(1)}, bf16[32,1280]{1,0:T(8,128)(2,1)S(1)}, u32[]{:S(2)}, u32[]{:S(2)}) collective-permute-start(bf16[32,1280]{1,0:T(8,128)(2,1)S(1)} %slice_bitcast_fusion.5), channel_id=1, source_target_pairs={{0,4},{4,0},{8,12},{12,8},{16,20},{20,16},{24,28},{28,24},{1,5},{5... | collective-permute-start | bytes 245768 | tf_op jit(solution)/shard_map/ppermute | solution.py:246
  23.1 1.3 %collective-permute-start.4 = (bf16[32,1280]{1,0:T(8,128)(2,1)S(1)}, bf16[32,1280]{1,0:T(8,128)(2,1)S(1)}, u32[]{:S(2)}, u32[]{:S(2)}) collective-permute-start(bf16[32,1280]{1,0:T(8,128)(2,1)S(1)} %slice_bitcast_fusion.4), channel_id=1, source_target_pairs={{0,4},{4,0},{8,12},{12,8},{16,20},{20,16},{24,28},{28,24},{1,5},{5... | collective-permute-start | bytes 245768 | tf_op jit(solution)/shard_map/ppermute | solution.py:246
  23.1 5.4 %collective-permute-start.6 = (bf16[32,1280]{1,0:T(8,128)(2,1)S(1)}, bf16[32,1280]{1,0:T(8,128)(2,1)S(1)}, u32[]{:S(2)}, u32[]{:S(2)}) collective-permute-start(bf16[32,1280]{1,0:T(8,128)(2,1)S(1)} %slice_bitcast_fusion.3), channel_id=1, source_target_pairs={{0,4},{4,0},{8,12},{12,8},{16,20},{20,16},{24,28},{28,24},{1,5},{5... | collective-permute-start | bytes 245768 | tf_op jit(solution)/shard_map/ppermute | solution.py:246
  23.7 8.8 %collective-permute-start.11 = (bf16[32,1280]{1,0:T(8,128)(2,1)S(1)}, bf16[32,1280]{1,0:T(8,128)(2,1)S(1)}, u32[]{:S(2)}, u32[]{:S(2)}) collective-permute-start(bf16[32,1280]{1,0:T(8,128)(2,1)S(1)} %slice_bitcast_fusion.2), channel_id=1, source_target_pairs={{0,4},{4,0},{8,12},{12,8},{16,20},{20,16},{24,28},{28,24},{1,5},{5... | collective-permute-start | bytes 245768 | tf_op jit(solution)/shard_map/ppermute | solution.py:246
  23.8 8.7 %collective-permute-start.13 = (bf16[32,1280]{1,0:T(8,128)(2,1)S(1)}, bf16[32,1280]{1,0:T(8,128)(2,1)S(1)}, u32[]{:S(2)}, u32[]{:S(2)}) collective-permute-start(bf16[32,1280]{1,0:T(8,128)(2,1)S(1)} %slice_bitcast_fusion.1), channel_id=1, source_target_pairs={{0,4},{4,0},{8,12},{12,8},{16,20},{20,16},{24,28},{28,24},{1,5},{5... | collective-permute-start | bytes 245768 | tf_op jit(solution)/shard_map/ppermute | solution.py:246
  24.4 8.1 %collective-permute-start.15 = (bf16[32,1280]{1,0:T(8,128)(2,1)S(1)}, bf16[32,1280]{1,0:T(8,128)(2,1)S(1)}, u32[]{:S(2)}, u32[]{:S(2)}) collective-permute-start(bf16[32,1280]{1,0:T(8,128)(2,1)S(1)} %slice_bitcast_fusion), channel_id=1, source_target_pairs={{0,4},{4,0},{8,12},{12,8},{16,20},{20,16},{24,28},{28,24},{1,5},{5... | collective-permute-start | bytes 245768 | tf_op jit(solution)/shard_map/ppermute | solution.py:246
  42.8 3.9 %collective-permute-start.16 = (bf16[32,1280]{1,0:T(8,128)(2,1)S(1)}, bf16[32,1280]{1,0:T(8,128)(2,1)S(1)}, u32[]{:S(2)}, u32[]{:S(2)}) collective-permute-start(bf16[32,1280]{1,0:T(8,128)(2,1)S(1)} %get-tuple-element.52), channel_id=1, source_target_pairs={{0,4},{4,0},{8,12},{12,8},{16,20},{20,16},{24,28},{28,24},{1,5},{5... | collective-permute-start | bytes 245768 | tf_op jit(solution)/shard_map/ppermute | solution.py:246
  43.2 5.3 %collective-permute-start.17 = (bf16[32,1280]{1,0:T(8,128)(2,1)S(1)}, bf16[32,1280]{1,0:T(8,128)(2,1)S(1)}, u32[]{:S(2)}, u32[]{:S(2)}) collective-permute-start(bf16[32,1280]{1,0:T(8,128)(2,1)S(1)} %get-tuple-element.53), channel_id=1, source_target_pairs={{0,8},{4,12},{8,0},{12,4},{16,24},{20,28},{24,16},{28,20},{1,9},{5... | collective-permute-start | bytes 245768 | tf_op jit(solution)/shard_map/ppermute | solution.py:246
  43.2 5.9 %collective-permute-start.18 = (bf16[32,1280]{1,0:T(8,128)(2,1)S(1)}, bf16[32,1280]{1,0:T(8,128)(2,1)S(1)}, u32[]{:S(2)}, u32[]{:S(2)}) collective-permute-start(bf16[32,1280]{1,0:T(8,128)(2,1)S(1)} %get-tuple-element.54), channel_id=1, source_target_pairs={{0,12},{4,8},{8,4},{12,0},{16,28},{20,24},{24,20},{28,16},{1,13},{... | collective-permute-start | bytes 245768 | tf_op jit(solution)/shard_map/ppermute | solution.py:246
  44.7 5.3 %collective-permute-start.19 = (bf16[32,1280]{1,0:T(8,128)(2,1)S(1)}, bf16[32,1280]{1,0:T(8,128)(2,1)S(1)}, u32[]{:S(2)}, u32[]{:S(2)}) collective-permute-start(bf16[32,1280]{1,0:T(8,128)(2,1)S(1)} %get-tuple-element.55), channel_id=1, source_target_pairs={{0,16},{4,20},{8,24},{12,28},{16,0},{20,4},{24,8},{28,12},{1,17},{... | collective-permute-start | bytes 245768 | tf_op jit(solution)/shard_map/ppermute | solution.py:246
  45.7 8.9 %collective-permute-start.20 = (bf16[32,1280]{1,0:T(8,128)(2,1)S(1)}, bf16[32,1280]{1,0:T(8,128)(2,1)S(1)}, u32[]{:S(2)}, u32[]{:S(2)}) collective-permute-start(bf16[32,1280]{1,0:T(8,128)(2,1)S(1)} %get-tuple-element.56), channel_id=1, source_target_pairs={{0,20},{4,16},{8,28},{12,24},{16,4},{20,0},{24,12},{28,8},{1,21},{... | collective-permute-start | bytes 245768 | tf_op jit(solution)/shard_map/ppermute | solution.py:246
  46.7 7.9 %collective-permute-start.21 = (bf16[32,1280]{1,0:T(8,128)(2,1)S(1)}, bf16[32,1280]{1,0:T(8,128)(2,1)S(1)}, u32[]{:S(2)}, u32[]{:S(2)}) collective-permute-start(bf16[32,1280]{1,0:T(8,128)(2,1)S(1)} %get-tuple-element.57), channel_id=1, source_target_pairs={{0,24},{4,28},{8,16},{12,20},{16,8},{20,12},{24,0},{28,4},{1,25},{... | collective-permute-start | bytes 245768 | tf_op jit(solution)/shard_map/ppermute | solution.py:246
  48.5 6.1 %collective-permute-start.22 = (bf16[32,1280]{1,0:T(8,128)(2,1)S(1)}, bf16[32,1280]{1,0:T(8,128)(2,1)S(1)}, u32[]{:S(2)}, u32[]{:S(2)}) collective-permute-start(bf16[32,1280]{1,0:T(8,128)(2,1)S(1)} %get-tuple-element.58), channel_id=1, source_target_pairs={{0,28},{4,24},{8,20},{12,16},{16,12},{20,8},{24,4},{28,0},{1,29},{... | collective-permute-start | bytes 245768 | tf_op jit(solution)/shard_map/ppermute | solution.py:246
where the time goes:
time: 55.6 us; the launch traced here: 55.5 us
  Pallas kernels  20.8 us (37%)
  starting transfers between devices  19.6 us (35%)
  waiting for transfers between devices  14.9 us (27%)
    ppermute x23, starting transfers between devices, swap(): lax.ppermute(value, axis, [(i, i ^ mask) for i in range(lax.axis_size(axi...  19.6 us
    ppermute x23, waiting for transfers between devices, swap(): lax.ppermute(value, axis, [(i, i ^ mask) for i in range(lax.axis_size(axi...  14.9 us
    pallas_call x1, Pallas kernels, body(): pl.pallas_call(functools.partial(backward_kernel, **sizes), in_specs=[sme...  10.2 us
    pallas_call x1, Pallas kernels, body(): pl.pallas_call(functools.partial(forward_kernel, **sizes), in_specs=[smem...  3.99 us
    pallas_call x1, Pallas kernels, body(): pl.pallas_call(load_kernel, in_specs=[hbm] * len(parameters), out_specs=[...  3.93 us
    pallas_call x1, Pallas kernels, body(): pl.pallas_call(functools.partial(pack_kernel, peers=peers), in_specs=[sme...  1.58 us
  transfers between devices with their start and end apart: 23, of which 7 were waited for; matrix products, arithmetic and copies ran while one was open for 0% of the time, Pallas kernels for 15%

commit v1 on v0

--- a/solution.py
+++ b/solution.py
@@ -52,56 +52,51 @@
     return jnp.concatenate([kept * mask for mask in token_masks], axis=0)
 
 
-def pack_kernel(me_ref, tokens_ref, cotangent_ref, *refs, peers):
-    outs = refs[:peers // 2]
-    energy_ref, held_ref, sems = refs[peers // 2:]
-    me = me_ref[0]
-    frame_rows = held_ref.shape[0]
-    frame_copies = [
-        pltpu.make_async_copy(cotangent_ref.at[frame], held_ref.at[frame], sems.at[peers + frame])
-        for frame in range(frame_rows)
-    ]
+def pack_kernel(me_ref, tokens_ref, *refs):
+    outs, sems = refs[:-1], refs[-1]
+    me = me_ref[0]
     copies = [
         pltpu.make_async_copy(
             tokens_ref.at[:, me ^ mask], outs[mask // 2].at[mask % 2], sems.at[mask]
         )
-        for mask in range(peers)
+        for mask in range(2 * len(outs))
     ]
-    for copy in frame_copies + copies:
+    for copy in copies:
+        copy.start()
+    for copy in copies:
+        copy.wait()
+
+
+def energy_kernel(cotangent_ref, energy_ref, held_ref, sems):
+    frame_rows, groups = held_ref.shape[:2]
+    copies = [
+        pltpu.make_async_copy(cotangent_ref.at[frame], held_ref.at[frame], sems.at[frame])
+        for frame in range(frame_rows)
+    ]
+    for copy in copies:
         copy.start()
     for frame in range(frame_rows):
-        frame_copies[frame].wait()
+        copies[frame].wait()
         total = jnp.zeros(held_ref.shape[2:], jnp.float32)
-        for group in range(peers):
+        for group in range(groups):
             grad = held_ref[frame, group].astype(jnp.float32)
             total += grad * grad
         energy_ref[frame:frame + 1, :] = jnp.broadcast_to(
             jnp.sum(total, keepdims=True), (1, LANES)
         )
-    for copy in copies:
-        copy.wait()
-
-
-def scale_kernel(me_ref, energy_ref, other_ref, cotangent_ref, *outs, peers, count):
-    me = me_ref[0]
-    factor = lax.rsqrt((energy_ref[...] + other_ref[...]) / count + 1e-06)
-    frame_rows = cotangent_ref.shape[0]
+
+
+def scale_kernel(me_ref, held_ref, *refs, peers, count):
+    energies, outs = refs[:-(peers // 2)], refs[-(peers // 2):]
+    me = me_ref[0]
+    factor = lax.rsqrt(sum(energy[...] for energy in energies) / count + 1e-06)
+    frame_rows = held_ref.shape[0]
     for mask in range(peers):
         for frame in range(frame_rows):
-            grad = cotangent_ref[frame, me ^ mask].astype(jnp.float32)
+            grad = held_ref[frame, me ^ mask].astype(jnp.float32)
             outs[mask // 2][mask % 2, frame] = (
                 grad * factor[frame:frame + 1, :1]
             ).astype(jnp.bfloat16)
-
-
-def load_kernel(*refs):
-    count = len(refs) // 2
-    sems = refs[-1]
-    copies = [pltpu.make_async_copy(refs[i], refs[count + i], sems.at[i]) for i in range(count)]
-    for copy in copies:
-        copy.start()
-    for copy in copies:
-        copy.wait()
 
 
 def place_kernel(me_ref, *refs, peers):
@@ -285,14 +280,21 @@
     return received
 
 
-def tile_sum(value):
-    mask = 1
-    other = jnp.zeros_like(value)
-    while mask < lax.axis_size("tile"):
-        value = value + other if mask > 1 else value
-        other = swap(value, "tile", mask)
-        mask *= 2
-    return value, other
+def tile_masks(peers):
+    stages, stride = [], 1
+    while stride < peers:
+        radix = min(4, peers // stride)
+        stages.append([stride * step for step in range(radix - 1, 0, -1)])
+        stride *= radix
+    return stages
+
+
+def tile_terms(value):
+    terms = [value]
+    for masks in tile_masks(lax.axis_size("tile")):
+        value = sum(terms[1:], terms[0])
+        terms = [value] + [swap(value, "tile", mask) for mask in masks]
+    return terms
 
 
 def body(tokens, cotangent, w_query, w_key, w_value, conv_taps, conv_bias):
@@ -313,38 +315,38 @@
     sent_shape = low((2, frame_rows, toks, channels))
     split = (frame_rows, peers, toks, channels)
 
-    *sent_tokens, energy, held = pl.pallas_call(
-        functools.partial(pack_kernel, peers=peers),
-        in_specs=[smem, hbm, hbm],
-        out_specs=[vmem] * (peers // 2 + 2),
-        out_shape=[sent_shape] * (peers // 2)
-        + [pltpu.VMEM((frame_rows, LANES), jnp.float32), low(split)],
-        scratch_shapes=[pltpu.SemaphoreType.DMA((peers + frame_rows,))],
-        compiler_params=grant(8),
+    sent_tokens = pl.pallas_call(
+        pack_kernel,
+        in_specs=[smem, hbm],
+        out_specs=[vmem] * (peers // 2),
+        out_shape=[sent_shape] * (peers // 2),
+        scratch_shapes=[pltpu.SemaphoreType.DMA((peers,))],
+        compiler_params=grant(4),
         name="pack",
-    )(me_arg, off_chip(tokens.reshape(split)), off_chip(cotangent.reshape(split)))
-    energy_here, energy_there = tile_sum(energy)
+    )(me_arg, off_chip(tokens.reshape(split)))
     token_blocks = gather_tokens(sent_tokens)
+    energy, held = pl.pallas_call(
+        energy_kernel,
+        in_specs=[hbm],
+        out_specs=[vmem] * 2,
+        out_shape=[pltpu.VMEM((frame_rows, LANES), jnp.float32), low(split)],
+        scratch_shapes=[pltpu.SemaphoreType.DMA((frame_rows,))],
+        compiler_params=grant(4),
+        name="energy",
+    )(off_chip(cotangent.reshape(split)))
+    terms = tile_terms(energy)
     sent_grads = pl.pallas_call(
         functools.partial(scale_kernel, peers=peers, count=spatial_all * channels),
-        in_specs=[smem, vmem, vmem, vmem],
+        in_specs=[smem] + [vmem] * (1 + len(terms)),
         out_specs=[vmem] * (peers // 2),
         out_shape=[sent_shape] * (peers // 2),
         compiler_params=grant(8),
+        cost_estimate=pl.CostEstimate(flops=1 << 34, bytes_accessed=1 << 25, transcendentals=0),
         name="scale",
-    )(me_arg, on_chip(energy_here), on_chip(energy_there), on_chip(held))
+    )(me_arg, on_chip(held), *map(on_chip, terms))
     grad_blocks = gather_tokens(sent_grads)
 
-    parameters = (conv_taps, conv_bias, w_query, w_key, w_value)
-    conv_taps, conv_bias, *weights = map(on_chip, pl.pallas_call(
-        load_kernel,
-        in_specs=[hbm] * len(parameters),
-        out_specs=[vmem] * len(parameters),
-        out_shape=[pltpu.VMEM(value.shape, value.dtype) for value in parameters],
-        scratch_shapes=[pltpu.SemaphoreType.DMA((len(parameters),))],
-        compiler_params=grant(4),
-        name="load",
-    )(*map(off_chip, parameters)))
+    weights = (w_query, w_key, w_value)
     sizes = dict(frames=frames, toks=toks, peers=peers)
     query, key, value, prob = pl.pallas_call(
         functools.partial(forward_kernel, **sizes),

time: 55.6 us -> 54.8 us (0.986)
  Pallas kernels: 20.8 us -> 18 us
  waiting for transfers between devices: 14.9 us -> 16.6 us
    pallas_call x2, Pallas kernels: 5.52 us -> 2.74 us  [the longest x1 1.5 us: body(): pl.pallas_call(energy_kernel, in_specs=[hbm], out_specs=[vmem] * 2, out_s...]
    ppermute x23 -> x24, waiting for transfers between devices: 14.9 us -> 16.6 us  [swap(): lax.ppermute(value, axis, [(i, i ^ mask) for i in range(lax.axis_size(axi...]
    ppermute x23 -> x24, starting transfers between devices: 19.6 us -> 19.7 us  [swap(): lax.ppermute(value, axis, [(i, i ^ mask) for i in range(lax.axis_size(axi...]
  transfers between devices with their start and end apart: 23 -> 24, of which waited for: 7 -> 10; matrix products, arithmetic and copies ran while one was open for 0% -> 0% of each run, Pallas kernels for 15% -> 10%
where the time goes in v1:
time: 54.8 us; the launch traced here: 54.6 us
  starting transfers between devices  19.7 us (36%)
  Pallas kernels  18 us (33%)
  waiting for transfers between devices  16.6 us (30%)
    ppermute x24, starting transfers between devices, swap(): lax.ppermute(value, axis, [(i, i ^ mask) for i in range(lax.axis_size(axi...  19.7 us
    ppermute x24, waiting for transfers between devices, swap(): lax.ppermute(value, axis, [(i, i ^ mask) for i in range(lax.axis_size(axi...  16.6 us
    pallas_call x1, Pallas kernels, body(): pl.pallas_call(functools.partial(backward_kernel, **sizes), in_specs=[sme...  10.2 us
    pallas_call x1, Pallas kernels, body(): pl.pallas_call(functools.partial(forward_kernel, **sizes), in_specs=[smem...  3.98 us
    pallas_call x1, Pallas kernels, body(): pl.pallas_call(energy_kernel, in_specs=[hbm], out_specs=[vmem] * 2, out_s...  1.5 us
    pallas_call x1, Pallas kernels, body(): pl.pallas_call(pack_kernel, in_specs=[smem, hbm], out_specs=[vmem] * (pee...  1.24 us
  transfers between devices with their start and end apart: 24, of which 10 were waited for; matrix products, arithmetic and copies ran while one was open for 0% of the time, Pallas kernels for 10%

profile of v1, /device:TPU:0, one launch (start us, length us, event | category | flops | bytes accessed | tf_op | source)
XLA Modules:
  0.0 54.6 jit_solution(17493820075420367758)
XLA Ops:
  0.0 1.5 %energy.1 = (f32[4,128]{1,0:T(4,128)S(1)}, bf16[4,8,8,1280]{3,2,1,0:T(8,128)(2,1)S(1)}) custom-call(bf16[4,8,8,1280]{3,2,1,0:T(8,128)(2,1)} %bitcast.52), custom_call_target="tpu_custom_call" | custom-call | tf_op jit(solution)/shard_map/energy/pallas_call | solution.py:328
  1.5 5.1 %collective-permute-start.7 = (f32[4,128]{1,0:T(4,128)S(1)}, f32[4,128]{1,0:T(4,128)S(1)}, u32[]{:S(2)}, u32[]{:S(2)}) collective-permute-start(f32[4,128]{1,0:T(4,128)S(1)} %get-tuple-element.36.refs_0_), channel_id=1, source_target_pairs={{0,3},{1,2},{2,1},{3,0},{4,7},{5,6},{6,5},{7,4},{8,11},{9,10},{10,... | collective-permute-start | bytes 6152 | tf_op jit(solution)/shard_map/ppermute | solution.py:241
  6.7 0.6 %collective-permute-start.9 = (f32[4,128]{1,0:T(4,128)S(1)}, f32[4,128]{1,0:T(4,128)S(1)}, u32[]{:S(2)}, u32[]{:S(2)}) collective-permute-start(f32[4,128]{1,0:T(4,128)S(1)} %get-tuple-element.36.refs_0_), channel_id=1, source_target_pairs={{0,1},{1,0},{2,3},{3,2},{4,5},{5,4},{6,7},{7,6},{8,9},{9,8},{10,11... | collective-permute-start | bytes 6152 | tf_op jit(solution)/shard_map/ppermute | solution.py:241
  7.3 1.2 %pack.1 = (bf16[2,4,8,1280]{3,2,1,0:T(8,128)(2,1)S(1)}, bf16[2,4,8,1280]{3,2,1,0:T(8,128)(2,1)S(1)}, bf16[2,4,8,1280]{3,2,1,0:T(8,128)(2,1)S(1)}, bf16[2,4,8,1280]{3,2,1,0:T(8,128)(2,1)S(1)}) custom-call(s32[1]{0:T(128)} %bitcast.me_ref, bf16[4,8,8,1280]{3,2,1,0:T(8,128)(2,1)} %bitcast.53), custom_call_target="tpu_custom_call" | custom-call | tf_op jit(solution)/shard_map/pack/pallas_call | solution.py:318
  8.5 1.7 %collective-permute-start.1 = (bf16[2,4,8,1280]{3,2,1,0:T(8,128)(2,1)S(1)}, bf16[2,4,8,1280]{3,2,1,0:T(8,128)(2,1)S(1)}, u32[]{:S(2)}, u32[]{:S(2)}) collective-permute-start(bf16[2,4,8,1280]{3,2,1,0:T(8,128)(2,1)S(1)} %get-tuple-element.28), channel_id=1, source_target_pairs={{0,8},{4,12},{8,0},{12,4},{16,24},{20,28},{24,16},{28,20},{1,9},{5... | collective-permute-start | bytes 491528 | tf_op jit(solution)/shard_map/ppermute | solution.py:241
  10.2 1.5 %collective-permute-start.3 = (bf16[2,4,8,1280]{3,2,1,0:T(8,128)(2,1)S(1)}, bf16[2,4,8,1280]{3,2,1,0:T(8,128)(2,1)S(1)}, u32[]{:S(2)}, u32[]{:S(2)}) collective-permute-start(bf16[2,4,8,1280]{3,2,1,0:T(8,128)(2,1)S(1)} %get-tuple-element.29), channel_id=1, source_target_pairs={{0,16},{4,20},{8,24},{12,28},{16,0},{20,4},{24,8},{28,12},{1,17},{... | collective-permute-start | bytes 491528 | tf_op jit(solution)/shard_map/ppermute | solution.py:241
  11.8 0.4 collective-permute-start.5
  12.2 0.2 scale.1
  12.4 1.7 %collective-permute-start.11 = (bf16[2,4,8,1280]{3,2,1,0:T(8,128)(2,1)S(1)}, bf16[2,4,8,1280]{3,2,1,0:T(8,128)(2,1)S(1)}, u32[]{:S(2)}, u32[]{:S(2)}) collective-permute-start(bf16[2,4,8,1280]{3,2,1,0:T(8,128)(2,1)S(1)} %get-tuple-element.38), channel_id=1, source_target_pairs={{0,8},{4,12},{8,0},{12,4},{16,24},{20,28},{24,16},{28,20},{1,9},{5... | collective-permute-start | bytes 491528 | tf_op jit(solution)/shard_map/ppermute | solution.py:241
  14.1 0.9 %collective-permute-done.1 = bf16[2,4,8,1280]{3,2,1,0:T(8,128)(2,1)S(1)} collective-permute-done((bf16[2,4,8,1280]{3,2,1,0:T(8,128)(2,1)S(1)}, bf16[2,4,8,1280]{3,2,1,0:T(8,128)(2,1)S(1)}, u32[]{:S(2)}, u32[]{:S(2)}) %collective-permute-start.1) | collective-permute-done | bytes 163872 | tf_op jit(solution)/shard_map/ppermute | solution.py:241
  15.0 1.7 %collective-permute-start.13 = (bf16[2,4,8,1280]{3,2,1,0:T(8,128)(2,1)S(1)}, bf16[2,4,8,1280]{3,2,1,0:T(8,128)(2,1)S(1)}, u32[]{:S(2)}, u32[]{:S(2)}) collective-permute-start(bf16[2,4,8,1280]{3,2,1,0:T(8,128)(2,1)S(1)} %get-tuple-element.39), channel_id=1, source_target_pairs={{0,16},{4,20},{8,24},{12,28},{16,0},{20,4},{24,8},{28,12},{1,17},{... | collective-permute-start | bytes 491528 | tf_op jit(solution)/shard_map/ppermute | solution.py:241
  16.7 2.4 %collective-permute-done.3 = bf16[2,4,8,1280]{3,2,1,0:T(8,128)(2,1)S(1)} collective-permute-done((bf16[2,4,8,1280]{3,2,1,0:T(8,128)(2,1)S(1)}, bf16[2,4,8,1280]{3,2,1,0:T(8,128)(2,1)S(1)}, u32[]{:S(2)}, u32[]{:S(2)}) %collective-permute-start.3) | collective-permute-done | bytes 163872 | tf_op jit(solution)/shard_map/ppermute | solution.py:241
  19.2 0.7 %collective-permute-done.5 = bf16[2,4,8,1280]{3,2,1,0:T(8,128)(2,1)S(1)} collective-permute-done((bf16[2,4,8,1280]{3,2,1,0:T(8,128)(2,1)S(1)}, bf16[2,4,8,1280]{3,2,1,0:T(8,128)(2,1)S(1)}, u32[]{:S(2)}, u32[]{:S(2)}) %collective-permute-start.5) | collective-permute-done | bytes 163872 | tf_op jit(solution)/shard_map/ppermute | solution.py:241
  19.9 2.5 %collective-permute-done.11 = bf16[2,4,8,1280]{3,2,1,0:T(8,128)(2,1)S(1)} collective-permute-done((bf16[2,4,8,1280]{3,2,1,0:T(8,128)(2,1)S(1)}, bf16[2,4,8,1280]{3,2,1,0:T(8,128)(2,1)S(1)}, u32[]{:S(2)}, u32[]{:S(2)}) %collective-permute-start.11) | collective-permute-done | bytes 163872 | tf_op jit(solution)/shard_map/ppermute | solution.py:241
  22.4 3.7 %collective-permute-done.13 = bf16[2,4,8,1280]{3,2,1,0:T(8,128)(2,1)S(1)} collective-permute-done((bf16[2,4,8,1280]{3,2,1,0:T(8,128)(2,1)S(1)}, bf16[2,4,8,1280]{3,2,1,0:T(8,128)(2,1)S(1)}, u32[]{:S(2)}, u32[]{:S(2)}) %collective-permute-start.13) | collective-permute-done | bytes 163872 | tf_op jit(solution)/shard_map/ppermute | solution.py:241
  26.1 0.6 %collective-permute-start.6 = (bf16[32,1280]{1,0:T(8,128)(2,1)S(1)}, bf16[32,1280]{1,0:T(8,128)(2,1)S(1)}, u32[]{:S(2)}, u32[]{:S(2)}) collective-permute-start(bf16[32,1280]{1,0:T(8,128)(2,1)S(1)} %slice_bitcast_fusion.3), channel_id=1, source_target_pairs={{0,4},{4,0},{8,12},{12,8},{16,20},{20,16},{24,28},{28,24},{1,5},{5... | collective-permute-start | bytes 245768 | tf_op jit(solution)/shard_map/ppermute | solution.py:241
  26.8 0.5 collective-permute-start.14
  27.3 0.1 collective-permute-done.4.refs_5_
  27.4 0.2 collective-permute-start.16
  27.6 4.0 %forward.1 = (bf16[256,1280]{1,0:T(8,128)(2,1)S(1)}, bf16[256,1280]{1,0:T(8,128)(2,1)S(1)}, bf16[256,1280]{1,0:T(8,128)(2,1)S(1)}, f32[20,32,256]{2,1,0:T(8,128)S(1)}) custom-call(s32[1]{0:T(128)} %bitcast.me_ref, f32[3,1280]{1,0:T(4,128)S(1)} %copy-done.3, f32[1280]{0:T(1024)S(1)} %copy-done.4, bf16[1280,1280]{1,0:T(8,128)(2,1)S(1)} %copy-done, ...), custom_call_target="tpu_custom_call" | custom-call | tf_op jit(solution)/shard_map/forward/pallas_call | solution.py:351
  31.7 10.2 %backward.1 = (bf16[32,1280]{1,0:T(8,128)(2,1)S(1)}, bf16[32,1280]{1,0:T(8,128)(2,1)S(1)}, bf16[32,1280]{1,0:T(8,128)(2,1)S(1)}, bf16[32,1280]{1,0:T(8,128)(2,1)...) custom-call(s32[1]{0:T(128)} %bitcast.me_ref, ...), custom_call_target="tpu_custom_call" | custom-call | tf_op jit(solution)/shard_map/backward/pallas_call | solution.py:362
  41.9 0.4 collective-permute-start.17
  42.3 0.4 collective-permute-start.18
  42.7 1.1 %collective-permute-start.19 = (bf16[32,1280]{1,0:T(8,128)(2,1)S(1)}, bf16[32,1280]{1,0:T(8,128)(2,1)S(1)}, u32[]{:S(2)}, u32[]{:S(2)}) collective-permute-start(bf16[32,1280]{1,0:T(8,128)(2,1)S(1)} %get-tuple-element.44), channel_id=1, source_target_pairs={{0,12},{4,8},{8,4},{12,0},{16,28},{20,24},{24,20},{28,16},{1,13},{... | collective-permute-start | bytes 245768 | tf_op jit(solution)/shard_map/ppermute | solution.py:241
  43.8 0.9 %collective-permute-start.20 = (bf16[32,1280]{1,0:T(8,128)(2,1)S(1)}, bf16[32,1280]{1,0:T(8,128)(2,1)S(1)}, u32[]{:S(2)}, u32[]{:S(2)}) collective-permute-start(bf16[32,1280]{1,0:T(8,128)(2,1)S(1)} %get-tuple-element.45), channel_id=1, source_target_pairs={{0,16},{4,20},{8,24},{12,28},{16,0},{20,4},{24,8},{28,12},{1,17},{... | collective-permute-start | bytes 245768 | tf_op jit(solution)/shard_map/ppermute | solution.py:241
  44.7 1.1 %collective-permute-start.21 = (bf16[32,1280]{1,0:T(8,128)(2,1)S(1)}, bf16[32,1280]{1,0:T(8,128)(2,1)S(1)}, u32[]{:S(2)}, u32[]{:S(2)}) collective-permute-start(bf16[32,1280]{1,0:T(8,128)(2,1)S(1)} %get-tuple-element.46), channel_id=1, source_target_pairs={{0,20},{4,16},{8,28},{12,24},{16,4},{20,0},{24,12},{28,8},{1,21},{... | collective-permute-start | bytes 245768 | tf_op jit(solution)/shard_map/ppermute | solution.py:241
  45.8 1.1 %collective-permute-start.22 = (bf16[32,1280]{1,0:T(8,128)(2,1)S(1)}, bf16[32,1280]{1,0:T(8,128)(2,1)S(1)}, u32[]{:S(2)}, u32[]{:S(2)}) collective-permute-start(bf16[32,1280]{1,0:T(8,128)(2,1)S(1)} %get-tuple-element.47), channel_id=1, source_target_pairs={{0,24},{4,28},{8,16},{12,20},{16,8},{20,12},{24,0},{28,4},{1,25},{... | collective-permute-start | bytes 245768 | tf_op jit(solution)/shard_map/ppermute | solution.py:241
  46.9 0.7 %collective-permute-done.18 = bf16[32,1280]{1,0:T(8,128)(2,1)S(1)} collective-permute-done((bf16[32,1280]{1,0:T(8,128)(2,1)S(1)}, bf16[32,1280]{1,0:T(8,128)(2,1)S(1)}, u32[]{:S(2)}, u32[]{:S(2)}) %collective-permute-start.18) | collective-permute-done | bytes 81952 | tf_op jit(solution)/shard_map/ppermute | solution.py:241
  47.6 0.6 %collective-permute-start.23 = (bf16[32,1280]{1,0:T(8,128)(2,1)S(1)}, bf16[32,1280]{1,0:T(8,128)(2,1)S(1)}, u32[]{:S(2)}, u32[]{:S(2)}) collective-permute-start(bf16[32,1280]{1,0:T(8,128)(2,1)S(1)} %get-tuple-element.48), channel_id=1, source_target_pairs={{0,28},{4,24},{8,20},{12,16},{16,12},{20,8},{24,4},{28,0},{1,29},{... | collective-permute-start | bytes 245768 | tf_op jit(solution)/shard_map/ppermute | solution.py:241
  48.2 0.9 %collective-permute-done.20 = bf16[32,1280]{1,0:T(8,128)(2,1)S(1)} collective-permute-done((bf16[32,1280]{1,0:T(8,128)(2,1)S(1)}, bf16[32,1280]{1,0:T(8,128)(2,1)S(1)}, u32[]{:S(2)}, u32[]{:S(2)}) %collective-permute-start.20) | collective-permute-done | bytes 81952 | tf_op jit(solution)/shard_map/ppermute | solution.py:241
  49.1 4.6 %collective-permute-done.21 = bf16[32,1280]{1,0:T(8,128)(2,1)S(1)} collective-permute-done((bf16[32,1280]{1,0:T(8,128)(2,1)S(1)}, bf16[32,1280]{1,0:T(8,128)(2,1)S(1)}, u32[]{:S(2)}, u32[]{:S(2)}) %collective-permute-start.21) | collective-permute-done | bytes 81952 | tf_op jit(solution)/shard_map/ppermute | solution.py:241
  53.7 0.9 %place.1 = bf16[4,8,8,1280]{3,2,1,0:T(8,128)(2,1)} custom-call(s32[1]{0:T(128)} %bitcast.me_ref, bf16[4,8,1280]{2,1,0:T(8,128)(2,1)S(1)} %bitcast.44, bf16[4,8,1280]{2,1,0:T(8,128)(2,1)S(1)} %bitcast.45, bf16[4,8,1280]{2,1,0:T(8,128)(2,1)S(1)} %bitcast.46, bf16[4,8,1280]{2,1,0:T(8,128)(2,1)S(1)} %bitcast.47, bf16[4,8,1280]{2,1,0:T(8,128)(2,1)S(1)} %bitcast.48, ...), custom_call_target="tpu_custom_call" | custom-call | tf_op jit(solution)/shard_map/place/pallas_call | solution.py:376
  (40 shorter events, 0.3 us)
Async XLA Ops:
  1.5 10.3 %collective-permute-start.7 = (f32[4,128]{1,0:T(4,128)S(1)}, f32[4,128]{1,0:T(4,128)S(1)}, u32[]{:S(2)}, u32[]{:S(2)}) collective-permute-start(f32[4,128]{1,0:T(4,128)S(1)} %get-tuple-element.36.refs_0_), channel_id=1, source_target_pairs={{0,3},{1,2},{2,1},{3,0},{4,7},{5,6},{6,5},{7,4},{8,11},{9,10},{10,... | collective-permute-start | bytes 6152 | tf_op jit(solution)/shard_map/ppermute | solution.py:241
  6.7 5.5 %collective-permute-start.8 = (f32[4,128]{1,0:T(4,128)S(1)}, f32[4,128]{1,0:T(4,128)S(1)}, u32[]{:S(2)}, u32[]{:S(2)}) collective-permute-start(f32[4,128]{1,0:T(4,128)S(1)} %get-tuple-element.36.refs_0_), channel_id=1, source_target_pairs={{0,2},{1,3},{2,0},{3,1},{4,6},{5,7},{6,4},{7,5},{8,10},{9,11},{10,... | collective-permute-start | bytes 6152 | tf_op jit(solution)/shard_map/ppermute | solution.py:241
  6.7 5.5 %collective-permute-start.9 = (f32[4,128]{1,0:T(4,128)S(1)}, f32[4,128]{1,0:T(4,128)S(1)}, u32[]{:S(2)}, u32[]{:S(2)}) collective-permute-start(f32[4,128]{1,0:T(4,128)S(1)} %get-tuple-element.36.refs_0_), channel_id=1, source_target_pairs={{0,1},{1,0},{2,3},{3,2},{4,5},{5,4},{6,7},{7,6},{8,9},{9,8},{10,11... | collective-permute-start | bytes 6152 | tf_op jit(solution)/shard_map/ppermute | solution.py:241
  8.5 6.5 %collective-permute-start.1 = (bf16[2,4,8,1280]{3,2,1,0:T(8,128)(2,1)S(1)}, bf16[2,4,8,1280]{3,2,1,0:T(8,128)(2,1)S(1)}, u32[]{:S(2)}, u32[]{:S(2)}) collective-permute-start(bf16[2,4,8,1280]{3,2,1,0:T(8,128)(2,1)S(1)} %get-tuple-element.28), channel_id=1, source_target_pairs={{0,8},{4,12},{8,0},{12,4},{16,24},{20,28},{24,16},{28,20},{1,9},{5... | collective-permute-start | bytes 491528 | tf_op jit(solution)/shard_map/ppermute | solution.py:241
  10.2 8.9 %collective-permute-start.3 = (bf16[2,4,8,1280]{3,2,1,0:T(8,128)(2,1)S(1)}, bf16[2,4,8,1280]{3,2,1,0:T(8,128)(2,1)S(1)}, u32[]{:S(2)}, u32[]{:S(2)}) collective-permute-start(bf16[2,4,8,1280]{3,2,1,0:T(8,128)(2,1)S(1)} %get-tuple-element.29), channel_id=1, source_target_pairs={{0,16},{4,20},{8,24},{12,28},{16,0},{20,4},{24,8},{28,12},{1,17},{... | collective-permute-start | bytes 491528 | tf_op jit(solution)/shard_map/ppermute | solution.py:241
  11.8 8.1 %collective-permute-start.5 = (bf16[2,4,8,1280]{3,2,1,0:T(8,128)(2,1)S(1)}, bf16[2,4,8,1280]{3,2,1,0:T(8,128)(2,1)S(1)}, u32[]{:S(2)}, u32[]{:S(2)}) collective-permute-start(bf16[2,4,8,1280]{3,2,1,0:T(8,128)(2,1)S(1)} %get-tuple-element.30), channel_id=1, source_target_pairs={{0,24},{4,28},{8,16},{12,20},{16,8},{20,12},{24,0},{28,4},{1,25},{... | collective-permute-start | bytes 491528 | tf_op jit(solution)/shard_map/ppermute | solution.py:241
  12.2 14.5 %collective-permute-start = (bf16[32,1280]{1,0:T(8,128)(2,1)S(1)}, bf16[32,1280]{1,0:T(8,128)(2,1)S(1)}, u32[]{:S(2)}, u32[]{:S(2)}) collective-permute-start(bf16[32,1280]{1,0:T(8,128)(2,1)S(1)} %slice_bitcast_fusion.7), channel_id=1, source_target_pairs={{0,4},{4,0},{8,12},{12,8},{16,20},{20,16},{24,28},{28,24},{1,5},{5... | collective-permute-start | bytes 245768 | tf_op jit(solution)/shard_map/ppermute | solution.py:241
  12.2 15.4 %copy-start = (bf16[1280,1280]{1,0:T(8,128)(2,1)S(1)}, bf16[1280,1280]{1,0:T(8,128)(2,1)}, u32[]{:S(2)}) copy-start(bf16[1280,1280]{1,0:T(8,128)(2,1)} %wq_ref.3) | copy-start | bytes 9830404
  12.2 15.4 %copy-start.1 = (bf16[1280,1280]{1,0:T(8,128)(2,1)S(1)}, bf16[1280,1280]{1,0:T(8,128)(2,1)}, u32[]{:S(2)}) copy-start(bf16[1280,1280]{1,0:T(8,128)(2,1)} %wk_ref.3) | copy-start | bytes 9830404
  12.2 15.4 %copy-start.2 = (bf16[1280,1280]{1,0:T(8,128)(2,1)S(1)}, bf16[1280,1280]{1,0:T(8,128)(2,1)}, u32[]{:S(2)}) copy-start(bf16[1280,1280]{1,0:T(8,128)(2,1)} %wv_ref.3) | copy-start | bytes 9830404
  12.2 15.4 %copy-start.3 = (f32[3,1280]{1,0:T(4,128)S(1)}, f32[3,1280]{1,0:T(4,128)}, u32[]{:S(2)}) copy-start(f32[3,1280]{1,0:T(4,128)} %taps_ref.3) | copy-start | bytes 46084
  12.2 15.4 %copy-start.4 = (f32[1280]{0:T(1024)S(1)}, f32[1280]{0:T(1024)}, u32[]{:S(2)}) copy-start(f32[1280]{0:T(1024)} %bias_ref.1) | copy-start | bytes 15364
  12.4 10.0 %collective-permute-start.11 = (bf16[2,4,8,1280]{3,2,1,0:T(8,128)(2,1)S(1)}, bf16[2,4,8,1280]{3,2,1,0:T(8,128)(2,1)S(1)}, u32[]{:S(2)}, u32[]{:S(2)}) collective-permute-start(bf16[2,4,8,1280]{3,2,1,0:T(8,128)(2,1)S(1)} %get-tuple-element.38), channel_id=1, source_target_pairs={{0,8},{4,12},{8,0},{12,4},{16,24},{20,28},{24,16},{28,20},{1,9},{5... | collective-permute-start | bytes 491528 | tf_op jit(solution)/shard_map/ppermute | solution.py:241
  15.0 11.1 %collective-permute-start.13 = (bf16[2,4,8,1280]{3,2,1,0:T(8,128)(2,1)S(1)}, bf16[2,4,8,1280]{3,2,1,0:T(8,128)(2,1)S(1)}, u32[]{:S(2)}, u32[]{:S(2)}) collective-permute-start(bf16[2,4,8,1280]{3,2,1,0:T(8,128)(2,1)S(1)} %get-tuple-element.39), channel_id=1, source_target_pairs={{0,16},{4,20},{8,24},{12,28},{16,0},{20,4},{24,8},{28,12},{1,17},{... | collective-permute-start | bytes 491528 | tf_op jit(solution)/shard_map/ppermute | solution.py:241
  19.1 7.0 %collective-permute-start.15 = (bf16[2,4,8,1280]{3,2,1,0:T(8,128)(2,1)S(1)}, bf16[2,4,8,1280]{3,2,1,0:T(8,128)(2,1)S(1)}, u32[]{:S(2)}, u32[]{:S(2)}) collective-permute-start(bf16[2,4,8,1280]{3,2,1,0:T(8,128)(2,1)S(1)} %get-tuple-element.40), channel_id=1, source_target_pairs={{0,24},{4,28},{8,16},{12,20},{16,8},{20,12},{24,0},{28,4},{1,25},{... | collective-permute-start | bytes 491528 | tf_op jit(solution)/shard_map/ppermute | solution.py:241
  19.9 11.8 %collective-permute-start.10 = (bf16[32,1280]{1,0:T(8,128)(2,1)S(1)}, bf16[32,1280]{1,0:T(8,128)(2,1)S(1)}, u32[]{:S(2)}, u32[]{:S(2)}) collective-permute-start(bf16[32,1280]{1,0:T(8,128)(2,1)S(1)} %slice_bitcast_fusion.6), channel_id=1, source_target_pairs={{0,4},{4,0},{8,12},{12,8},{16,20},{20,16},{24,28},{28,24},{1,5},{5... | collective-permute-start | bytes 245768 | tf_op jit(solution)/shard_map/ppermute | solution.py:241
  22.4 4.4 %collective-permute-start.2 = (bf16[32,1280]{1,0:T(8,128)(2,1)S(1)}, bf16[32,1280]{1,0:T(8,128)(2,1)S(1)}, u32[]{:S(2)}, u32[]{:S(2)}) collective-permute-start(bf16[32,1280]{1,0:T(8,128)(2,1)S(1)} %slice_bitcast_fusion.5), channel_id=1, source_target_pairs={{0,4},{4,0},{8,12},{12,8},{16,20},{20,16},{24,28},{28,24},{1,5},{5... | collective-permute-start | bytes 245768 | tf_op jit(solution)/shard_map/ppermute | solution.py:241
  26.1 1.3 %collective-permute-start.4 = (bf16[32,1280]{1,0:T(8,128)(2,1)S(1)}, bf16[32,1280]{1,0:T(8,128)(2,1)S(1)}, u32[]{:S(2)}, u32[]{:S(2)}) collective-permute-start(bf16[32,1280]{1,0:T(8,128)(2,1)S(1)} %slice_bitcast_fusion.4), channel_id=1, source_target_pairs={{0,4},{4,0},{8,12},{12,8},{16,20},{20,16},{24,28},{28,24},{1,5},{5... | collective-permute-start | bytes 245768 | tf_op jit(solution)/shard_map/ppermute | solution.py:241
  26.1 1.5 %collective-permute-start.6 = (bf16[32,1280]{1,0:T(8,128)(2,1)S(1)}, bf16[32,1280]{1,0:T(8,128)(2,1)S(1)}, u32[]{:S(2)}, u32[]{:S(2)}) collective-permute-start(bf16[32,1280]{1,0:T(8,128)(2,1)S(1)} %slice_bitcast_fusion.3), channel_id=1, source_target_pairs={{0,4},{4,0},{8,12},{12,8},{16,20},{20,16},{24,28},{28,24},{1,5},{5... | collective-permute-start | bytes 245768 | tf_op jit(solution)/shard_map/ppermute | solution.py:241
  26.7 4.9 %collective-permute-start.12 = (bf16[32,1280]{1,0:T(8,128)(2,1)S(1)}, bf16[32,1280]{1,0:T(8,128)(2,1)S(1)}, u32[]{:S(2)}, u32[]{:S(2)}) collective-permute-start(bf16[32,1280]{1,0:T(8,128)(2,1)S(1)} %slice_bitcast_fusion.2), channel_id=1, source_target_pairs={{0,4},{4,0},{8,12},{12,8},{16,20},{20,16},{24,28},{28,24},{1,5},{5... | collective-permute-start | bytes 245768 | tf_op jit(solution)/shard_map/ppermute | solution.py:241
  26.8 4.8 %collective-permute-start.14 = (bf16[32,1280]{1,0:T(8,128)(2,1)S(1)}, bf16[32,1280]{1,0:T(8,128)(2,1)S(1)}, u32[]{:S(2)}, u32[]{:S(2)}) collective-permute-start(bf16[32,1280]{1,0:T(8,128)(2,1)S(1)} %slice_bitcast_fusion.1), channel_id=1, source_target_pairs={{0,4},{4,0},{8,12},{12,8},{16,20},{20,16},{24,28},{28,24},{1,5},{5... | collective-permute-start | bytes 245768 | tf_op jit(solution)/shard_map/ppermute | solution.py:241
  27.4 4.3 %collective-permute-start.16 = (bf16[32,1280]{1,0:T(8,128)(2,1)S(1)}, bf16[32,1280]{1,0:T(8,128)(2,1)S(1)}, u32[]{:S(2)}, u32[]{:S(2)}) collective-permute-start(bf16[32,1280]{1,0:T(8,128)(2,1)S(1)} %slice_bitcast_fusion), channel_id=1, source_target_pairs={{0,4},{4,0},{8,12},{12,8},{16,20},{20,16},{24,28},{28,24},{1,5},{5... | collective-permute-start | bytes 245768 | tf_op jit(solution)/shard_map/ppermute | solution.py:241
  41.9 3.9 %collective-permute-start.17 = (bf16[32,1280]{1,0:T(8,128)(2,1)S(1)}, bf16[32,1280]{1,0:T(8,128)(2,1)S(1)}, u32[]{:S(2)}, u32[]{:S(2)}) collective-permute-start(bf16[32,1280]{1,0:T(8,128)(2,1)S(1)} %get-tuple-element.42), channel_id=1, source_target_pairs={{0,4},{4,0},{8,12},{12,8},{16,20},{20,16},{24,28},{28,24},{1,5},{5... | collective-permute-start | bytes 245768 | tf_op jit(solution)/shard_map/ppermute | solution.py:241
  42.3 5.3 %collective-permute-start.18 = (bf16[32,1280]{1,0:T(8,128)(2,1)S(1)}, bf16[32,1280]{1,0:T(8,128)(2,1)S(1)}, u32[]{:S(2)}, u32[]{:S(2)}) collective-permute-start(bf16[32,1280]{1,0:T(8,128)(2,1)S(1)} %get-tuple-element.43), channel_id=1, source_target_pairs={{0,8},{4,12},{8,0},{12,4},{16,24},{20,28},{24,16},{28,20},{1,9},{5... | collective-permute-start | bytes 245768 | tf_op jit(solution)/shard_map/ppermute | solution.py:241
  42.7 5.5 %collective-permute-start.19 = (bf16[32,1280]{1,0:T(8,128)(2,1)S(1)}, bf16[32,1280]{1,0:T(8,128)(2,1)S(1)}, u32[]{:S(2)}, u32[]{:S(2)}) collective-permute-start(bf16[32,1280]{1,0:T(8,128)(2,1)S(1)} %get-tuple-element.44), channel_id=1, source_target_pairs={{0,12},{4,8},{8,4},{12,0},{16,28},{20,24},{24,20},{28,16},{1,13},{... | collective-permute-start | bytes 245768 | tf_op jit(solution)/shard_map/ppermute | solution.py:241
  43.8 5.3 %collective-permute-start.20 = (bf16[32,1280]{1,0:T(8,128)(2,1)S(1)}, bf16[32,1280]{1,0:T(8,128)(2,1)S(1)}, u32[]{:S(2)}, u32[]{:S(2)}) collective-permute-start(bf16[32,1280]{1,0:T(8,128)(2,1)S(1)} %get-tuple-element.45), channel_id=1, source_target_pairs={{0,16},{4,20},{8,24},{12,28},{16,0},{20,4},{24,8},{28,12},{1,17},{... | collective-permute-start | bytes 245768 | tf_op jit(solution)/shard_map/ppermute | solution.py:241
  44.7 9.0 %collective-permute-start.21 = (bf16[32,1280]{1,0:T(8,128)(2,1)S(1)}, bf16[32,1280]{1,0:T(8,128)(2,1)S(1)}, u32[]{:S(2)}, u32[]{:S(2)}) collective-permute-start(bf16[32,1280]{1,0:T(8,128)(2,1)S(1)} %get-tuple-element.46), channel_id=1, source_target_pairs={{0,20},{4,16},{8,28},{12,24},{16,4},{20,0},{24,12},{28,8},{1,21},{... | collective-permute-start | bytes 245768 | tf_op jit(solution)/shard_map/ppermute | solution.py:241
  45.8 7.9 %collective-permute-start.22 = (bf16[32,1280]{1,0:T(8,128)(2,1)S(1)}, bf16[32,1280]{1,0:T(8,128)(2,1)S(1)}, u32[]{:S(2)}, u32[]{:S(2)}) collective-permute-start(bf16[32,1280]{1,0:T(8,128)(2,1)S(1)} %get-tuple-element.47), channel_id=1, source_target_pairs={{0,24},{4,28},{8,16},{12,20},{16,8},{20,12},{24,0},{28,4},{1,25},{... | collective-permute-start | bytes 245768 | tf_op jit(solution)/shard_map/ppermute | solution.py:241
  47.6 6.1 %collective-permute-start.23 = (bf16[32,1280]{1,0:T(8,128)(2,1)S(1)}, bf16[32,1280]{1,0:T(8,128)(2,1)S(1)}, u32[]{:S(2)}, u32[]{:S(2)}) collective-permute-start(bf16[32,1280]{1,0:T(8,128)(2,1)S(1)} %get-tuple-element.48), channel_id=1, source_target_pairs={{0,28},{4,24},{8,20},{12,16},{16,12},{20,8},{24,4},{28,0},{1,29},{... | collective-permute-start | bytes 245768 | tf_op jit(solution)/shard_map/ppermute | solution.py:241

commit v2 on v0

--- a/solution.py
+++ b/solution.py
@@ -82,26 +82,17 @@
         copy.wait()
 
 
-def scale_kernel(me_ref, energy_ref, other_ref, cotangent_ref, *outs, peers, count):
-    me = me_ref[0]
-    factor = lax.rsqrt((energy_ref[...] + other_ref[...]) / count + 1e-06)
-    frame_rows = cotangent_ref.shape[0]
+def scale_kernel(me_ref, held_ref, *refs, peers, count):
+    energies, outs = refs[:-(peers // 2)], refs[-(peers // 2):]
+    me = me_ref[0]
+    factor = lax.rsqrt(sum(energy[...] for energy in energies) / count + 1e-06)
+    frame_rows = held_ref.shape[0]
     for mask in range(peers):
         for frame in range(frame_rows):
-            grad = cotangent_ref[frame, me ^ mask].astype(jnp.float32)
+            grad = held_ref[frame, me ^ mask].astype(jnp.float32)
             outs[mask // 2][mask % 2, frame] = (
                 grad * factor[frame:frame + 1, :1]
             ).astype(jnp.bfloat16)
-
-
-def load_kernel(*refs):
-    count = len(refs) // 2
-    sems = refs[-1]
-    copies = [pltpu.make_async_copy(refs[i], refs[count + i], sems.at[i]) for i in range(count)]
-    for copy in copies:
-        copy.start()
-    for copy in copies:
-        copy.wait()
 
 
 def place_kernel(me_ref, *refs, peers):
@@ -285,14 +276,12 @@
     return received
 
 
-def tile_sum(value):
-    mask = 1
-    other = jnp.zeros_like(value)
-    while mask < lax.axis_size("tile"):
-        value = value + other if mask > 1 else value
-        other = swap(value, "tile", mask)
-        mask *= 2
-    return value, other
+def tile_terms(value):
+    terms = [value]
+    for stage in range(lax.axis_size("tile").bit_length() - 1):
+        value = sum(terms[1:], terms[0])
+        terms = [value, swap(value, "tile", 1 << stage)]
+    return terms
 
 
 def body(tokens, cotangent, w_query, w_key, w_value, conv_taps, conv_bias):
@@ -323,28 +312,20 @@
         compiler_params=grant(8),
         name="pack",
     )(me_arg, off_chip(tokens.reshape(split)), off_chip(cotangent.reshape(split)))
-    energy_here, energy_there = tile_sum(energy)
     token_blocks = gather_tokens(sent_tokens)
+    terms = tile_terms(energy)
     sent_grads = pl.pallas_call(
         functools.partial(scale_kernel, peers=peers, count=spatial_all * channels),
-        in_specs=[smem, vmem, vmem, vmem],
+        in_specs=[smem] + [vmem] * (1 + len(terms)),
         out_specs=[vmem] * (peers // 2),
         out_shape=[sent_shape] * (peers // 2),
         compiler_params=grant(8),
+        cost_estimate=pl.CostEstimate(flops=1 << 34, bytes_accessed=1 << 25, transcendentals=0),
         name="scale",
-    )(me_arg, on_chip(energy_here), on_chip(energy_there), on_chip(held))
+    )(me_arg, on_chip(held), *map(on_chip, terms))
     grad_blocks = gather_tokens(sent_grads)
 
-    parameters = (conv_taps, conv_bias, w_query, w_key, w_value)
-    conv_taps, conv_bias, *weights = map(on_chip, pl.pallas_call(
-        load_kernel,
-        in_specs=[hbm] * len(parameters),
-        out_specs=[vmem] * len(parameters),
-        out_shape=[pltpu.VMEM(value.shape, value.dtype) for value in parameters],
-        scratch_shapes=[pltpu.SemaphoreType.DMA((len(parameters),))],
-        compiler_params=grant(4),
-        name="load",
-    )(*map(off_chip, parameters)))
+    weights = (w_query, w_key, w_value)
     sizes = dict(frames=frames, toks=toks, peers=peers)
     query, key, value, prob = pl.pallas_call(
         functools.partial(forward_kernel, **sizes),

time: 55.6 us -> 51.8 us (0.932)
  Pallas kernels: 20.8 us -> 16.8 us
    pallas_call x1 -> x0, Pallas kernels: 3.93 us -> none  [body(): pl.pallas_call(load_kernel, in_specs=[hbm] * len(parameters), out_specs=[...]
  transfers between devices with their start and end apart: 23 -> 23, of which waited for: 7 -> 8; matrix products, arithmetic and copies ran while one was open for 0% -> 0% of each run, Pallas kernels for 15% -> 8%
where the time goes in v2:
time: 51.8 us; the launch traced here: 51.7 us
  starting transfers between devices  19.6 us (38%)
  Pallas kernels  16.8 us (32%)
  waiting for transfers between devices  15 us (29%)
    ppermute x23, starting transfers between devices, swap(): lax.ppermute(value, axis, [(i, i ^ mask) for i in range(lax.axis_size(axi...  19.6 us
    ppermute x23, waiting for transfers between devices, swap(): lax.ppermute(value, axis, [(i, i ^ mask) for i in range(lax.axis_size(axi...  15 us
    pallas_call x1, Pallas kernels, body(): pl.pallas_call(functools.partial(backward_kernel, **sizes), in_specs=[sme...  10.2 us
    pallas_call x1, Pallas kernels, body(): pl.pallas_call(functools.partial(forward_kernel, **sizes), in_specs=[smem...  3.98 us
    pallas_call x1, Pallas kernels, body(): pl.pallas_call(functools.partial(pack_kernel, peers=peers), in_specs=[sme...  1.58 us
  transfers between devices with their start and end apart: 23, of which 8 were waited for; matrix products, arithmetic and copies ran while one was open for 0% of the time, Pallas kernels for 8%

profile of v2, /device:TPU:0, one launch (start us, length us, event | category | flops | bytes accessed | tf_op | source)
XLA Modules:
  0.0 51.7 jit_solution(15023086663404491886)
XLA Ops:
  0.0 1.6 %pack.1 = (bf16[2,4,8,1280]{3,2,1,0:T(8,128)(2,1)S(1)}, bf16[2,4,8,1280]{3,2,1,0:T(8,128)(2,1)S(1)}, bf16[2,4,8,1280]{3,2,1,0:T(8,128)(2,1)S(1)}, bf16[2,4,8,128...) custom-call(s32[1]{0:T(128)} %bitcast.me_ref, bf16[4,8,8,1280]{3,2,1,0:T(8,128)(2,1)} %bitcast.52, ...), custom_call_target="tpu_custom_call" | custom-call | tf_op jit(solution)/shard_map/pack/pallas_call | solution.py:305
  1.6 3.1 %collective-permute-start.7 = (f32[4,128]{1,0:T(4,128)S(1)}, f32[4,128]{1,0:T(4,128)S(1)}, u32[]{:S(2)}, u32[]{:S(2)}) collective-permute-start(f32[4,128]{1,0:T(4,128)S(1)} %get-tuple-element.36), channel_id=1, source_target_pairs={{0,1},{1,0},{2,3},{3,2},{4,5},{5,4},{6,7},{7,6},{8,9},{9,8},{10,11... | collective-permute-start | bytes 6152 | tf_op jit(solution)/shard_map/ppermute | solution.py:237
  4.7 1.5 %collective-permute-start.1 = (bf16[2,4,8,1280]{3,2,1,0:T(8,128)(2,1)S(1)}, bf16[2,4,8,1280]{3,2,1,0:T(8,128)(2,1)S(1)}, u32[]{:S(2)}, u32[]{:S(2)}) collective-permute-start(bf16[2,4,8,1280]{3,2,1,0:T(8,128)(2,1)S(1)} %get-tuple-element.28), channel_id=1, source_target_pairs={{0,8},{4,12},{8,0},{12,4},{16,24},{20,28},{24,16},{28,20},{1,9},{5... | collective-permute-start | bytes 491528 | tf_op jit(solution)/shard_map/ppermute | solution.py:237
  6.2 1.5 %collective-permute-start.3 = (bf16[2,4,8,1280]{3,2,1,0:T(8,128)(2,1)S(1)}, bf16[2,4,8,1280]{3,2,1,0:T(8,128)(2,1)S(1)}, u32[]{:S(2)}, u32[]{:S(2)}) collective-permute-start(bf16[2,4,8,1280]{3,2,1,0:T(8,128)(2,1)S(1)} %get-tuple-element.29), channel_id=1, source_target_pairs={{0,16},{4,20},{8,24},{12,28},{16,0},{20,4},{24,8},{28,12},{1,17},{... | collective-permute-start | bytes 491528 | tf_op jit(solution)/shard_map/ppermute | solution.py:237
  7.7 0.5 collective-permute-start.5
  8.2 2.6 %collective-permute-start.8 = (f32[4,128]{1,0:T(4,128)S(1)}, f32[4,128]{1,0:T(4,128)S(1)}, u32[]{:S(2)}, u32[]{:S(2)}) collective-permute-start(f32[4,128]{1,0:T(4,128)S(1)} %add.3.refs_0_), channel_id=1, source_target_pairs={{0,2},{1,3},{2,0},{3,1},{4,6},{5,7},{6,4},{7,5},{8,10},{9,11},{10,... | collective-permute-start | bytes 6152 | tf_op jit(solution)/shard_map/ppermute | solution.py:237
  10.8 1.9 %collective-permute-done.8.refs_1_ = f32[4,128]{1,0:T(4,128)S(1)} collective-permute-done((f32[4,128]{1,0:T(4,128)S(1)}, f32[4,128]{1,0:T(4,128)S(1)}, u32[]{:S(2)}, u32[]{:S(2)}) %collective-permute-start.8) | collective-permute-done | bytes 2080 | tf_op jit(solution)/shard_map/ppermute | solution.py:237
  12.7 0.2 scale.1
  12.9 1.6 %collective-permute-start.10 = (bf16[2,4,8,1280]{3,2,1,0:T(8,128)(2,1)S(1)}, bf16[2,4,8,1280]{3,2,1,0:T(8,128)(2,1)S(1)}, u32[]{:S(2)}, u32[]{:S(2)}) collective-permute-start(bf16[2,4,8,1280]{3,2,1,0:T(8,128)(2,1)S(1)} %get-tuple-element.38), channel_id=1, source_target_pairs={{0,8},{4,12},{8,0},{12,4},{16,24},{20,28},{24,16},{28,20},{1,9},{5... | collective-permute-start | bytes 491528 | tf_op jit(solution)/shard_map/ppermute | solution.py:237
  14.4 1.6 %collective-permute-start.12 = (bf16[2,4,8,1280]{3,2,1,0:T(8,128)(2,1)S(1)}, bf16[2,4,8,1280]{3,2,1,0:T(8,128)(2,1)S(1)}, u32[]{:S(2)}, u32[]{:S(2)}) collective-permute-start(bf16[2,4,8,1280]{3,2,1,0:T(8,128)(2,1)S(1)} %get-tuple-element.39), channel_id=1, source_target_pairs={{0,16},{4,20},{8,24},{12,28},{16,0},{20,4},{24,8},{28,12},{1,17},{... | collective-permute-start | bytes 491528 | tf_op jit(solution)/shard_map/ppermute | solution.py:237
  16.0 0.5 %collective-permute-start.14 = (bf16[2,4,8,1280]{3,2,1,0:T(8,128)(2,1)S(1)}, bf16[2,4,8,1280]{3,2,1,0:T(8,128)(2,1)S(1)}, u32[]{:S(2)}, u32[]{:S(2)}) collective-permute-start(bf16[2,4,8,1280]{3,2,1,0:T(8,128)(2,1)S(1)} %get-tuple-element.40), channel_id=1, source_target_pairs={{0,24},{4,28},{8,16},{12,20},{16,8},{20,12},{24,0},{28,4},{1,25},{... | collective-permute-start | bytes 491528 | tf_op jit(solution)/shard_map/ppermute | solution.py:237
  16.6 0.1 collective-permute-start.9
  16.7 3.1 %collective-permute-done.10 = bf16[2,4,8,1280]{3,2,1,0:T(8,128)(2,1)S(1)} collective-permute-done((bf16[2,4,8,1280]{3,2,1,0:T(8,128)(2,1)S(1)}, bf16[2,4,8,1280]{3,2,1,0:T(8,128)(2,1)S(1)}, u32[]{:S(2)}, u32[]{:S(2)}) %collective-permute-start.10) | collective-permute-done | bytes 163872 | tf_op jit(solution)/shard_map/ppermute | solution.py:237
  19.8 3.3 %collective-permute-done.12 = bf16[2,4,8,1280]{3,2,1,0:T(8,128)(2,1)S(1)} collective-permute-done((bf16[2,4,8,1280]{3,2,1,0:T(8,128)(2,1)S(1)}, bf16[2,4,8,1280]{3,2,1,0:T(8,128)(2,1)S(1)}, u32[]{:S(2)}, u32[]{:S(2)}) %collective-permute-start.12) | collective-permute-done | bytes 163872 | tf_op jit(solution)/shard_map/ppermute | solution.py:237
  23.2 0.6 %collective-permute-start.6 = (bf16[32,1280]{1,0:T(8,128)(2,1)S(1)}, bf16[32,1280]{1,0:T(8,128)(2,1)S(1)}, u32[]{:S(2)}, u32[]{:S(2)}) collective-permute-start(bf16[32,1280]{1,0:T(8,128)(2,1)S(1)} %slice_bitcast_fusion.3), channel_id=1, source_target_pairs={{0,4},{4,0},{8,12},{12,8},{16,20},{20,16},{24,28},{28,24},{1,5},{5... | collective-permute-start | bytes 245768 | tf_op jit(solution)/shard_map/ppermute | solution.py:237
  23.7 0.1 collective-permute-start.11
  23.8 0.5 collective-permute-start.13
  24.3 0.1 collective-permute-done.4.refs_5_
  24.4 0.2 collective-permute-start.15
  24.6 0.1 collective-permute-done.6.refs_7_
  24.7 4.0 %forward.1 = (bf16[256,1280]{1,0:T(8,128)(2,1)S(1)}, bf16[256,1280]{1,0:T(8,128)(2,1)S(1)}, bf16[256,1280]{1,0:T(8,128)(2,1)S(1)}, f32[20,32,256]{2,1,0:T(8,128)S(1)}) custom-call(s32[1]{0:T(128)} %bitcast.me_ref, f32[3,1280]{1,0:T(4,128)S(1)} %copy-done.3, f32[1280]{0:T(1024)S(1)} %copy-done.4, bf16[1280,1280]{1,0:T(8,128)(2,1)S(1)} %copy-done, ...), custom_call_target="tpu_custom_call" | custom-call | tf_op jit(solution)/shard_map/forward/pallas_call | solution.py:330
  28.7 10.2 %backward.1 = (bf16[32,1280]{1,0:T(8,128)(2,1)S(1)}, bf16[32,1280]{1,0:T(8,128)(2,1)S(1)}, bf16[32,1280]{1,0:T(8,128)(2,1)S(1)}, bf16[32,1280]{1,0:T(8,128)(2,1)...) custom-call(s32[1]{0:T(128)} %bitcast.me_ref, ...), custom_call_target="tpu_custom_call" | custom-call | tf_op jit(solution)/shard_map/backward/pallas_call | solution.py:341
  38.9 0.4 collective-permute-start.16
  39.4 1.4 %collective-permute-start.18 = (bf16[32,1280]{1,0:T(8,128)(2,1)S(1)}, bf16[32,1280]{1,0:T(8,128)(2,1)S(1)}, u32[]{:S(2)}, u32[]{:S(2)}) collective-permute-start(bf16[32,1280]{1,0:T(8,128)(2,1)S(1)} %get-tuple-element.44), channel_id=1, source_target_pairs={{0,12},{4,8},{8,4},{12,0},{16,28},{20,24},{24,20},{28,16},{1,13},{... | collective-permute-start | bytes 245768 | tf_op jit(solution)/shard_map/ppermute | solution.py:237
  40.8 1.0 %collective-permute-start.19 = (bf16[32,1280]{1,0:T(8,128)(2,1)S(1)}, bf16[32,1280]{1,0:T(8,128)(2,1)S(1)}, u32[]{:S(2)}, u32[]{:S(2)}) collective-permute-start(bf16[32,1280]{1,0:T(8,128)(2,1)S(1)} %get-tuple-element.45), channel_id=1, source_target_pairs={{0,16},{4,20},{8,24},{12,28},{16,0},{20,4},{24,8},{28,12},{1,17},{... | collective-permute-start | bytes 245768 | tf_op jit(solution)/shard_map/ppermute | solution.py:237
  41.9 1.0 %collective-permute-start.20 = (bf16[32,1280]{1,0:T(8,128)(2,1)S(1)}, bf16[32,1280]{1,0:T(8,128)(2,1)S(1)}, u32[]{:S(2)}, u32[]{:S(2)}) collective-permute-start(bf16[32,1280]{1,0:T(8,128)(2,1)S(1)} %get-tuple-element.46), channel_id=1, source_target_pairs={{0,20},{4,16},{8,28},{12,24},{16,4},{20,0},{24,12},{28,8},{1,21},{... | collective-permute-start | bytes 245768 | tf_op jit(solution)/shard_map/ppermute | solution.py:237
  42.8 0.8 %collective-permute-start.21 = (bf16[32,1280]{1,0:T(8,128)(2,1)S(1)}, bf16[32,1280]{1,0:T(8,128)(2,1)S(1)}, u32[]{:S(2)}, u32[]{:S(2)}) collective-permute-start(bf16[32,1280]{1,0:T(8,128)(2,1)S(1)} %get-tuple-element.47), channel_id=1, source_target_pairs={{0,24},{4,28},{8,16},{12,20},{16,8},{20,12},{24,0},{28,4},{1,25},{... | collective-permute-start | bytes 245768 | tf_op jit(solution)/shard_map/ppermute | solution.py:237
  43.7 1.0 %collective-permute-done.17 = bf16[32,1280]{1,0:T(8,128)(2,1)S(1)} collective-permute-done((bf16[32,1280]{1,0:T(8,128)(2,1)S(1)}, bf16[32,1280]{1,0:T(8,128)(2,1)S(1)}, u32[]{:S(2)}, u32[]{:S(2)}) %collective-permute-start.17) | collective-permute-done | bytes 81952 | tf_op jit(solution)/shard_map/ppermute | solution.py:237
  44.7 0.6 %collective-permute-start.22 = (bf16[32,1280]{1,0:T(8,128)(2,1)S(1)}, bf16[32,1280]{1,0:T(8,128)(2,1)S(1)}, u32[]{:S(2)}, u32[]{:S(2)}) collective-permute-start(bf16[32,1280]{1,0:T(8,128)(2,1)S(1)} %get-tuple-element.48), channel_id=1, source_target_pairs={{0,28},{4,24},{8,20},{12,16},{16,12},{20,8},{24,4},{28,0},{1,29},{... | collective-permute-start | bytes 245768 | tf_op jit(solution)/shard_map/ppermute | solution.py:237
  45.3 0.9 %collective-permute-done.19 = bf16[32,1280]{1,0:T(8,128)(2,1)S(1)} collective-permute-done((bf16[32,1280]{1,0:T(8,128)(2,1)S(1)}, bf16[32,1280]{1,0:T(8,128)(2,1)S(1)}, u32[]{:S(2)}, u32[]{:S(2)}) %collective-permute-start.19) | collective-permute-done | bytes 81952 | tf_op jit(solution)/shard_map/ppermute | solution.py:237
  46.2 4.6 %collective-permute-done.20 = bf16[32,1280]{1,0:T(8,128)(2,1)S(1)} collective-permute-done((bf16[32,1280]{1,0:T(8,128)(2,1)S(1)}, bf16[32,1280]{1,0:T(8,128)(2,1)S(1)}, u32[]{:S(2)}, u32[]{:S(2)}) %collective-permute-start.20) | collective-permute-done | bytes 81952 | tf_op jit(solution)/shard_map/ppermute | solution.py:237
  50.8 0.9 %place.1 = bf16[4,8,8,1280]{3,2,1,0:T(8,128)(2,1)} custom-call(s32[1]{0:T(128)} %bitcast.me_ref, bf16[4,8,1280]{2,1,0:T(8,128)(2,1)S(1)} %bitcast.44, bf16[4,8,1280]{2,1,0:T(8,128)(2,1)S(1)} %bitcast.45, bf16[4,8,1280]{2,1,0:T(8,128)(2,1)S(1)} %bitcast.46, bf16[4,8,1280]{2,1,0:T(8,128)(2,1)S(1)} %bitcast.47, bf16[4,8,1280]{2,1,0:T(8,128)(2,1)S(1)} %bitcast.48, ...), custom_call_target="tpu_custom_call" | custom-call | tf_op jit(solution)/shard_map/place/pallas_call | solution.py:355
  (38 shorter events, 0.2 us)
Async XLA Ops:
  1.6 6.6 %collective-permute-start.7 = (f32[4,128]{1,0:T(4,128)S(1)}, f32[4,128]{1,0:T(4,128)S(1)}, u32[]{:S(2)}, u32[]{:S(2)}) collective-permute-start(f32[4,128]{1,0:T(4,128)S(1)} %get-tuple-element.36), channel_id=1, source_target_pairs={{0,1},{1,0},{2,3},{3,2},{4,5},{5,4},{6,7},{7,6},{8,9},{9,8},{10,11... | collective-permute-start | bytes 6152 | tf_op jit(solution)/shard_map/ppermute | solution.py:237
  4.7 9.7 %collective-permute-start.1 = (bf16[2,4,8,1280]{3,2,1,0:T(8,128)(2,1)S(1)}, bf16[2,4,8,1280]{3,2,1,0:T(8,128)(2,1)S(1)}, u32[]{:S(2)}, u32[]{:S(2)}) collective-permute-start(bf16[2,4,8,1280]{3,2,1,0:T(8,128)(2,1)S(1)} %get-tuple-element.28), channel_id=1, source_target_pairs={{0,8},{4,12},{8,0},{12,4},{16,24},{20,28},{24,16},{28,20},{1,9},{5... | collective-permute-start | bytes 491528 | tf_op jit(solution)/shard_map/ppermute | solution.py:237
  6.2 9.8 %collective-permute-start.3 = (bf16[2,4,8,1280]{3,2,1,0:T(8,128)(2,1)S(1)}, bf16[2,4,8,1280]{3,2,1,0:T(8,128)(2,1)S(1)}, u32[]{:S(2)}, u32[]{:S(2)}) collective-permute-start(bf16[2,4,8,1280]{3,2,1,0:T(8,128)(2,1)S(1)} %get-tuple-element.29), channel_id=1, source_target_pairs={{0,16},{4,20},{8,24},{12,28},{16,0},{20,4},{24,8},{28,12},{1,17},{... | collective-permute-start | bytes 491528 | tf_op jit(solution)/shard_map/ppermute | solution.py:237
  7.7 8.9 %collective-permute-start.5 = (bf16[2,4,8,1280]{3,2,1,0:T(8,128)(2,1)S(1)}, bf16[2,4,8,1280]{3,2,1,0:T(8,128)(2,1)S(1)}, u32[]{:S(2)}, u32[]{:S(2)}) collective-permute-start(bf16[2,4,8,1280]{3,2,1,0:T(8,128)(2,1)S(1)} %get-tuple-element.30), channel_id=1, source_target_pairs={{0,24},{4,28},{8,16},{12,20},{16,8},{20,12},{24,0},{28,4},{1,25},{... | collective-permute-start | bytes 491528 | tf_op jit(solution)/shard_map/ppermute | solution.py:237
  8.2 4.5 %collective-permute-start.8 = (f32[4,128]{1,0:T(4,128)S(1)}, f32[4,128]{1,0:T(4,128)S(1)}, u32[]{:S(2)}, u32[]{:S(2)}) collective-permute-start(f32[4,128]{1,0:T(4,128)S(1)} %add.3.refs_0_), channel_id=1, source_target_pairs={{0,2},{1,3},{2,0},{3,1},{4,6},{5,7},{6,4},{7,5},{8,10},{9,11},{10,... | collective-permute-start | bytes 6152 | tf_op jit(solution)/shard_map/ppermute | solution.py:237
  10.8 12.9 %collective-permute-start = (bf16[32,1280]{1,0:T(8,128)(2,1)S(1)}, bf16[32,1280]{1,0:T(8,128)(2,1)S(1)}, u32[]{:S(2)}, u32[]{:S(2)}) collective-permute-start(bf16[32,1280]{1,0:T(8,128)(2,1)S(1)} %slice_bitcast_fusion.7), channel_id=1, source_target_pairs={{0,4},{4,0},{8,12},{12,8},{16,20},{20,16},{24,28},{28,24},{1,5},{5... | collective-permute-start | bytes 245768 | tf_op jit(solution)/shard_map/ppermute | solution.py:237
  12.7 12.0 %copy-start = (bf16[1280,1280]{1,0:T(8,128)(2,1)S(1)}, bf16[1280,1280]{1,0:T(8,128)(2,1)}, u32[]{:S(2)}) copy-start(bf16[1280,1280]{1,0:T(8,128)(2,1)} %wq_ref.3) | copy-start | bytes 9830404
  12.7 12.0 %copy-start.1 = (bf16[1280,1280]{1,0:T(8,128)(2,1)S(1)}, bf16[1280,1280]{1,0:T(8,128)(2,1)}, u32[]{:S(2)}) copy-start(bf16[1280,1280]{1,0:T(8,128)(2,1)} %wk_ref.3) | copy-start | bytes 9830404
  12.7 12.0 %copy-start.2 = (bf16[1280,1280]{1,0:T(8,128)(2,1)S(1)}, bf16[1280,1280]{1,0:T(8,128)(2,1)}, u32[]{:S(2)}) copy-start(bf16[1280,1280]{1,0:T(8,128)(2,1)} %wv_ref.3) | copy-start | bytes 9830404
  12.7 12.0 %copy-start.3 = (f32[3,1280]{1,0:T(4,128)S(1)}, f32[3,1280]{1,0:T(4,128)}, u32[]{:S(2)}) copy-start(f32[3,1280]{1,0:T(4,128)} %taps_ref.3) | copy-start | bytes 46084
  12.7 12.0 %copy-start.4 = (f32[1280]{0:T(1024)S(1)}, f32[1280]{0:T(1024)}, u32[]{:S(2)}) copy-start(f32[1280]{0:T(1024)} %bias_ref.1) | copy-start | bytes 15364
  12.9 6.9 %collective-permute-start.10 = (bf16[2,4,8,1280]{3,2,1,0:T(8,128)(2,1)S(1)}, bf16[2,4,8,1280]{3,2,1,0:T(8,128)(2,1)S(1)}, u32[]{:S(2)}, u32[]{:S(2)}) collective-permute-start(bf16[2,4,8,1280]{3,2,1,0:T(8,128)(2,1)S(1)} %get-tuple-element.38), channel_id=1, source_target_pairs={{0,8},{4,12},{8,0},{12,4},{16,24},{20,28},{24,16},{28,20},{1,9},{5... | collective-permute-start | bytes 491528 | tf_op jit(solution)/shard_map/ppermute | solution.py:237
  14.4 8.7 %collective-permute-start.12 = (bf16[2,4,8,1280]{3,2,1,0:T(8,128)(2,1)S(1)}, bf16[2,4,8,1280]{3,2,1,0:T(8,128)(2,1)S(1)}, u32[]{:S(2)}, u32[]{:S(2)}) collective-permute-start(bf16[2,4,8,1280]{3,2,1,0:T(8,128)(2,1)S(1)} %get-tuple-element.39), channel_id=1, source_target_pairs={{0,16},{4,20},{8,24},{12,28},{16,0},{20,4},{24,8},{28,12},{1,17},{... | collective-permute-start | bytes 491528 | tf_op jit(solution)/shard_map/ppermute | solution.py:237
  16.0 7.1 %collective-permute-start.14 = (bf16[2,4,8,1280]{3,2,1,0:T(8,128)(2,1)S(1)}, bf16[2,4,8,1280]{3,2,1,0:T(8,128)(2,1)S(1)}, u32[]{:S(2)}, u32[]{:S(2)}) collective-permute-start(bf16[2,4,8,1280]{3,2,1,0:T(8,128)(2,1)S(1)} %get-tuple-element.40), channel_id=1, source_target_pairs={{0,24},{4,28},{8,16},{12,20},{16,8},{20,12},{24,0},{28,4},{1,25},{... | collective-permute-start | bytes 491528 | tf_op jit(solution)/shard_map/ppermute | solution.py:237
  16.6 12.1 %collective-permute-start.9 = (bf16[32,1280]{1,0:T(8,128)(2,1)S(1)}, bf16[32,1280]{1,0:T(8,128)(2,1)S(1)}, u32[]{:S(2)}, u32[]{:S(2)}) collective-permute-start(bf16[32,1280]{1,0:T(8,128)(2,1)S(1)} %slice_bitcast_fusion.6), channel_id=1, source_target_pairs={{0,4},{4,0},{8,12},{12,8},{16,20},{20,16},{24,28},{28,24},{1,5},{5... | collective-permute-start | bytes 245768 | tf_op jit(solution)/shard_map/ppermute | solution.py:237
  19.8 4.0 %collective-permute-start.2 = (bf16[32,1280]{1,0:T(8,128)(2,1)S(1)}, bf16[32,1280]{1,0:T(8,128)(2,1)S(1)}, u32[]{:S(2)}, u32[]{:S(2)}) collective-permute-start(bf16[32,1280]{1,0:T(8,128)(2,1)S(1)} %slice_bitcast_fusion.5), channel_id=1, source_target_pairs={{0,4},{4,0},{8,12},{12,8},{16,20},{20,16},{24,28},{28,24},{1,5},{5... | collective-permute-start | bytes 245768 | tf_op jit(solution)/shard_map/ppermute | solution.py:237
  23.1 1.3 %collective-permute-start.4 = (bf16[32,1280]{1,0:T(8,128)(2,1)S(1)}, bf16[32,1280]{1,0:T(8,128)(2,1)S(1)}, u32[]{:S(2)}, u32[]{:S(2)}) collective-permute-start(bf16[32,1280]{1,0:T(8,128)(2,1)S(1)} %slice_bitcast_fusion.4), channel_id=1, source_target_pairs={{0,4},{4,0},{8,12},{12,8},{16,20},{20,16},{24,28},{28,24},{1,5},{5... | collective-permute-start | bytes 245768 | tf_op jit(solution)/shard_map/ppermute | solution.py:237
  23.2 1.5 %collective-permute-start.6 = (bf16[32,1280]{1,0:T(8,128)(2,1)S(1)}, bf16[32,1280]{1,0:T(8,128)(2,1)S(1)}, u32[]{:S(2)}, u32[]{:S(2)}) collective-permute-start(bf16[32,1280]{1,0:T(8,128)(2,1)S(1)} %slice_bitcast_fusion.3), channel_id=1, source_target_pairs={{0,4},{4,0},{8,12},{12,8},{16,20},{20,16},{24,28},{28,24},{1,5},{5... | collective-permute-start | bytes 245768 | tf_op jit(solution)/shard_map/ppermute | solution.py:237
  23.7 4.9 %collective-permute-start.11 = (bf16[32,1280]{1,0:T(8,128)(2,1)S(1)}, bf16[32,1280]{1,0:T(8,128)(2,1)S(1)}, u32[]{:S(2)}, u32[]{:S(2)}) collective-permute-start(bf16[32,1280]{1,0:T(8,128)(2,1)S(1)} %slice_bitcast_fusion.2), channel_id=1, source_target_pairs={{0,4},{4,0},{8,12},{12,8},{16,20},{20,16},{24,28},{28,24},{1,5},{5... | collective-permute-start | bytes 245768 | tf_op jit(solution)/shard_map/ppermute | solution.py:237
  23.8 4.8 %collective-permute-start.13 = (bf16[32,1280]{1,0:T(8,128)(2,1)S(1)}, bf16[32,1280]{1,0:T(8,128)(2,1)S(1)}, u32[]{:S(2)}, u32[]{:S(2)}) collective-permute-start(bf16[32,1280]{1,0:T(8,128)(2,1)S(1)} %slice_bitcast_fusion.1), channel_id=1, source_target_pairs={{0,4},{4,0},{8,12},{12,8},{16,20},{20,16},{24,28},{28,24},{1,5},{5... | collective-permute-start | bytes 245768 | tf_op jit(solution)/shard_map/ppermute | solution.py:237
  24.4 4.3 %collective-permute-start.15 = (bf16[32,1280]{1,0:T(8,128)(2,1)S(1)}, bf16[32,1280]{1,0:T(8,128)(2,1)S(1)}, u32[]{:S(2)}, u32[]{:S(2)}) collective-permute-start(bf16[32,1280]{1,0:T(8,128)(2,1)S(1)} %slice_bitcast_fusion), channel_id=1, source_target_pairs={{0,4},{4,0},{8,12},{12,8},{16,20},{20,16},{24,28},{28,24},{1,5},{5... | collective-permute-start | bytes 245768 | tf_op jit(solution)/shard_map/ppermute | solution.py:237
  38.9 3.9 %collective-permute-start.16 = (bf16[32,1280]{1,0:T(8,128)(2,1)S(1)}, bf16[32,1280]{1,0:T(8,128)(2,1)S(1)}, u32[]{:S(2)}, u32[]{:S(2)}) collective-permute-start(bf16[32,1280]{1,0:T(8,128)(2,1)S(1)} %get-tuple-element.42), channel_id=1, source_target_pairs={{0,4},{4,0},{8,12},{12,8},{16,20},{20,16},{24,28},{28,24},{1,5},{5... | collective-permute-start | bytes 245768 | tf_op jit(solution)/shard_map/ppermute | solution.py:237
  39.3 5.3 %collective-permute-start.17 = (bf16[32,1280]{1,0:T(8,128)(2,1)S(1)}, bf16[32,1280]{1,0:T(8,128)(2,1)S(1)}, u32[]{:S(2)}, u32[]{:S(2)}) collective-permute-start(bf16[32,1280]{1,0:T(8,128)(2,1)S(1)} %get-tuple-element.43), channel_id=1, source_target_pairs={{0,8},{4,12},{8,0},{12,4},{16,24},{20,28},{24,16},{28,20},{1,9},{5... | collective-permute-start | bytes 245768 | tf_op jit(solution)/shard_map/ppermute | solution.py:237
  39.4 5.9 %collective-permute-start.18 = (bf16[32,1280]{1,0:T(8,128)(2,1)S(1)}, bf16[32,1280]{1,0:T(8,128)(2,1)S(1)}, u32[]{:S(2)}, u32[]{:S(2)}) collective-permute-start(bf16[32,1280]{1,0:T(8,128)(2,1)S(1)} %get-tuple-element.44), channel_id=1, source_target_pairs={{0,12},{4,8},{8,4},{12,0},{16,28},{20,24},{24,20},{28,16},{1,13},{... | collective-permute-start | bytes 245768 | tf_op jit(solution)/shard_map/ppermute | solution.py:237
  40.8 5.3 %collective-permute-start.19 = (bf16[32,1280]{1,0:T(8,128)(2,1)S(1)}, bf16[32,1280]{1,0:T(8,128)(2,1)S(1)}, u32[]{:S(2)}, u32[]{:S(2)}) collective-permute-start(bf16[32,1280]{1,0:T(8,128)(2,1)S(1)} %get-tuple-element.45), channel_id=1, source_target_pairs={{0,16},{4,20},{8,24},{12,28},{16,0},{20,4},{24,8},{28,12},{1,17},{... | collective-permute-start | bytes 245768 | tf_op jit(solution)/shard_map/ppermute | solution.py:237
  41.9 8.9 %collective-permute-start.20 = (bf16[32,1280]{1,0:T(8,128)(2,1)S(1)}, bf16[32,1280]{1,0:T(8,128)(2,1)S(1)}, u32[]{:S(2)}, u32[]{:S(2)}) collective-permute-start(bf16[32,1280]{1,0:T(8,128)(2,1)S(1)} %get-tuple-element.46), channel_id=1, source_target_pairs={{0,20},{4,16},{8,28},{12,24},{16,4},{20,0},{24,12},{28,8},{1,21},{... | collective-permute-start | bytes 245768 | tf_op jit(solution)/shard_map/ppermute | solution.py:237
  42.8 7.9 %collective-permute-start.21 = (bf16[32,1280]{1,0:T(8,128)(2,1)S(1)}, bf16[32,1280]{1,0:T(8,128)(2,1)S(1)}, u32[]{:S(2)}, u32[]{:S(2)}) collective-permute-start(bf16[32,1280]{1,0:T(8,128)(2,1)S(1)} %get-tuple-element.47), channel_id=1, source_target_pairs={{0,24},{4,28},{8,16},{12,20},{16,8},{20,12},{24,0},{28,4},{1,25},{... | collective-permute-start | bytes 245768 | tf_op jit(solution)/shard_map/ppermute | solution.py:237
  44.7 6.1 %collective-permute-start.22 = (bf16[32,1280]{1,0:T(8,128)(2,1)S(1)}, bf16[32,1280]{1,0:T(8,128)(2,1)S(1)}, u32[]{:S(2)}, u32[]{:S(2)}) collective-permute-start(bf16[32,1280]{1,0:T(8,128)(2,1)S(1)} %get-tuple-element.48), channel_id=1, source_target_pairs={{0,28},{4,24},{8,20},{12,16},{16,12},{20,8},{24,4},{28,0},{1,29},{... | collective-permute-start | bytes 245768 | tf_op jit(solution)/shard_map/ppermute | solution.py:237

commit v3 on v2

--- a/solution.py
+++ b/solution.py
@@ -114,7 +114,13 @@
     return block[0] if mask % 2 == 0 else block
 
 
-def forward_kernel(me_ref, taps_ref, bias_ref, wq_ref, wk_ref, wv_ref, *refs, frames, toks, peers):
+def order_kernel(order_ref, *, frames, toks):
+    order_ref[0] = reorder_matrix(frames, toks, True)
+    order_ref[1] = reorder_matrix(frames, toks, False)
+
+
+def forward_kernel(me_ref, order_ref, taps_ref, bias_ref, wq_ref, wk_ref, wv_ref, *refs,
+                   frames, toks, peers):
     blocks = refs[:peers]
     q_ref, k_ref, v_ref, prob_ref, source_ref, hidden_ref = refs[peers:]
     rows, channels = hidden_ref.shape
@@ -123,7 +129,6 @@
     for mask in range(peers):
         start = pl.multiple_of((me ^ mask) * part, part)
         source_ref[pl.ds(start, part), :] = block_of(blocks, mask).astype(jnp.float32)
-    order = reorder_matrix(frames, toks, True)
     for col in range(0, channels, BLOCK):
         cols = slice(col, col + BLOCK)
         source = source_ref[:, cols]
@@ -134,7 +139,7 @@
         )
         hidden = (source + mixed + bias_ref[cols].reshape(1, BLOCK)).astype(jnp.bfloat16)
         hidden_ref[:, cols] = jnp.dot(
-            order, hidden, preferred_element_type=jnp.float32
+            order_ref[0], hidden, preferred_element_type=jnp.float32
         ).astype(jnp.bfloat16)
 
     masks = half_masks(LANES)
@@ -160,8 +165,8 @@
                     prob_ref[start // HEAD_DIM + head, :, here] = expo * inverse
 
 
-def backward_kernel(me_ref, taps_ref, wq_ref, wk_ref, wv_ref, q_ref, k_ref, v_ref, prob_ref,
-                    *refs, frames, toks, peers):
+def backward_kernel(me_ref, order_ref, taps_ref, wq_ref, wk_ref, wv_ref, q_ref, k_ref, v_ref,
+                    prob_ref, *refs, frames, toks, peers):
     blocks = refs[:peers]
     outs = refs[peers:2 * peers]
     grad_ref, left_ref, result_ref = refs[2 * peers:]
@@ -171,11 +176,10 @@
     for mask in range(peers):
         start = pl.multiple_of((me ^ mask) * part, part)
         result_ref[pl.ds(start, part), :] = block_of(blocks, mask)
-    order = reorder_matrix(frames, toks, True)
     for col in range(0, channels, BLOCK):
         cols = slice(col, col + BLOCK)
         grad_ref[:, cols] = jnp.dot(
-            order, result_ref[:, cols], preferred_element_type=jnp.float32
+            order_ref[0], result_ref[:, cols], preferred_element_type=jnp.float32
         ).astype(jnp.bfloat16)
 
     masks = half_masks(LANES)
@@ -184,44 +188,62 @@
         (token_of == tok).astype(jnp.float32).astype(jnp.bfloat16) for tok in range(LANES // frames)
     ]
     inv_root = 1.0 / math.sqrt(HEAD_DIM)
-    for start in range(0, channels, LANES):
-        cols = slice(start, start + LANES)
-        for row in range(0, rows, LANES):
-            here = slice(row, row + LANES)
-            g_pair = grad_ref[here, cols]
-            full = lax.dot_general(
-                split_pair(v_ref[here, cols], masks), g_pair, NT, preferred_element_type=jnp.float32
-            )
-            prob_wide, score_wide = [], []
-            for head in range(2):
-                prob = prob_ref[start // HEAD_DIM + head, :, here]
-                prob_low = prob.astype(jnp.bfloat16)
-                grad_prob = compact(full[head * LANES:(head + 1) * LANES], frames)
-                delta = jnp.sum(prob_low.astype(jnp.float32) * grad_prob, axis=0, keepdims=True)
-                d_scores = (prob * (grad_prob - delta)).astype(jnp.bfloat16)
-                prob_wide.append(expand(prob_low, token_masks))
-                score_wide.append(expand(d_scores, token_masks))
-            left_ref[0, here, cols] = (lax.dot_general(
-                jnp.concatenate(score_wide, axis=0), split_pair(k_ref[here, cols], masks),
-                TN, preferred_element_type=jnp.float32,
-            ) * inv_root).astype(jnp.bfloat16)
-            left_ref[1, here, cols] = (jnp.dot(
-                jnp.concatenate(score_wide, axis=1), split_pair(q_ref[here, cols], masks),
-                preferred_element_type=jnp.float32,
-            ) * inv_root).astype(jnp.bfloat16)
-            left_ref[2, here, cols] = jnp.dot(
-                jnp.concatenate(prob_wide, axis=1), split_pair(g_pair, masks),
-                preferred_element_type=jnp.float32,
-            ).astype(jnp.bfloat16)
-
-    order = reorder_matrix(frames, toks, False)
+    places = [
+        (slice(row, row + LANES), slice(col, col + LANES), col // HEAD_DIM)
+        for col in range(0, channels, LANES) for row in range(0, rows, LANES)
+    ]
+
+    def grad_probs(here, cols, head):
+        return lax.dot_general(
+            split_pair(v_ref[here, cols], masks), grad_ref[here, cols],
+            NT, preferred_element_type=jnp.float32,
+        )
+
+    def widen(full, here, cols, head):
+        prob_wide, score_wide = [], []
+        for half in range(2):
+            prob = prob_ref[head + half, :, here]
+            prob_low = prob.astype(jnp.bfloat16)
+            grad_prob = compact(full[half * LANES:(half + 1) * LANES], frames)
+            delta = jnp.sum(prob_low.astype(jnp.float32) * grad_prob, axis=0, keepdims=True)
+            d_scores = (prob * (grad_prob - delta)).astype(jnp.bfloat16)
+            prob_wide.append(expand(prob_low, token_masks))
+            score_wide.append(expand(d_scores, token_masks))
+        return prob_wide, score_wide
+
+    def contract(wide, here, cols, head):
+        prob_wide, score_wide = wide
+        left_ref[0, here, cols] = (lax.dot_general(
+            jnp.concatenate(score_wide, axis=0), split_pair(k_ref[here, cols], masks),
+            TN, preferred_element_type=jnp.float32,
+        ) * inv_root).astype(jnp.bfloat16)
+        left_ref[1, here, cols] = (jnp.dot(
+            jnp.concatenate(score_wide, axis=1), split_pair(q_ref[here, cols], masks),
+            preferred_element_type=jnp.float32,
+        ) * inv_root).astype(jnp.bfloat16)
+        left_ref[2, here, cols] = jnp.dot(
+            jnp.concatenate(prob_wide, axis=1), split_pair(grad_ref[here, cols], masks),
+            preferred_element_type=jnp.float32,
+        ).astype(jnp.bfloat16)
+
+    fulls, wides = {}, {}
+    for index in range(len(places) + 2):
+        if index < len(places):
+            fulls[index] = grad_probs(*places[index])
+        if 0 <= index - 1 < len(places):
+            wides[index - 1] = widen(fulls.pop(index - 1), *places[index - 1])
+        if 0 <= index - 2:
+            contract(wides.pop(index - 2), *places[index - 2])
+
+    total = sum(
+        lax.dot_general(weight_ref[...], left_ref[index], NT, preferred_element_type=jnp.float32)
+        for index, weight_ref in enumerate((wq_ref, wk_ref, wv_ref))
+    ).astype(jnp.bfloat16)
     for col in range(0, channels, BLOCK):
         cols = slice(col, col + BLOCK)
-        total = sum(
-            lax.dot_general(left_ref[index], weight_ref[cols, :], NT, preferred_element_type=jnp.float32)
-            for index, weight_ref in enumerate((wq_ref, wk_ref, wv_ref))
-        )
-        source = jnp.dot(order, total.astype(jnp.bfloat16), preferred_element_type=jnp.float32)
+        source = lax.dot_general(
+            order_ref[1], total[cols], NT, preferred_element_type=jnp.float32
+        )
         result_ref[:, cols] = (
             source
             + taps_ref[0:1, cols] * pltpu.roll(source, rows - toks, 0)
@@ -327,9 +349,16 @@
 
     weights = (w_query, w_key, w_value)
     sizes = dict(frames=frames, toks=toks, peers=peers)
+    order = on_chip(pl.pallas_call(
+        functools.partial(order_kernel, frames=frames, toks=toks),
+        out_specs=vmem,
+        out_shape=low((2, rows, rows)),
+        compiler_params=grant(4),
+        name="order",
+    )())
     query, key, value, prob = pl.pallas_call(
         functools.partial(forward_kernel, **sizes),
-        in_specs=[smem] + [vmem] * (5 + peers),
+        in_specs=[smem] + [vmem] * (6 + peers),
         out_specs=[vmem] * 4,
         out_shape=[low((rows, channels))] * 3 + [pltpu.VMEM((heads, frames, rows), jnp.float32)],
         scratch_shapes=[
@@ -337,10 +366,10 @@
         ],
         compiler_params=grant(20),
         name="forward",
-    )(me_arg, conv_taps, conv_bias, *weights, *map(on_chip, token_blocks))
+    )(me_arg, order, conv_taps, conv_bias, *weights, *map(on_chip, token_blocks))
     results = pl.pallas_call(
         functools.partial(backward_kernel, **sizes),
-        in_specs=[smem] + [vmem] * (8 + peers),
+        in_specs=[smem] + [vmem] * (9 + peers),
         out_specs=[vmem] * peers,
         out_shape=[low((part, channels))] * peers,
         scratch_shapes=[
@@ -350,7 +379,7 @@
         ],
         compiler_params=grant(20),
         name="backward",
-    )(me_arg, conv_taps, *weights, *map(on_chip, (query, key, value, prob)), *map(on_chip, grad_blocks))
+    )(me_arg, order, conv_taps, *weights, *map(on_chip, (query, key, value, prob)), *map(on_chip, grad_blocks))
     received = [block.reshape(frame_rows, toks, channels) for block in spread_frames(results)]
     output = pl.pallas_call(
         functools.partial(place_kernel, peers=peers),

time: 51.8 us -> 46.7 us (0.902)
  Pallas kernels: 16.8 us -> 11.8 us
    pallas_call x1, Pallas kernels: 10.2 us -> 5.1 us  [body(): pl.pallas_call(functools.partial(backward_kernel, **sizes), in_specs=[sme...]
  transfers between devices with their start and end apart: 23 -> 23, of which waited for: 8 -> 7; matrix products, arithmetic and copies ran while one was open for 0% -> 0% of each run, Pallas kernels for 8% -> 9%
where the time goes in v3:
time: 46.7 us; the launch traced here: 46.5 us
  starting transfers between devices  19.6 us (42%)
  waiting for transfers between devices  14.9 us (32%)
  Pallas kernels  11.8 us (25%)
    ppermute x23, starting transfers between devices, swap(): lax.ppermute(value, axis, [(i, i ^ mask) for i in range(lax.axis_size(axi...  19.6 us
    ppermute x23, waiting for transfers between devices, swap(): lax.ppermute(value, axis, [(i, i ^ mask) for i in range(lax.axis_size(axi...  14.9 us
    pallas_call x1, Pallas kernels, body(): pl.pallas_call(functools.partial(backward_kernel, **sizes), in_specs=[sme...  5.1 us
    pallas_call x1, Pallas kernels, body(): pl.pallas_call(functools.partial(forward_kernel, **sizes), in_specs=[smem...  3.93 us
    pallas_call x1, Pallas kernels, body(): pl.pallas_call(functools.partial(pack_kernel, peers=peers), in_specs=[sme...  1.58 us
  transfers between devices with their start and end apart: 23, of which 7 were waited for; matrix products, arithmetic and copies ran while one was open for 0% of the time, Pallas kernels for 9%

profile of v3, /device:TPU:0, one launch (start us, length us, event | category | flops | bytes accessed | tf_op | source)
XLA Modules:
  0.0 46.5 jit_solution(5788613560186015688)
XLA Ops:
  0.0 1.6 %pack.1 = (bf16[2,4,8,1280]{3,2,1,0:T(8,128)(2,1)S(1)}, bf16[2,4,8,1280]{3,2,1,0:T(8,128)(2,1)S(1)}, bf16[2,4,8,1280]{3,2,1,0:T(8,128)(2,1)S(1)}, bf16[2,4,8,128...) custom-call(s32[1]{0:T(128)} %bitcast.me_ref, bf16[4,8,8,1280]{3,2,1,0:T(8,128)(2,1)} %bitcast.52, ...), custom_call_target="tpu_custom_call" | custom-call | tf_op jit(solution)/shard_map/pack/pallas_call | solution.py:327
  1.6 3.1 %collective-permute-start.7 = (f32[4,128]{1,0:T(4,128)S(1)}, f32[4,128]{1,0:T(4,128)S(1)}, u32[]{:S(2)}, u32[]{:S(2)}) collective-permute-start(f32[4,128]{1,0:T(4,128)S(1)} %get-tuple-element.36), channel_id=1, source_target_pairs={{0,1},{1,0},{2,3},{3,2},{4,5},{5,4},{6,7},{7,6},{8,9},{9,8},{10,11... | collective-permute-start | bytes 6152 | tf_op jit(solution)/shard_map/ppermute | solution.py:259
  4.7 1.5 %collective-permute-start.1 = (bf16[2,4,8,1280]{3,2,1,0:T(8,128)(2,1)S(1)}, bf16[2,4,8,1280]{3,2,1,0:T(8,128)(2,1)S(1)}, u32[]{:S(2)}, u32[]{:S(2)}) collective-permute-start(bf16[2,4,8,1280]{3,2,1,0:T(8,128)(2,1)S(1)} %get-tuple-element.28), channel_id=1, source_target_pairs={{0,8},{4,12},{8,0},{12,4},{16,24},{20,28},{24,16},{28,20},{1,9},{5... | collective-permute-start | bytes 491528 | tf_op jit(solution)/shard_map/ppermute | solution.py:259
  6.2 1.5 %collective-permute-start.3 = (bf16[2,4,8,1280]{3,2,1,0:T(8,128)(2,1)S(1)}, bf16[2,4,8,1280]{3,2,1,0:T(8,128)(2,1)S(1)}, u32[]{:S(2)}, u32[]{:S(2)}) collective-permute-start(bf16[2,4,8,1280]{3,2,1,0:T(8,128)(2,1)S(1)} %get-tuple-element.29), channel_id=1, source_target_pairs={{0,16},{4,20},{8,24},{12,28},{16,0},{20,4},{24,8},{28,12},{1,17},{... | collective-permute-start | bytes 491528 | tf_op jit(solution)/shard_map/ppermute | solution.py:259
  7.7 0.5 %collective-permute-start.5 = (bf16[2,4,8,1280]{3,2,1,0:T(8,128)(2,1)S(1)}, bf16[2,4,8,1280]{3,2,1,0:T(8,128)(2,1)S(1)}, u32[]{:S(2)}, u32[]{:S(2)}) collective-permute-start(bf16[2,4,8,1280]{3,2,1,0:T(8,128)(2,1)S(1)} %get-tuple-element.30), channel_id=1, source_target_pairs={{0,24},{4,28},{8,16},{12,20},{16,8},{20,12},{24,0},{28,4},{1,25},{... | collective-permute-start | bytes 491528 | tf_op jit(solution)/shard_map/ppermute | solution.py:259
  8.2 2.6 %collective-permute-start.8 = (f32[4,128]{1,0:T(4,128)S(1)}, f32[4,128]{1,0:T(4,128)S(1)}, u32[]{:S(2)}, u32[]{:S(2)}) collective-permute-start(f32[4,128]{1,0:T(4,128)S(1)} %add.3.refs_0_), channel_id=1, source_target_pairs={{0,2},{1,3},{2,0},{3,1},{4,6},{5,7},{6,4},{7,5},{8,10},{9,11},{10,... | collective-permute-start | bytes 6152 | tf_op jit(solution)/shard_map/ppermute | solution.py:259
  10.8 1.9 %collective-permute-done.8.refs_1_ = f32[4,128]{1,0:T(4,128)S(1)} collective-permute-done((f32[4,128]{1,0:T(4,128)S(1)}, f32[4,128]{1,0:T(4,128)S(1)}, u32[]{:S(2)}, u32[]{:S(2)}) %collective-permute-start.8) | collective-permute-done | bytes 2080 | tf_op jit(solution)/shard_map/ppermute | solution.py:259
  12.7 0.2 scale.1
  12.9 1.6 %collective-permute-start.10 = (bf16[2,4,8,1280]{3,2,1,0:T(8,128)(2,1)S(1)}, bf16[2,4,8,1280]{3,2,1,0:T(8,128)(2,1)S(1)}, u32[]{:S(2)}, u32[]{:S(2)}) collective-permute-start(bf16[2,4,8,1280]{3,2,1,0:T(8,128)(2,1)S(1)} %get-tuple-element.38), channel_id=1, source_target_pairs={{0,8},{4,12},{8,0},{12,4},{16,24},{20,28},{24,16},{28,20},{1,9},{5... | collective-permute-start | bytes 491528 | tf_op jit(solution)/shard_map/ppermute | solution.py:259
  14.4 1.6 %collective-permute-start.12 = (bf16[2,4,8,1280]{3,2,1,0:T(8,128)(2,1)S(1)}, bf16[2,4,8,1280]{3,2,1,0:T(8,128)(2,1)S(1)}, u32[]{:S(2)}, u32[]{:S(2)}) collective-permute-start(bf16[2,4,8,1280]{3,2,1,0:T(8,128)(2,1)S(1)} %get-tuple-element.39), channel_id=1, source_target_pairs={{0,16},{4,20},{8,24},{12,28},{16,0},{20,4},{24,8},{28,12},{1,17},{... | collective-permute-start | bytes 491528 | tf_op jit(solution)/shard_map/ppermute | solution.py:259
  16.0 0.5 %collective-permute-start.14 = (bf16[2,4,8,1280]{3,2,1,0:T(8,128)(2,1)S(1)}, bf16[2,4,8,1280]{3,2,1,0:T(8,128)(2,1)S(1)}, u32[]{:S(2)}, u32[]{:S(2)}) collective-permute-start(bf16[2,4,8,1280]{3,2,1,0:T(8,128)(2,1)S(1)} %get-tuple-element.40), channel_id=1, source_target_pairs={{0,24},{4,28},{8,16},{12,20},{16,8},{20,12},{24,0},{28,4},{1,25},{... | collective-permute-start | bytes 491528 | tf_op jit(solution)/shard_map/ppermute | solution.py:259
  16.6 0.1 collective-permute-start.9
  16.7 3.1 %collective-permute-done.10 = bf16[2,4,8,1280]{3,2,1,0:T(8,128)(2,1)S(1)} collective-permute-done((bf16[2,4,8,1280]{3,2,1,0:T(8,128)(2,1)S(1)}, bf16[2,4,8,1280]{3,2,1,0:T(8,128)(2,1)S(1)}, u32[]{:S(2)}, u32[]{:S(2)}) %collective-permute-start.10) | collective-permute-done | bytes 163872 | tf_op jit(solution)/shard_map/ppermute | solution.py:259
  19.8 3.3 %collective-permute-done.12 = bf16[2,4,8,1280]{3,2,1,0:T(8,128)(2,1)S(1)} collective-permute-done((bf16[2,4,8,1280]{3,2,1,0:T(8,128)(2,1)S(1)}, bf16[2,4,8,1280]{3,2,1,0:T(8,128)(2,1)S(1)}, u32[]{:S(2)}, u32[]{:S(2)}) %collective-permute-start.12) | collective-permute-done | bytes 163872 | tf_op jit(solution)/shard_map/ppermute | solution.py:259
  23.2 0.6 %collective-permute-start.6 = (bf16[32,1280]{1,0:T(8,128)(2,1)S(1)}, bf16[32,1280]{1,0:T(8,128)(2,1)S(1)}, u32[]{:S(2)}, u32[]{:S(2)}) collective-permute-start(bf16[32,1280]{1,0:T(8,128)(2,1)S(1)} %slice_bitcast_fusion.3), channel_id=1, source_target_pairs={{0,4},{4,0},{8,12},{12,8},{16,20},{20,16},{24,28},{28,24},{1,5},{5... | collective-permute-start | bytes 245768 | tf_op jit(solution)/shard_map/ppermute | solution.py:259
  23.7 0.1 collective-permute-start.11
  23.8 0.5 %collective-permute-start.13 = (bf16[32,1280]{1,0:T(8,128)(2,1)S(1)}, bf16[32,1280]{1,0:T(8,128)(2,1)S(1)}, u32[]{:S(2)}, u32[]{:S(2)}) collective-permute-start(bf16[32,1280]{1,0:T(8,128)(2,1)S(1)} %slice_bitcast_fusion.1), channel_id=1, source_target_pairs={{0,4},{4,0},{8,12},{12,8},{16,20},{20,16},{24,28},{28,24},{1,5},{5... | collective-permute-start | bytes 245768 | tf_op jit(solution)/shard_map/ppermute | solution.py:259
  24.3 0.1 collective-permute-done.4.refs_5_
  24.4 0.2 collective-permute-start.15
  24.6 0.1 order.1.order_ref
  24.7 3.9 %forward.1 = (bf16[256,1280]{1,0:T(8,128)(2,1)S(1)}, bf16[256,1280]{1,0:T(8,128)(2,1)S(1)}, bf16[256,1280]{1,0:T(8,128)(2,1)S(1)}, f32[20,32,256]{2,1,0:T(8,128)S(1)}) custom-call(s32[1]{0:T(128)} %bitcast.me_ref, bf16[2,256,256]{2,1,0:T(8,128)(2,1)S(1)} %order.1.order_ref, f32[3,1280]{1,0:T(4,128)S(1)} %copy-done.3, f32[1280]{0:T(1024)S(1)} %copy-done.4, ...), custom_call_target="tpu_custom_call" | custom-call | tf_op jit(solution)/shard_map/forward/pallas_call | solution.py:359
  28.7 5.1 %backward.1 = (bf16[32,1280]{1,0:T(8,128)(2,1)S(1)}, bf16[32,1280]{1,0:T(8,128)(2,1)S(1)}, bf16[32,1280]{1,0:T(8,128)(2,1)S(1)}, bf16[32,1280]{1,0:T(8,128)(2,1)...) custom-call(s32[1]{0:T(128)} %bitcast.me_ref, ...), custom_call_target="tpu_custom_call" | custom-call | tf_op jit(solution)/shard_map/backward/pallas_call | solution.py:370
  33.8 0.4 collective-permute-start.16
  34.3 1.5 %collective-permute-start.18 = (bf16[32,1280]{1,0:T(8,128)(2,1)S(1)}, bf16[32,1280]{1,0:T(8,128)(2,1)S(1)}, u32[]{:S(2)}, u32[]{:S(2)}) collective-permute-start(bf16[32,1280]{1,0:T(8,128)(2,1)S(1)} %get-tuple-element.44), channel_id=1, source_target_pairs={{0,12},{4,8},{8,4},{12,0},{16,28},{20,24},{24,20},{28,16},{1,13},{... | collective-permute-start | bytes 245768 | tf_op jit(solution)/shard_map/ppermute | solution.py:259
  35.7 1.0 %collective-permute-start.19 = (bf16[32,1280]{1,0:T(8,128)(2,1)S(1)}, bf16[32,1280]{1,0:T(8,128)(2,1)S(1)}, u32[]{:S(2)}, u32[]{:S(2)}) collective-permute-start(bf16[32,1280]{1,0:T(8,128)(2,1)S(1)} %get-tuple-element.45), channel_id=1, source_target_pairs={{0,16},{4,20},{8,24},{12,28},{16,0},{20,4},{24,8},{28,12},{1,17},{... | collective-permute-start | bytes 245768 | tf_op jit(solution)/shard_map/ppermute | solution.py:259
  36.8 1.0 %collective-permute-start.20 = (bf16[32,1280]{1,0:T(8,128)(2,1)S(1)}, bf16[32,1280]{1,0:T(8,128)(2,1)S(1)}, u32[]{:S(2)}, u32[]{:S(2)}) collective-permute-start(bf16[32,1280]{1,0:T(8,128)(2,1)S(1)} %get-tuple-element.46), channel_id=1, source_target_pairs={{0,20},{4,16},{8,28},{12,24},{16,4},{20,0},{24,12},{28,8},{1,21},{... | collective-permute-start | bytes 245768 | tf_op jit(solution)/shard_map/ppermute | solution.py:259
  37.7 0.8 %collective-permute-start.21 = (bf16[32,1280]{1,0:T(8,128)(2,1)S(1)}, bf16[32,1280]{1,0:T(8,128)(2,1)S(1)}, u32[]{:S(2)}, u32[]{:S(2)}) collective-permute-start(bf16[32,1280]{1,0:T(8,128)(2,1)S(1)} %get-tuple-element.47), channel_id=1, source_target_pairs={{0,24},{4,28},{8,16},{12,20},{16,8},{20,12},{24,0},{28,4},{1,25},{... | collective-permute-start | bytes 245768 | tf_op jit(solution)/shard_map/ppermute | solution.py:259
  38.6 1.0 %collective-permute-done.17 = bf16[32,1280]{1,0:T(8,128)(2,1)S(1)} collective-permute-done((bf16[32,1280]{1,0:T(8,128)(2,1)S(1)}, bf16[32,1280]{1,0:T(8,128)(2,1)S(1)}, u32[]{:S(2)}, u32[]{:S(2)}) %collective-permute-start.17) | collective-permute-done | bytes 81952 | tf_op jit(solution)/shard_map/ppermute | solution.py:259
  39.5 0.6 %collective-permute-start.22 = (bf16[32,1280]{1,0:T(8,128)(2,1)S(1)}, bf16[32,1280]{1,0:T(8,128)(2,1)S(1)}, u32[]{:S(2)}, u32[]{:S(2)}) collective-permute-start(bf16[32,1280]{1,0:T(8,128)(2,1)S(1)} %get-tuple-element.48), channel_id=1, source_target_pairs={{0,28},{4,24},{8,20},{12,16},{16,12},{20,8},{24,4},{28,0},{1,29},{... | collective-permute-start | bytes 245768 | tf_op jit(solution)/shard_map/ppermute | solution.py:259
  40.2 0.9 %collective-permute-done.19 = bf16[32,1280]{1,0:T(8,128)(2,1)S(1)} collective-permute-done((bf16[32,1280]{1,0:T(8,128)(2,1)S(1)}, bf16[32,1280]{1,0:T(8,128)(2,1)S(1)}, u32[]{:S(2)}, u32[]{:S(2)}) %collective-permute-start.19) | collective-permute-done | bytes 81952 | tf_op jit(solution)/shard_map/ppermute | solution.py:259
  41.1 4.6 %collective-permute-done.20 = bf16[32,1280]{1,0:T(8,128)(2,1)S(1)} collective-permute-done((bf16[32,1280]{1,0:T(8,128)(2,1)S(1)}, bf16[32,1280]{1,0:T(8,128)(2,1)S(1)}, u32[]{:S(2)}, u32[]{:S(2)}) %collective-permute-start.20) | collective-permute-done | bytes 81952 | tf_op jit(solution)/shard_map/ppermute | solution.py:259
  45.6 0.9 %place.1 = bf16[4,8,8,1280]{3,2,1,0:T(8,128)(2,1)} custom-call(s32[1]{0:T(128)} %bitcast.me_ref, bf16[4,8,1280]{2,1,0:T(8,128)(2,1)S(1)} %bitcast.44, bf16[4,8,1280]{2,1,0:T(8,128)(2,1)S(1)} %bitcast.45, bf16[4,8,1280]{2,1,0:T(8,128)(2,1)S(1)} %bitcast.46, bf16[4,8,1280]{2,1,0:T(8,128)(2,1)S(1)} %bitcast.47, bf16[4,8,1280]{2,1,0:T(8,128)(2,1)S(1)} %bitcast.48, ...), custom_call_target="tpu_custom_call" | custom-call | tf_op jit(solution)/shard_map/place/pallas_call | solution.py:384
  (39 shorter events, 0.1 us)
Async XLA Ops:
  1.6 6.6 %collective-permute-start.7 = (f32[4,128]{1,0:T(4,128)S(1)}, f32[4,128]{1,0:T(4,128)S(1)}, u32[]{:S(2)}, u32[]{:S(2)}) collective-permute-start(f32[4,128]{1,0:T(4,128)S(1)} %get-tuple-element.36), channel_id=1, source_target_pairs={{0,1},{1,0},{2,3},{3,2},{4,5},{5,4},{6,7},{7,6},{8,9},{9,8},{10,11... | collective-permute-start | bytes 6152 | tf_op jit(solution)/shard_map/ppermute | solution.py:259
  4.7 9.7 %collective-permute-start.1 = (bf16[2,4,8,1280]{3,2,1,0:T(8,128)(2,1)S(1)}, bf16[2,4,8,1280]{3,2,1,0:T(8,128)(2,1)S(1)}, u32[]{:S(2)}, u32[]{:S(2)}) collective-permute-start(bf16[2,4,8,1280]{3,2,1,0:T(8,128)(2,1)S(1)} %get-tuple-element.28), channel_id=1, source_target_pairs={{0,8},{4,12},{8,0},{12,4},{16,24},{20,28},{24,16},{28,20},{1,9},{5... | collective-permute-start | bytes 491528 | tf_op jit(solution)/shard_map/ppermute | solution.py:259
  6.2 9.8 %collective-permute-start.3 = (bf16[2,4,8,1280]{3,2,1,0:T(8,128)(2,1)S(1)}, bf16[2,4,8,1280]{3,2,1,0:T(8,128)(2,1)S(1)}, u32[]{:S(2)}, u32[]{:S(2)}) collective-permute-start(bf16[2,4,8,1280]{3,2,1,0:T(8,128)(2,1)S(1)} %get-tuple-element.29), channel_id=1, source_target_pairs={{0,16},{4,20},{8,24},{12,28},{16,0},{20,4},{24,8},{28,12},{1,17},{... | collective-permute-start | bytes 491528 | tf_op jit(solution)/shard_map/ppermute | solution.py:259
  7.7 8.9 %collective-permute-start.5 = (bf16[2,4,8,1280]{3,2,1,0:T(8,128)(2,1)S(1)}, bf16[2,4,8,1280]{3,2,1,0:T(8,128)(2,1)S(1)}, u32[]{:S(2)}, u32[]{:S(2)}) collective-permute-start(bf16[2,4,8,1280]{3,2,1,0:T(8,128)(2,1)S(1)} %get-tuple-element.30), channel_id=1, source_target_pairs={{0,24},{4,28},{8,16},{12,20},{16,8},{20,12},{24,0},{28,4},{1,25},{... | collective-permute-start | bytes 491528 | tf_op jit(solution)/shard_map/ppermute | solution.py:259
  8.2 4.5 %collective-permute-start.8 = (f32[4,128]{1,0:T(4,128)S(1)}, f32[4,128]{1,0:T(4,128)S(1)}, u32[]{:S(2)}, u32[]{:S(2)}) collective-permute-start(f32[4,128]{1,0:T(4,128)S(1)} %add.3.refs_0_), channel_id=1, source_target_pairs={{0,2},{1,3},{2,0},{3,1},{4,6},{5,7},{6,4},{7,5},{8,10},{9,11},{10,... | collective-permute-start | bytes 6152 | tf_op jit(solution)/shard_map/ppermute | solution.py:259
  10.8 12.9 %collective-permute-start = (bf16[32,1280]{1,0:T(8,128)(2,1)S(1)}, bf16[32,1280]{1,0:T(8,128)(2,1)S(1)}, u32[]{:S(2)}, u32[]{:S(2)}) collective-permute-start(bf16[32,1280]{1,0:T(8,128)(2,1)S(1)} %slice_bitcast_fusion.7), channel_id=1, source_target_pairs={{0,4},{4,0},{8,12},{12,8},{16,20},{20,16},{24,28},{28,24},{1,5},{5... | collective-permute-start | bytes 245768 | tf_op jit(solution)/shard_map/ppermute | solution.py:259
  12.7 12.0 %copy-start = (bf16[1280,1280]{1,0:T(8,128)(2,1)S(1)}, bf16[1280,1280]{1,0:T(8,128)(2,1)}, u32[]{:S(2)}) copy-start(bf16[1280,1280]{1,0:T(8,128)(2,1)} %wq_ref.3) | copy-start | bytes 9830404
  12.7 12.0 %copy-start.1 = (bf16[1280,1280]{1,0:T(8,128)(2,1)S(1)}, bf16[1280,1280]{1,0:T(8,128)(2,1)}, u32[]{:S(2)}) copy-start(bf16[1280,1280]{1,0:T(8,128)(2,1)} %wk_ref.3) | copy-start | bytes 9830404
  12.7 12.0 %copy-start.2 = (bf16[1280,1280]{1,0:T(8,128)(2,1)S(1)}, bf16[1280,1280]{1,0:T(8,128)(2,1)}, u32[]{:S(2)}) copy-start(bf16[1280,1280]{1,0:T(8,128)(2,1)} %wv_ref.3) | copy-start | bytes 9830404
  12.7 12.0 %copy-start.3 = (f32[3,1280]{1,0:T(4,128)S(1)}, f32[3,1280]{1,0:T(4,128)}, u32[]{:S(2)}) copy-start(f32[3,1280]{1,0:T(4,128)} %taps_ref.3) | copy-start | bytes 46084
  12.7 12.0 %copy-start.4 = (f32[1280]{0:T(1024)S(1)}, f32[1280]{0:T(1024)}, u32[]{:S(2)}) copy-start(f32[1280]{0:T(1024)} %bias_ref.1) | copy-start | bytes 15364
  12.9 6.9 %collective-permute-start.10 = (bf16[2,4,8,1280]{3,2,1,0:T(8,128)(2,1)S(1)}, bf16[2,4,8,1280]{3,2,1,0:T(8,128)(2,1)S(1)}, u32[]{:S(2)}, u32[]{:S(2)}) collective-permute-start(bf16[2,4,8,1280]{3,2,1,0:T(8,128)(2,1)S(1)} %get-tuple-element.38), channel_id=1, source_target_pairs={{0,8},{4,12},{8,0},{12,4},{16,24},{20,28},{24,16},{28,20},{1,9},{5... | collective-permute-start | bytes 491528 | tf_op jit(solution)/shard_map/ppermute | solution.py:259
  14.4 8.7 %collective-permute-start.12 = (bf16[2,4,8,1280]{3,2,1,0:T(8,128)(2,1)S(1)}, bf16[2,4,8,1280]{3,2,1,0:T(8,128)(2,1)S(1)}, u32[]{:S(2)}, u32[]{:S(2)}) collective-permute-start(bf16[2,4,8,1280]{3,2,1,0:T(8,128)(2,1)S(1)} %get-tuple-element.39), channel_id=1, source_target_pairs={{0,16},{4,20},{8,24},{12,28},{16,0},{20,4},{24,8},{28,12},{1,17},{... | collective-permute-start | bytes 491528 | tf_op jit(solution)/shard_map/ppermute | solution.py:259
  16.0 7.1 %collective-permute-start.14 = (bf16[2,4,8,1280]{3,2,1,0:T(8,128)(2,1)S(1)}, bf16[2,4,8,1280]{3,2,1,0:T(8,128)(2,1)S(1)}, u32[]{:S(2)}, u32[]{:S(2)}) collective-permute-start(bf16[2,4,8,1280]{3,2,1,0:T(8,128)(2,1)S(1)} %get-tuple-element.40), channel_id=1, source_target_pairs={{0,24},{4,28},{8,16},{12,20},{16,8},{20,12},{24,0},{28,4},{1,25},{... | collective-permute-start | bytes 491528 | tf_op jit(solution)/shard_map/ppermute | solution.py:259
  16.6 12.1 %collective-permute-start.9 = (bf16[32,1280]{1,0:T(8,128)(2,1)S(1)}, bf16[32,1280]{1,0:T(8,128)(2,1)S(1)}, u32[]{:S(2)}, u32[]{:S(2)}) collective-permute-start(bf16[32,1280]{1,0:T(8,128)(2,1)S(1)} %slice_bitcast_fusion.6), channel_id=1, source_target_pairs={{0,4},{4,0},{8,12},{12,8},{16,20},{20,16},{24,28},{28,24},{1,5},{5... | collective-permute-start | bytes 245768 | tf_op jit(solution)/shard_map/ppermute | solution.py:259
  19.8 4.0 %collective-permute-start.2 = (bf16[32,1280]{1,0:T(8,128)(2,1)S(1)}, bf16[32,1280]{1,0:T(8,128)(2,1)S(1)}, u32[]{:S(2)}, u32[]{:S(2)}) collective-permute-start(bf16[32,1280]{1,0:T(8,128)(2,1)S(1)} %slice_bitcast_fusion.5), channel_id=1, source_target_pairs={{0,4},{4,0},{8,12},{12,8},{16,20},{20,16},{24,28},{28,24},{1,5},{5... | collective-permute-start | bytes 245768 | tf_op jit(solution)/shard_map/ppermute | solution.py:259
  23.1 1.3 %collective-permute-start.4 = (bf16[32,1280]{1,0:T(8,128)(2,1)S(1)}, bf16[32,1280]{1,0:T(8,128)(2,1)S(1)}, u32[]{:S(2)}, u32[]{:S(2)}) collective-permute-start(bf16[32,1280]{1,0:T(8,128)(2,1)S(1)} %slice_bitcast_fusion.4), channel_id=1, source_target_pairs={{0,4},{4,0},{8,12},{12,8},{16,20},{20,16},{24,28},{28,24},{1,5},{5... | collective-permute-start | bytes 245768 | tf_op jit(solution)/shard_map/ppermute | solution.py:259
  23.2 1.5 %collective-permute-start.6 = (bf16[32,1280]{1,0:T(8,128)(2,1)S(1)}, bf16[32,1280]{1,0:T(8,128)(2,1)S(1)}, u32[]{:S(2)}, u32[]{:S(2)}) collective-permute-start(bf16[32,1280]{1,0:T(8,128)(2,1)S(1)} %slice_bitcast_fusion.3), channel_id=1, source_target_pairs={{0,4},{4,0},{8,12},{12,8},{16,20},{20,16},{24,28},{28,24},{1,5},{5... | collective-permute-start | bytes 245768 | tf_op jit(solution)/shard_map/ppermute | solution.py:259
  23.7 4.9 %collective-permute-start.11 = (bf16[32,1280]{1,0:T(8,128)(2,1)S(1)}, bf16[32,1280]{1,0:T(8,128)(2,1)S(1)}, u32[]{:S(2)}, u32[]{:S(2)}) collective-permute-start(bf16[32,1280]{1,0:T(8,128)(2,1)S(1)} %slice_bitcast_fusion.2), channel_id=1, source_target_pairs={{0,4},{4,0},{8,12},{12,8},{16,20},{20,16},{24,28},{28,24},{1,5},{5... | collective-permute-start | bytes 245768 | tf_op jit(solution)/shard_map/ppermute | solution.py:259
  23.8 4.8 %collective-permute-start.13 = (bf16[32,1280]{1,0:T(8,128)(2,1)S(1)}, bf16[32,1280]{1,0:T(8,128)(2,1)S(1)}, u32[]{:S(2)}, u32[]{:S(2)}) collective-permute-start(bf16[32,1280]{1,0:T(8,128)(2,1)S(1)} %slice_bitcast_fusion.1), channel_id=1, source_target_pairs={{0,4},{4,0},{8,12},{12,8},{16,20},{20,16},{24,28},{28,24},{1,5},{5... | collective-permute-start | bytes 245768 | tf_op jit(solution)/shard_map/ppermute | solution.py:259
  24.4 4.3 %collective-permute-start.15 = (bf16[32,1280]{1,0:T(8,128)(2,1)S(1)}, bf16[32,1280]{1,0:T(8,128)(2,1)S(1)}, u32[]{:S(2)}, u32[]{:S(2)}) collective-permute-start(bf16[32,1280]{1,0:T(8,128)(2,1)S(1)} %slice_bitcast_fusion), channel_id=1, source_target_pairs={{0,4},{4,0},{8,12},{12,8},{16,20},{20,16},{24,28},{28,24},{1,5},{5... | collective-permute-start | bytes 245768 | tf_op jit(solution)/shard_map/ppermute | solution.py:259
  33.8 3.9 %collective-permute-start.16 = (bf16[32,1280]{1,0:T(8,128)(2,1)S(1)}, bf16[32,1280]{1,0:T(8,128)(2,1)S(1)}, u32[]{:S(2)}, u32[]{:S(2)}) collective-permute-start(bf16[32,1280]{1,0:T(8,128)(2,1)S(1)} %get-tuple-element.42), channel_id=1, source_target_pairs={{0,4},{4,0},{8,12},{12,8},{16,20},{20,16},{24,28},{28,24},{1,5},{5... | collective-permute-start | bytes 245768 | tf_op jit(solution)/shard_map/ppermute | solution.py:259
  34.2 5.3 %collective-permute-start.17 = (bf16[32,1280]{1,0:T(8,128)(2,1)S(1)}, bf16[32,1280]{1,0:T(8,128)(2,1)S(1)}, u32[]{:S(2)}, u32[]{:S(2)}) collective-permute-start(bf16[32,1280]{1,0:T(8,128)(2,1)S(1)} %get-tuple-element.43), channel_id=1, source_target_pairs={{0,8},{4,12},{8,0},{12,4},{16,24},{20,28},{24,16},{28,20},{1,9},{5... | collective-permute-start | bytes 245768 | tf_op jit(solution)/shard_map/ppermute | solution.py:259
  34.3 5.9 %collective-permute-start.18 = (bf16[32,1280]{1,0:T(8,128)(2,1)S(1)}, bf16[32,1280]{1,0:T(8,128)(2,1)S(1)}, u32[]{:S(2)}, u32[]{:S(2)}) collective-permute-start(bf16[32,1280]{1,0:T(8,128)(2,1)S(1)} %get-tuple-element.44), channel_id=1, source_target_pairs={{0,12},{4,8},{8,4},{12,0},{16,28},{20,24},{24,20},{28,16},{1,13},{... | collective-permute-start | bytes 245768 | tf_op jit(solution)/shard_map/ppermute | solution.py:259
  35.7 5.3 %collective-permute-start.19 = (bf16[32,1280]{1,0:T(8,128)(2,1)S(1)}, bf16[32,1280]{1,0:T(8,128)(2,1)S(1)}, u32[]{:S(2)}, u32[]{:S(2)}) collective-permute-start(bf16[32,1280]{1,0:T(8,128)(2,1)S(1)} %get-tuple-element.45), channel_id=1, source_target_pairs={{0,16},{4,20},{8,24},{12,28},{16,0},{20,4},{24,8},{28,12},{1,17},{... | collective-permute-start | bytes 245768 | tf_op jit(solution)/shard_map/ppermute | solution.py:259
  36.8 8.9 %collective-permute-start.20 = (bf16[32,1280]{1,0:T(8,128)(2,1)S(1)}, bf16[32,1280]{1,0:T(8,128)(2,1)S(1)}, u32[]{:S(2)}, u32[]{:S(2)}) collective-permute-start(bf16[32,1280]{1,0:T(8,128)(2,1)S(1)} %get-tuple-element.46), channel_id=1, source_target_pairs={{0,20},{4,16},{8,28},{12,24},{16,4},{20,0},{24,12},{28,8},{1,21},{... | collective-permute-start | bytes 245768 | tf_op jit(solution)/shard_map/ppermute | solution.py:259
  37.7 7.9 %collective-permute-start.21 = (bf16[32,1280]{1,0:T(8,128)(2,1)S(1)}, bf16[32,1280]{1,0:T(8,128)(2,1)S(1)}, u32[]{:S(2)}, u32[]{:S(2)}) collective-permute-start(bf16[32,1280]{1,0:T(8,128)(2,1)S(1)} %get-tuple-element.47), channel_id=1, source_target_pairs={{0,24},{4,28},{8,16},{12,20},{16,8},{20,12},{24,0},{28,4},{1,25},{... | collective-permute-start | bytes 245768 | tf_op jit(solution)/shard_map/ppermute | solution.py:259
  39.5 6.1 %collective-permute-start.22 = (bf16[32,1280]{1,0:T(8,128)(2,1)S(1)}, bf16[32,1280]{1,0:T(8,128)(2,1)S(1)}, u32[]{:S(2)}, u32[]{:S(2)}) collective-permute-start(bf16[32,1280]{1,0:T(8,128)(2,1)S(1)} %get-tuple-element.48), channel_id=1, source_target_pairs={{0,28},{4,24},{8,20},{12,16},{16,12},{20,8},{24,4},{28,0},{1,29},{... | collective-permute-start | bytes 245768 | tf_op jit(solution)/shard_map/ppermute | solution.py:259

commit v4 on v3

--- a/solution.py
+++ b/solution.py
@@ -95,13 +95,12 @@
             ).astype(jnp.bfloat16)
 
 
-def place_kernel(me_ref, *refs, peers):
-    blocks = refs[:peers]
-    out_ref, sems = refs[peers:]
+def place_kernel(me_ref, *refs, masks):
+    out_ref, sems = refs[-2:]
     me = me_ref[0]
     copies = [
-        pltpu.make_async_copy(blocks[mask], out_ref.at[:, me ^ mask], sems.at[mask])
-        for mask in range(peers)
+        pltpu.make_async_copy(refs[index], out_ref.at[:, me ^ mask], sems.at[index])
+        for index, mask in enumerate(masks)
     ]
     for copy in copies:
         copy.start()
@@ -109,9 +108,16 @@
         copy.wait()
 
 
+def join_kernel(*refs):
+    for index, pair_ref in enumerate(refs[:-1]):
+        refs[-1][index] = pair_ref[1]
+
+
 def block_of(blocks, mask):
-    block = blocks[mask][...]
-    return block[0] if mask % 2 == 0 else block
+    chip = mask // 2
+    if mask % 2 == 0:
+        return blocks[chip][0]
+    return blocks[-1][chip - 1] if chip else blocks[-2][...]
 
 
 def order_kernel(order_ref, *, frames, toks):
@@ -121,8 +127,8 @@
 
 def forward_kernel(me_ref, order_ref, taps_ref, bias_ref, wq_ref, wk_ref, wv_ref, *refs,
                    frames, toks, peers):
-    blocks = refs[:peers]
-    q_ref, k_ref, v_ref, prob_ref, source_ref, hidden_ref = refs[peers:]
+    blocks = refs[:peers // 2 + 2]
+    q_ref, k_ref, v_ref, prob_ref, source_ref, hidden_ref = refs[peers // 2 + 2:]
     rows, channels = hidden_ref.shape
     part = rows // peers
     me = me_ref[0]
@@ -167,9 +173,9 @@
 
 def backward_kernel(me_ref, order_ref, taps_ref, wq_ref, wk_ref, wv_ref, q_ref, k_ref, v_ref,
                     prob_ref, *refs, frames, toks, peers):
-    blocks = refs[:peers]
-    outs = refs[peers:2 * peers]
-    grad_ref, left_ref, result_ref = refs[2 * peers:]
+    blocks = refs[:peers // 2 + 2]
+    outs = refs[peers // 2 + 2:-3]
+    grad_ref, left_ref, result_ref = refs[-3:]
     rows, channels = grad_ref.shape
     part = rows // peers
     me = me_ref[0]
@@ -272,7 +278,8 @@
 
 
 def far_first(peers):
-    return sorted(range(1, peers), key=lambda mask: (-bin(mask >> 1).count("1"), -mask))
+    masks = sorted(range(2, peers), key=lambda mask: (-bin(mask >> 1).count("1"), mask & 1, -mask))
+    return masks + [1]
 
 
 def gather_tokens(sent):
@@ -282,12 +289,17 @@
     for mask in far_first(peers):
         if mask % 2 == 0:
             parts[mask // 2] = swap(sent[mask // 2], "orbit", mask)
-    blocks = []
-    for chip in range(peers // 2):
-        pair = parts[chip].reshape(2, frame_rows * toks, channels)
-        mine = pair[1]
-        blocks += [pair, swap(mine, "orbit", 1)]
-    return blocks
+    parts = [part.reshape(2, frame_rows * toks, channels) for part in parts]
+    own = swap(parts[0][1], "orbit", 1)
+    others = pl.pallas_call(
+        join_kernel,
+        in_specs=[pl.BlockSpec(memory_space=pltpu.VMEM)] * (peers // 2 - 1),
+        out_specs=pl.BlockSpec(memory_space=pltpu.VMEM),
+        out_shape=pltpu.VMEM((peers // 2 - 1, frame_rows * toks, channels), jnp.bfloat16),
+        compiler_params=grant(4),
+        name="join",
+    )(*map(on_chip, parts[1:]))
+    return parts + [own, swap(others, "orbit", 1)]
 
 
 def spread_frames(blocks):
@@ -358,7 +370,7 @@
     )())
     query, key, value, prob = pl.pallas_call(
         functools.partial(forward_kernel, **sizes),
-        in_specs=[smem] + [vmem] * (6 + peers),
+        in_specs=[smem] + [vmem] * (8 + peers // 2),
         out_specs=[vmem] * 4,
         out_shape=[low((rows, channels))] * 3 + [pltpu.VMEM((heads, frames, rows), jnp.float32)],
         scratch_shapes=[
@@ -369,7 +381,7 @@
     )(me_arg, order, conv_taps, conv_bias, *weights, *map(on_chip, token_blocks))
     results = pl.pallas_call(
         functools.partial(backward_kernel, **sizes),
-        in_specs=[smem] + [vmem] * (9 + peers),
+        in_specs=[smem] + [vmem] * (11 + peers // 2),
         out_specs=[vmem] * peers,
         out_shape=[low((part, channels))] * peers,
         scratch_shapes=[
@@ -381,15 +393,21 @@
         name="backward",
     )(me_arg, order, conv_taps, *weights, *map(on_chip, (query, key, value, prob)), *map(on_chip, grad_blocks))
     received = [block.reshape(frame_rows, toks, channels) for block in spread_frames(results)]
-    output = pl.pallas_call(
-        functools.partial(place_kernel, peers=peers),
-        in_specs=[smem] + [vmem] * peers,
-        out_specs=hbm,
-        out_shape=jax.ShapeDtypeStruct(split, jnp.bfloat16),
-        scratch_shapes=[pltpu.SemaphoreType.DMA((peers,))],
-        compiler_params=grant(4),
-        name="place",
-    )(me_arg, *map(on_chip, received))
+    early = [mask for mask in range(peers) if bin(mask >> 1).count("1") != 1]
+    late = [mask for mask in range(peers) if mask not in early]
+    output = None
+    for masks in (early, late):
+        blocks = [on_chip(received[mask]) for mask in masks]
+        output = pl.pallas_call(
+            functools.partial(place_kernel, masks=masks),
+            in_specs=[smem] + [vmem] * len(masks) + [hbm] * (output is not None),
+            out_specs=hbm,
+            out_shape=jax.ShapeDtypeStruct(split, jnp.bfloat16),
+            scratch_shapes=[pltpu.SemaphoreType.DMA((len(masks),))],
+            input_output_aliases={} if output is None else {len(masks) + 1: 0},
+            compiler_params=grant(4),
+            name="place",
+        )(me_arg, *blocks, *([] if output is None else [output]))
     return output.reshape(frame_rows, tile_rows, channels)
 
 

time: 46.7 us -> 48 us (1.028)
  starting transfers between devices: 19.6 us -> 21.9 us
  waiting for transfers between devices: 14.9 us -> 13.4 us
  Pallas kernels: 11.8 us -> 12.4 us
    ppermute x23 -> x19, starting transfers between devices: 19.6 us -> 21.9 us  [swap(): lax.ppermute(value, axis, [(i, i ^ mask) for i in range(lax.axis_size(axi...]
    ppermute x23 -> x19, waiting for transfers between devices: 14.9 us -> 13.4 us  [swap(): lax.ppermute(value, axis, [(i, i ^ mask) for i in range(lax.axis_size(axi...]
    pallas_call x1 -> x4, Pallas kernels: 0.9 us -> 1.53 us  [the longest x2 1.5 us: body(): pl.pallas_call(functools.partial(place_kernel, masks=masks), in_specs=[sm...]
  transfers between devices with their start and end apart: 23 -> 19, of which waited for: 7 -> 10; matrix products, arithmetic and copies ran while one was open for 0% -> 0% of each run, Pallas kernels for 9% -> 10%
where the time goes in v4:
time: 48 us; the launch traced here: 47.9 us
  starting transfers between devices  21.9 us (46%)
  waiting for transfers between devices  13.4 us (28%)
  Pallas kernels  12.4 us (26%)
    ppermute x19, starting transfers between devices, swap(): lax.ppermute(value, axis, [(i, i ^ mask) for i in range(lax.axis_size(axi...  21.9 us
    ppermute x19, waiting for transfers between devices, swap(): lax.ppermute(value, axis, [(i, i ^ mask) for i in range(lax.axis_size(axi...  13.4 us
    pallas_call x1, Pallas kernels, body(): pl.pallas_call(functools.partial(backward_kernel, **sizes), in_specs=[sme...  5.1 us
    pallas_call x1, Pallas kernels, body(): pl.pallas_call(functools.partial(forward_kernel, **sizes), in_specs=[smem...  3.92 us
    pallas_call x1, Pallas kernels, body(): pl.pallas_call(functools.partial(pack_kernel, peers=peers), in_specs=[sme...  1.58 us
    pallas_call x2, Pallas kernels, body(): pl.pallas_call(functools.partial(place_kernel, masks=masks), in_specs=[sm...  1.5 us
  transfers between devices with their start and end apart: 19, of which 10 were waited for; matrix products, arithmetic and copies ran while one was open for 0% of the time, Pallas kernels for 10%

profile of v4, /device:TPU:0, one launch (start us, length us, event | category | flops | bytes accessed | tf_op | source)
XLA Modules:
  0.0 47.9 jit_solution(5213327684124987627)
XLA Ops:
  0.0 1.6 %pack.1 = (bf16[2,4,8,1280]{3,2,1,0:T(8,128)(2,1)S(1)}, bf16[2,4,8,1280]{3,2,1,0:T(8,128)(2,1)S(1)}, bf16[2,4,8,1280]{3,2,1,0:T(8,128)(2,1)S(1)}, bf16[2,4,8,128...) custom-call(s32[1]{0:T(128)} %bitcast.me_ref, bf16[4,8,8,1280]{3,2,1,0:T(8,128)(2,1)} %bitcast.46, ...), custom_call_target="tpu_custom_call" | custom-call | tf_op jit(solution)/shard_map/pack/pallas_call | solution.py:339
  1.6 3.1 %collective-permute-start.5 = (f32[4,128]{1,0:T(4,128)S(1)}, f32[4,128]{1,0:T(4,128)S(1)}, u32[]{:S(2)}, u32[]{:S(2)}) collective-permute-start(f32[4,128]{1,0:T(4,128)S(1)} %get-tuple-element.36), channel_id=1, source_target_pairs={{0,1},{1,0},{2,3},{3,2},{4,5},{5,4},{6,7},{7,6},{8,9},{9,8},{10,11... | collective-permute-start | bytes 6152 | tf_op jit(solution)/shard_map/ppermute | solution.py:265
  4.7 1.6 %collective-permute-done.5 = f32[4,128]{1,0:T(4,128)S(1)} collective-permute-done((f32[4,128]{1,0:T(4,128)S(1)}, f32[4,128]{1,0:T(4,128)S(1)}, u32[]{:S(2)}, u32[]{:S(2)}) %collective-permute-start.5) | collective-permute-done | bytes 2080 | tf_op jit(solution)/shard_map/ppermute | solution.py:265
  6.3 3.0 %collective-permute-start.6 = (f32[4,128]{1,0:T(4,128)S(1)}, f32[4,128]{1,0:T(4,128)S(1)}, u32[]{:S(2)}, u32[]{:S(2)}) collective-permute-start(f32[4,128]{1,0:T(4,128)S(1)} %add.3.refs_0_), channel_id=1, source_target_pairs={{0,2},{1,3},{2,0},{3,1},{4,6},{5,7},{6,4},{7,5},{8,10},{9,11},{10,... | collective-permute-start | bytes 6152 | tf_op jit(solution)/shard_map/ppermute | solution.py:265
  9.3 1.5 %collective-permute-start = (bf16[2,4,8,1280]{3,2,1,0:T(8,128)(2,1)S(1)}, bf16[2,4,8,1280]{3,2,1,0:T(8,128)(2,1)S(1)}, u32[]{:S(2)}, u32[]{:S(2)}) collective-permute-start(bf16[2,4,8,1280]{3,2,1,0:T(8,128)(2,1)S(1)} %get-tuple-element.28), channel_id=1, source_target_pairs={{0,8},{4,12},{8,0},{12,4},{16,24},{20,28},{24,16},{28,20},{1,9},{5... | collective-permute-start | bytes 491528 | tf_op jit(solution)/shard_map/ppermute | solution.py:265
  10.8 1.5 %collective-permute-start.1 = (bf16[2,4,8,1280]{3,2,1,0:T(8,128)(2,1)S(1)}, bf16[2,4,8,1280]{3,2,1,0:T(8,128)(2,1)S(1)}, u32[]{:S(2)}, u32[]{:S(2)}) collective-permute-start(bf16[2,4,8,1280]{3,2,1,0:T(8,128)(2,1)S(1)} %get-tuple-element.29), channel_id=1, source_target_pairs={{0,16},{4,20},{8,24},{12,28},{16,0},{20,4},{24,8},{28,12},{1,17},{... | collective-permute-start | bytes 491528 | tf_op jit(solution)/shard_map/ppermute | solution.py:265
  12.3 0.5 collective-permute-start.2
  12.8 0.2 scale.1
  13.0 1.6 %collective-permute-start.7 = (bf16[2,4,8,1280]{3,2,1,0:T(8,128)(2,1)S(1)}, bf16[2,4,8,1280]{3,2,1,0:T(8,128)(2,1)S(1)}, u32[]{:S(2)}, u32[]{:S(2)}) collective-permute-start(bf16[2,4,8,1280]{3,2,1,0:T(8,128)(2,1)S(1)} %get-tuple-element.38), channel_id=1, source_target_pairs={{0,8},{4,12},{8,0},{12,4},{16,24},{20,28},{24,16},{28,20},{1,9},{5... | collective-permute-start | bytes 491528 | tf_op jit(solution)/shard_map/ppermute | solution.py:265
  14.6 1.5 %collective-permute-start.8 = (bf16[2,4,8,1280]{3,2,1,0:T(8,128)(2,1)S(1)}, bf16[2,4,8,1280]{3,2,1,0:T(8,128)(2,1)S(1)}, u32[]{:S(2)}, u32[]{:S(2)}) collective-permute-start(bf16[2,4,8,1280]{3,2,1,0:T(8,128)(2,1)S(1)} %get-tuple-element.39), channel_id=1, source_target_pairs={{0,16},{4,20},{8,24},{12,28},{16,0},{20,4},{24,8},{28,12},{1,17},{... | collective-permute-start | bytes 491528 | tf_op jit(solution)/shard_map/ppermute | solution.py:265
  16.1 0.3 collective-permute-done
  16.4 2.4 %collective-permute-start.9 = (bf16[2,4,8,1280]{3,2,1,0:T(8,128)(2,1)S(1)}, bf16[2,4,8,1280]{3,2,1,0:T(8,128)(2,1)S(1)}, u32[]{:S(2)}, u32[]{:S(2)}) collective-permute-start(bf16[2,4,8,1280]{3,2,1,0:T(8,128)(2,1)S(1)} %get-tuple-element.40), channel_id=1, source_target_pairs={{0,24},{4,28},{8,16},{12,20},{16,8},{20,12},{24,0},{28,4},{1,25},{... | collective-permute-start | bytes 491528 | tf_op jit(solution)/shard_map/ppermute | solution.py:265
  18.8 2.5 %collective-permute-done.1 = bf16[2,4,8,1280]{3,2,1,0:T(8,128)(2,1)S(1)} collective-permute-done((bf16[2,4,8,1280]{3,2,1,0:T(8,128)(2,1)S(1)}, bf16[2,4,8,1280]{3,2,1,0:T(8,128)(2,1)S(1)}, u32[]{:S(2)}, u32[]{:S(2)}) %collective-permute-start.1) | collective-permute-done | bytes 163872 | tf_op jit(solution)/shard_map/ppermute | solution.py:265
  21.3 0.6 %collective-permute-start.4 = (bf16[3,32,1280]{2,1,0:T(8,128)(2,1)S(1)}, bf16[3,32,1280]{2,1,0:T(8,128)(2,1)S(1)}, u32[]{:S(2)}, u32[]{:S(2)}) collective-permute-start(bf16[3,32,1280]{2,1,0:T(8,128)(2,1)S(1)} %join.2), channel_id=1, source_target_pairs={{0,4},{4,0},{8,12},{12,8},{16,20},{20,16},{24,28},{28,24},{1,5},{5... | collective-permute-start | bytes 737288 | tf_op jit(solution)/shard_map/ppermute | solution.py:265
  21.9 1.3 %collective-permute-done.7 = bf16[2,4,8,1280]{3,2,1,0:T(8,128)(2,1)S(1)} collective-permute-done((bf16[2,4,8,1280]{3,2,1,0:T(8,128)(2,1)S(1)}, bf16[2,4,8,1280]{3,2,1,0:T(8,128)(2,1)S(1)}, u32[]{:S(2)}, u32[]{:S(2)}) %collective-permute-start.7) | collective-permute-done | bytes 163872 | tf_op jit(solution)/shard_map/ppermute | solution.py:265
  23.2 3.0 %collective-permute-done.8 = bf16[2,4,8,1280]{3,2,1,0:T(8,128)(2,1)S(1)} collective-permute-done((bf16[2,4,8,1280]{3,2,1,0:T(8,128)(2,1)S(1)}, bf16[2,4,8,1280]{3,2,1,0:T(8,128)(2,1)S(1)}, u32[]{:S(2)}, u32[]{:S(2)}) %collective-permute-start.8) | collective-permute-done | bytes 163872 | tf_op jit(solution)/shard_map/ppermute | solution.py:265
  26.3 0.5 %collective-permute-start.10 = (bf16[32,1280]{1,0:T(8,128)(2,1)S(1)}, bf16[32,1280]{1,0:T(8,128)(2,1)S(1)}, u32[]{:S(2)}, u32[]{:S(2)}) collective-permute-start(bf16[32,1280]{1,0:T(8,128)(2,1)S(1)} %slice_bitcast_fusion), channel_id=1, source_target_pairs={{0,4},{4,0},{8,12},{12,8},{16,20},{20,16},{24,28},{28,24},{1,5},{5... | collective-permute-start | bytes 245768 | tf_op jit(solution)/shard_map/ppermute | solution.py:265
  27.0 3.9 %forward.1 = (bf16[256,1280]{1,0:T(8,128)(2,1)S(1)}, bf16[256,1280]{1,0:T(8,128)(2,1)S(1)}, bf16[256,1280]{1,0:T(8,128)(2,1)S(1)}, f32[20,32,256]{2,1,0:T(8,128)S(1)}) custom-call(s32[1]{0:T(128)} %bitcast.me_ref, bf16[2,256,256]{2,1,0:T(8,128)(2,1)S(1)} %order.1.order_ref, f32[3,1280]{1,0:T(4,128)S(1)} %copy-done.3, f32[1280]{0:T(1024)S(1)} %copy-done.4, ...), custom_call_target="tpu_custom_call" | custom-call | tf_op jit(solution)/shard_map/forward/pallas_call | solution.py:371
  30.9 5.1 %backward.1 = (bf16[32,1280]{1,0:T(8,128)(2,1)S(1)}, bf16[32,1280]{1,0:T(8,128)(2,1)S(1)}, bf16[32,1280]{1,0:T(8,128)(2,1)S(1)}, bf16[32,1280]{1,0:T(8,128)(2,1)...) custom-call(s32[1]{0:T(128)} %bitcast.me_ref, ...), custom_call_target="tpu_custom_call" | custom-call | tf_op jit(solution)/shard_map/backward/pallas_call | solution.py:382
  36.0 0.1 collective-permute-start.16
  36.2 0.8 %collective-permute-start.17 = (bf16[32,1280]{1,0:T(8,128)(2,1)S(1)}, bf16[32,1280]{1,0:T(8,128)(2,1)S(1)}, u32[]{:S(2)}, u32[]{:S(2)}) collective-permute-start(bf16[32,1280]{1,0:T(8,128)(2,1)S(1)} %get-tuple-element.47), channel_id=1, source_target_pairs={{0,24},{4,28},{8,16},{12,20},{16,8},{20,12},{24,0},{28,4},{1,25},{... | collective-permute-start | bytes 245768 | tf_op jit(solution)/shard_map/ppermute | solution.py:265
  37.0 1.8 %collective-permute-start.18 = (bf16[32,1280]{1,0:T(8,128)(2,1)S(1)}, bf16[32,1280]{1,0:T(8,128)(2,1)S(1)}, u32[]{:S(2)}, u32[]{:S(2)}) collective-permute-start(bf16[32,1280]{1,0:T(8,128)(2,1)S(1)} %get-tuple-element.48), channel_id=1, source_target_pairs={{0,28},{4,24},{8,20},{12,16},{16,12},{20,8},{24,4},{28,0},{1,29},{... | collective-permute-start | bytes 245768 | tf_op jit(solution)/shard_map/ppermute | solution.py:265
  38.9 0.6 %collective-permute-start.12 = (bf16[32,1280]{1,0:T(8,128)(2,1)S(1)}, bf16[32,1280]{1,0:T(8,128)(2,1)S(1)}, u32[]{:S(2)}, u32[]{:S(2)}) collective-permute-start(bf16[32,1280]{1,0:T(8,128)(2,1)S(1)} %get-tuple-element.41), channel_id=1, source_target_pairs={{0,8},{4,12},{8,0},{12,4},{16,24},{20,28},{24,16},{28,20},{1,9},{5... | collective-permute-start | bytes 245768 | tf_op jit(solution)/shard_map/ppermute | solution.py:265
  39.5 1.1 %collective-permute-start.13 = (bf16[32,1280]{1,0:T(8,128)(2,1)S(1)}, bf16[32,1280]{1,0:T(8,128)(2,1)S(1)}, u32[]{:S(2)}, u32[]{:S(2)}) collective-permute-start(bf16[32,1280]{1,0:T(8,128)(2,1)S(1)} %get-tuple-element.42), channel_id=1, source_target_pairs={{0,12},{4,8},{8,4},{12,0},{16,28},{20,24},{24,20},{28,16},{1,13},{... | collective-permute-start | bytes 245768 | tf_op jit(solution)/shard_map/ppermute | solution.py:265
  40.6 1.0 %collective-permute-start.14 = (bf16[32,1280]{1,0:T(8,128)(2,1)S(1)}, bf16[32,1280]{1,0:T(8,128)(2,1)S(1)}, u32[]{:S(2)}, u32[]{:S(2)}) collective-permute-start(bf16[32,1280]{1,0:T(8,128)(2,1)S(1)} %get-tuple-element.43), channel_id=1, source_target_pairs={{0,16},{4,20},{8,24},{12,28},{16,0},{20,4},{24,8},{28,12},{1,17},{... | collective-permute-start | bytes 245768 | tf_op jit(solution)/shard_map/ppermute | solution.py:265
  41.6 0.8 %collective-permute-done.17 = bf16[32,1280]{1,0:T(8,128)(2,1)S(1)} collective-permute-done((bf16[32,1280]{1,0:T(8,128)(2,1)S(1)}, bf16[32,1280]{1,0:T(8,128)(2,1)S(1)}, u32[]{:S(2)}, u32[]{:S(2)}) %collective-permute-start.17) | collective-permute-done | bytes 81952 | tf_op jit(solution)/shard_map/ppermute | solution.py:265
  42.4 0.7 %collective-permute-done.18 = bf16[32,1280]{1,0:T(8,128)(2,1)S(1)} collective-permute-done((bf16[32,1280]{1,0:T(8,128)(2,1)S(1)}, bf16[32,1280]{1,0:T(8,128)(2,1)S(1)}, u32[]{:S(2)}, u32[]{:S(2)}) %collective-permute-start.18) | collective-permute-done | bytes 81952 | tf_op jit(solution)/shard_map/ppermute | solution.py:265
  43.1 0.8 %place.2.refs_4_ = bf16[4,8,8,1280]{3,2,1,0:T(8,128)(2,1)} custom-call(s32[1]{0:T(128)} %bitcast.me_ref, bf16[4,8,1280]{2,1,0:T(8,128)(2,1)S(1)} %bitcast.38, bf16[4,8,1280]{2,1,0:T(8,128)(2,1)S(1)} %bitcast.41, bf16[4,8,1280]{2,1,0:T(8,128)(2,1)S(1)} %bitcast.43, bf16[4,8,1280]{2,1,0:T(8,128)(2,1)S(1)} %bitcast.44), custom_call_target="tpu_custom_call" | custom-call | tf_op jit(solution)/shard_map/place/pallas_call | solution.py:401
  43.8 1.6 %collective-permute-done.12 = bf16[32,1280]{1,0:T(8,128)(2,1)S(1)} collective-permute-done((bf16[32,1280]{1,0:T(8,128)(2,1)S(1)}, bf16[32,1280]{1,0:T(8,128)(2,1)S(1)}, u32[]{:S(2)}, u32[]{:S(2)}) %collective-permute-start.12) | collective-permute-done | bytes 81952 | tf_op jit(solution)/shard_map/ppermute | solution.py:265
  45.5 0.7 %collective-permute-done.13 = bf16[32,1280]{1,0:T(8,128)(2,1)S(1)} collective-permute-done((bf16[32,1280]{1,0:T(8,128)(2,1)S(1)}, bf16[32,1280]{1,0:T(8,128)(2,1)S(1)}, u32[]{:S(2)}, u32[]{:S(2)}) %collective-permute-start.13) | collective-permute-done | bytes 81952 | tf_op jit(solution)/shard_map/ppermute | solution.py:265
  46.1 1.0 %collective-permute-done.15 = bf16[32,1280]{1,0:T(8,128)(2,1)S(1)} collective-permute-done((bf16[32,1280]{1,0:T(8,128)(2,1)S(1)}, bf16[32,1280]{1,0:T(8,128)(2,1)S(1)}, u32[]{:S(2)}, u32[]{:S(2)}) %collective-permute-start.15) | collective-permute-done | bytes 81952 | tf_op jit(solution)/shard_map/ppermute | solution.py:265
  47.1 0.8 %place.3 = bf16[4,8,8,1280]{3,2,1,0:T(8,128)(2,1)} custom-call(s32[1]{0:T(128)} %bitcast.me_ref, bf16[4,8,1280]{2,1,0:T(8,128)(2,1)S(1)} %bitcast.39, bf16[4,8,1280]{2,1,0:T(8,128)(2,1)S(1)} %bitcast.40, bf16[4,8,1280]{2,1,0:T(8,128)(2,1)S(1)} %bitcast.42, bf16[4,8,1280]{2,1,0:T(8,128)(2,1)S(1)} %bitcast.45, ...), custom_call_target="tpu_custom_call", output_to_operand_aliasing={{}: (5, {})} | custom-call | tf_op jit(solution)/shard_map/place/pallas_call | solution.py:401
  (28 shorter events, 0.3 us)
Async XLA Ops:
  1.6 4.7 %collective-permute-start.5 = (f32[4,128]{1,0:T(4,128)S(1)}, f32[4,128]{1,0:T(4,128)S(1)}, u32[]{:S(2)}, u32[]{:S(2)}) collective-permute-start(f32[4,128]{1,0:T(4,128)S(1)} %get-tuple-element.36), channel_id=1, source_target_pairs={{0,1},{1,0},{2,3},{3,2},{4,5},{5,4},{6,7},{7,6},{8,9},{9,8},{10,11... | collective-permute-start | bytes 6152 | tf_op jit(solution)/shard_map/ppermute | solution.py:265
  6.3 6.5 %collective-permute-start.6 = (f32[4,128]{1,0:T(4,128)S(1)}, f32[4,128]{1,0:T(4,128)S(1)}, u32[]{:S(2)}, u32[]{:S(2)}) collective-permute-start(f32[4,128]{1,0:T(4,128)S(1)} %add.3.refs_0_), channel_id=1, source_target_pairs={{0,2},{1,3},{2,0},{3,1},{4,6},{5,7},{6,4},{7,5},{8,10},{9,11},{10,... | collective-permute-start | bytes 6152 | tf_op jit(solution)/shard_map/ppermute | solution.py:265
  9.3 7.1 %collective-permute-start = (bf16[2,4,8,1280]{3,2,1,0:T(8,128)(2,1)S(1)}, bf16[2,4,8,1280]{3,2,1,0:T(8,128)(2,1)S(1)}, u32[]{:S(2)}, u32[]{:S(2)}) collective-permute-start(bf16[2,4,8,1280]{3,2,1,0:T(8,128)(2,1)S(1)} %get-tuple-element.28), channel_id=1, source_target_pairs={{0,8},{4,12},{8,0},{12,4},{16,24},{20,28},{24,16},{28,20},{1,9},{5... | collective-permute-start | bytes 491528 | tf_op jit(solution)/shard_map/ppermute | solution.py:265
  10.8 10.5 %collective-permute-start.1 = (bf16[2,4,8,1280]{3,2,1,0:T(8,128)(2,1)S(1)}, bf16[2,4,8,1280]{3,2,1,0:T(8,128)(2,1)S(1)}, u32[]{:S(2)}, u32[]{:S(2)}) collective-permute-start(bf16[2,4,8,1280]{3,2,1,0:T(8,128)(2,1)S(1)} %get-tuple-element.29), channel_id=1, source_target_pairs={{0,16},{4,20},{8,24},{12,28},{16,0},{20,4},{24,8},{28,12},{1,17},{... | collective-permute-start | bytes 491528 | tf_op jit(solution)/shard_map/ppermute | solution.py:265
  12.3 9.0 %collective-permute-start.2 = (bf16[2,4,8,1280]{3,2,1,0:T(8,128)(2,1)S(1)}, bf16[2,4,8,1280]{3,2,1,0:T(8,128)(2,1)S(1)}, u32[]{:S(2)}, u32[]{:S(2)}) collective-permute-start(bf16[2,4,8,1280]{3,2,1,0:T(8,128)(2,1)S(1)} %get-tuple-element.30), channel_id=1, source_target_pairs={{0,24},{4,28},{8,16},{12,20},{16,8},{20,12},{24,0},{28,4},{1,25},{... | collective-permute-start | bytes 491528 | tf_op jit(solution)/shard_map/ppermute | solution.py:265
  12.8 14.1 %copy-start = (bf16[1280,1280]{1,0:T(8,128)(2,1)S(1)}, bf16[1280,1280]{1,0:T(8,128)(2,1)}, u32[]{:S(2)}) copy-start(bf16[1280,1280]{1,0:T(8,128)(2,1)} %wq_ref.3) | copy-start | bytes 9830404
  12.8 14.1 %copy-start.1 = (bf16[1280,1280]{1,0:T(8,128)(2,1)S(1)}, bf16[1280,1280]{1,0:T(8,128)(2,1)}, u32[]{:S(2)}) copy-start(bf16[1280,1280]{1,0:T(8,128)(2,1)} %wk_ref.3) | copy-start | bytes 9830404
  12.8 14.2 %copy-start.2 = (bf16[1280,1280]{1,0:T(8,128)(2,1)S(1)}, bf16[1280,1280]{1,0:T(8,128)(2,1)}, u32[]{:S(2)}) copy-start(bf16[1280,1280]{1,0:T(8,128)(2,1)} %wv_ref.3) | copy-start | bytes 9830404
  12.8 14.2 %copy-start.3 = (f32[3,1280]{1,0:T(4,128)S(1)}, f32[3,1280]{1,0:T(4,128)}, u32[]{:S(2)}) copy-start(f32[3,1280]{1,0:T(4,128)} %taps_ref.3) | copy-start | bytes 46084
  12.8 14.2 %copy-start.4 = (f32[1280]{0:T(1024)S(1)}, f32[1280]{0:T(1024)}, u32[]{:S(2)}) copy-start(f32[1280]{0:T(1024)} %bias_ref.1) | copy-start | bytes 15364
  13.0 10.2 %collective-permute-start.7 = (bf16[2,4,8,1280]{3,2,1,0:T(8,128)(2,1)S(1)}, bf16[2,4,8,1280]{3,2,1,0:T(8,128)(2,1)S(1)}, u32[]{:S(2)}, u32[]{:S(2)}) collective-permute-start(bf16[2,4,8,1280]{3,2,1,0:T(8,128)(2,1)S(1)} %get-tuple-element.38), channel_id=1, source_target_pairs={{0,8},{4,12},{8,0},{12,4},{16,24},{20,28},{24,16},{28,20},{1,9},{5... | collective-permute-start | bytes 491528 | tf_op jit(solution)/shard_map/ppermute | solution.py:265
  14.6 11.7 %collective-permute-start.8 = (bf16[2,4,8,1280]{3,2,1,0:T(8,128)(2,1)S(1)}, bf16[2,4,8,1280]{3,2,1,0:T(8,128)(2,1)S(1)}, u32[]{:S(2)}, u32[]{:S(2)}) collective-permute-start(bf16[2,4,8,1280]{3,2,1,0:T(8,128)(2,1)S(1)} %get-tuple-element.39), channel_id=1, source_target_pairs={{0,16},{4,20},{8,24},{12,28},{16,0},{20,4},{24,8},{28,12},{1,17},{... | collective-permute-start | bytes 491528 | tf_op jit(solution)/shard_map/ppermute | solution.py:265
  16.4 9.8 %collective-permute-start.9 = (bf16[2,4,8,1280]{3,2,1,0:T(8,128)(2,1)S(1)}, bf16[2,4,8,1280]{3,2,1,0:T(8,128)(2,1)S(1)}, u32[]{:S(2)}, u32[]{:S(2)}) collective-permute-start(bf16[2,4,8,1280]{3,2,1,0:T(8,128)(2,1)S(1)} %get-tuple-element.40), channel_id=1, source_target_pairs={{0,24},{4,28},{8,16},{12,20},{16,8},{20,12},{24,0},{28,4},{1,25},{... | collective-permute-start | bytes 491528 | tf_op jit(solution)/shard_map/ppermute | solution.py:265
  21.3 5.6 %collective-permute-start.3 = (bf16[32,1280]{1,0:T(8,128)(2,1)S(1)}, bf16[32,1280]{1,0:T(8,128)(2,1)S(1)}, u32[]{:S(2)}, u32[]{:S(2)}) collective-permute-start(bf16[32,1280]{1,0:T(8,128)(2,1)S(1)} %slice_bitcast_fusion.1), channel_id=1, source_target_pairs={{0,4},{4,0},{8,12},{12,8},{16,20},{20,16},{24,28},{28,24},{1,5},{5... | collective-permute-start | bytes 245768 | tf_op jit(solution)/shard_map/ppermute | solution.py:265
  21.3 5.6 %collective-permute-start.4 = (bf16[3,32,1280]{2,1,0:T(8,128)(2,1)S(1)}, bf16[3,32,1280]{2,1,0:T(8,128)(2,1)S(1)}, u32[]{:S(2)}, u32[]{:S(2)}) collective-permute-start(bf16[3,32,1280]{2,1,0:T(8,128)(2,1)S(1)} %join.2), channel_id=1, source_target_pairs={{0,4},{4,0},{8,12},{12,8},{16,20},{20,16},{24,28},{28,24},{1,5},{5... | collective-permute-start | bytes 737288 | tf_op jit(solution)/shard_map/ppermute | solution.py:265
  26.2 4.7 %collective-permute-start.11 = (bf16[3,32,1280]{2,1,0:T(8,128)(2,1)S(1)}, bf16[3,32,1280]{2,1,0:T(8,128)(2,1)S(1)}, u32[]{:S(2)}, u32[]{:S(2)}) collective-permute-start(bf16[3,32,1280]{2,1,0:T(8,128)(2,1)S(1)} %join.3), channel_id=1, source_target_pairs={{0,4},{4,0},{8,12},{12,8},{16,20},{20,16},{24,28},{28,24},{1,5},{5... | collective-permute-start | bytes 737288 | tf_op jit(solution)/shard_map/ppermute | solution.py:265
  26.3 4.6 %collective-permute-start.10 = (bf16[32,1280]{1,0:T(8,128)(2,1)S(1)}, bf16[32,1280]{1,0:T(8,128)(2,1)S(1)}, u32[]{:S(2)}, u32[]{:S(2)}) collective-permute-start(bf16[32,1280]{1,0:T(8,128)(2,1)S(1)} %slice_bitcast_fusion), channel_id=1, source_target_pairs={{0,4},{4,0},{8,12},{12,8},{16,20},{20,16},{24,28},{28,24},{1,5},{5... | collective-permute-start | bytes 245768 | tf_op jit(solution)/shard_map/ppermute | solution.py:265
  36.0 4.5 %collective-permute-start.16 = (bf16[32,1280]{1,0:T(8,128)(2,1)S(1)}, bf16[32,1280]{1,0:T(8,128)(2,1)S(1)}, u32[]{:S(2)}, u32[]{:S(2)}) collective-permute-start(bf16[32,1280]{1,0:T(8,128)(2,1)S(1)} %get-tuple-element.46), channel_id=1, source_target_pairs={{0,4},{4,0},{8,12},{12,8},{16,20},{20,16},{24,28},{28,24},{1,5},{5... | collective-permute-start | bytes 245768 | tf_op jit(solution)/shard_map/ppermute | solution.py:265
  36.2 6.2 %collective-permute-start.17 = (bf16[32,1280]{1,0:T(8,128)(2,1)S(1)}, bf16[32,1280]{1,0:T(8,128)(2,1)S(1)}, u32[]{:S(2)}, u32[]{:S(2)}) collective-permute-start(bf16[32,1280]{1,0:T(8,128)(2,1)S(1)} %get-tuple-element.47), channel_id=1, source_target_pairs={{0,24},{4,28},{8,16},{12,20},{16,8},{20,12},{24,0},{28,4},{1,25},{... | collective-permute-start | bytes 245768 | tf_op jit(solution)/shard_map/ppermute | solution.py:265
  37.0 6.0 %collective-permute-start.18 = (bf16[32,1280]{1,0:T(8,128)(2,1)S(1)}, bf16[32,1280]{1,0:T(8,128)(2,1)S(1)}, u32[]{:S(2)}, u32[]{:S(2)}) collective-permute-start(bf16[32,1280]{1,0:T(8,128)(2,1)S(1)} %get-tuple-element.48), channel_id=1, source_target_pairs={{0,28},{4,24},{8,20},{12,16},{16,12},{20,8},{24,4},{28,0},{1,29},{... | collective-permute-start | bytes 245768 | tf_op jit(solution)/shard_map/ppermute | solution.py:265
  38.9 6.6 %collective-permute-start.12 = (bf16[32,1280]{1,0:T(8,128)(2,1)S(1)}, bf16[32,1280]{1,0:T(8,128)(2,1)S(1)}, u32[]{:S(2)}, u32[]{:S(2)}) collective-permute-start(bf16[32,1280]{1,0:T(8,128)(2,1)S(1)} %get-tuple-element.41), channel_id=1, source_target_pairs={{0,8},{4,12},{8,0},{12,4},{16,24},{20,28},{24,16},{28,20},{1,9},{5... | collective-permute-start | bytes 245768 | tf_op jit(solution)/shard_map/ppermute | solution.py:265
  39.5 6.6 %collective-permute-start.13 = (bf16[32,1280]{1,0:T(8,128)(2,1)S(1)}, bf16[32,1280]{1,0:T(8,128)(2,1)S(1)}, u32[]{:S(2)}, u32[]{:S(2)}) collective-permute-start(bf16[32,1280]{1,0:T(8,128)(2,1)S(1)} %get-tuple-element.42), channel_id=1, source_target_pairs={{0,12},{4,8},{8,4},{12,0},{16,28},{20,24},{24,20},{28,16},{1,13},{... | collective-permute-start | bytes 245768 | tf_op jit(solution)/shard_map/ppermute | solution.py:265
  40.6 5.5 %collective-permute-start.14 = (bf16[32,1280]{1,0:T(8,128)(2,1)S(1)}, bf16[32,1280]{1,0:T(8,128)(2,1)S(1)}, u32[]{:S(2)}, u32[]{:S(2)}) collective-permute-start(bf16[32,1280]{1,0:T(8,128)(2,1)S(1)} %get-tuple-element.43), channel_id=1, source_target_pairs={{0,16},{4,20},{8,24},{12,28},{16,0},{20,4},{24,8},{28,12},{1,17},{... | collective-permute-start | bytes 245768 | tf_op jit(solution)/shard_map/ppermute | solution.py:265
  42.4 4.7 %collective-permute-start.15 = (bf16[32,1280]{1,0:T(8,128)(2,1)S(1)}, bf16[32,1280]{1,0:T(8,128)(2,1)S(1)}, u32[]{:S(2)}, u32[]{:S(2)}) collective-permute-start(bf16[32,1280]{1,0:T(8,128)(2,1)S(1)} %get-tuple-element.44), channel_id=1, source_target_pairs={{0,20},{4,16},{8,28},{12,24},{16,4},{20,0},{24,12},{28,8},{1,21},{... | collective-permute-start | bytes 245768 | tf_op jit(solution)/shard_map/ppermute | solution.py:265

commit v5 on v4

--- a/solution.py
+++ b/solution.py
@@ -125,10 +125,10 @@
     order_ref[1] = reorder_matrix(frames, toks, False)
 
 
-def forward_kernel(me_ref, order_ref, taps_ref, bias_ref, wq_ref, wk_ref, wv_ref, *refs,
+def forward_kernel(me_ref, order_ref, taps_ref, bias_ref, wq_ref, wk_ref, *refs,
                    frames, toks, peers):
     blocks = refs[:peers // 2 + 2]
-    q_ref, k_ref, v_ref, prob_ref, source_ref, hidden_ref = refs[peers // 2 + 2:]
+    q_ref, k_ref, prob_ref, hidden_ref, source_ref = refs[peers // 2 + 2:]
     rows, channels = hidden_ref.shape
     part = rows // peers
     me = me_ref[0]
@@ -138,12 +138,12 @@
     for col in range(0, channels, BLOCK):
         cols = slice(col, col + BLOCK)
         source = source_ref[:, cols]
-        mixed = (
+        hidden = (
             taps_ref[0:1, cols] * pltpu.roll(source, toks, 0)
-            + taps_ref[1:2, cols] * source
+            + (1.0 + taps_ref[1:2, cols]) * source
             + taps_ref[2:3, cols] * pltpu.roll(source, rows - toks, 0)
-        )
-        hidden = (source + mixed + bias_ref[cols].reshape(1, BLOCK)).astype(jnp.bfloat16)
+            + bias_ref[cols].reshape(1, BLOCK)
+        ).astype(jnp.bfloat16)
         hidden_ref[:, cols] = jnp.dot(
             order_ref[0], hidden, preferred_element_type=jnp.float32
         ).astype(jnp.bfloat16)
@@ -152,7 +152,7 @@
     inv_root = 1.0 / math.sqrt(HEAD_DIM)
     for col in range(0, channels, BLOCK):
         block = slice(col, col + BLOCK)
-        for weight_ref, out_ref in ((wq_ref, q_ref), (wk_ref, k_ref), (wv_ref, v_ref)):
+        for weight_ref, out_ref in ((wq_ref, q_ref), (wk_ref, k_ref)):
             out_ref[:, block] = jnp.dot(
                 hidden_ref[...], weight_ref[:, block], preferred_element_type=jnp.float32
             ).astype(jnp.bfloat16)
@@ -171,6 +171,12 @@
                     prob_ref[start // HEAD_DIM + head, :, here] = expo * inverse
 
 
+def value_kernel(hidden_ref, wv_ref, v_ref):
+    v_ref[...] = jnp.dot(
+        hidden_ref[...], wv_ref[...], preferred_element_type=jnp.float32
+    ).astype(jnp.bfloat16)
+
+
 def backward_kernel(me_ref, order_ref, taps_ref, wq_ref, wk_ref, wv_ref, q_ref, k_ref, v_ref,
                     prob_ref, *refs, frames, toks, peers):
     blocks = refs[:peers // 2 + 2]
@@ -251,9 +257,8 @@
             order_ref[1], total[cols], NT, preferred_element_type=jnp.float32
         )
         result_ref[:, cols] = (
-            source
-            + taps_ref[0:1, cols] * pltpu.roll(source, rows - toks, 0)
-            + taps_ref[1:2, cols] * source
+            taps_ref[0:1, cols] * pltpu.roll(source, rows - toks, 0)
+            + (1.0 + taps_ref[1:2, cols]) * source
             + taps_ref[2:3, cols] * pltpu.roll(source, toks, 0)
         ).astype(jnp.bfloat16)
     for mask in range(peers):
@@ -368,17 +373,24 @@
         compiler_params=grant(4),
         name="order",
     )())
-    query, key, value, prob = pl.pallas_call(
+    query, key, prob, hidden = pl.pallas_call(
         functools.partial(forward_kernel, **sizes),
-        in_specs=[smem] + [vmem] * (8 + peers // 2),
+        in_specs=[smem] + [vmem] * (7 + peers // 2),
         out_specs=[vmem] * 4,
-        out_shape=[low((rows, channels))] * 3 + [pltpu.VMEM((heads, frames, rows), jnp.float32)],
-        scratch_shapes=[
-            pltpu.VMEM((rows, channels), jnp.float32), pltpu.VMEM((rows, channels), jnp.bfloat16)
-        ],
+        out_shape=[low((rows, channels))] * 2
+        + [pltpu.VMEM((heads, frames, rows), jnp.float32), low((rows, channels))],
+        scratch_shapes=[pltpu.VMEM((rows, channels), jnp.float32)],
         compiler_params=grant(20),
         name="forward",
-    )(me_arg, order, conv_taps, conv_bias, *weights, *map(on_chip, token_blocks))
+    )(me_arg, order, conv_taps, conv_bias, *weights[:2], *map(on_chip, token_blocks))
+    value = pl.pallas_call(
+        value_kernel,
+        in_specs=[vmem] * 2,
+        out_specs=vmem,
+        out_shape=low((rows, channels)),
+        compiler_params=grant(8),
+        name="value",
+    )(on_chip(hidden), weights[2])
     results = pl.pallas_call(
         functools.partial(backward_kernel, **sizes),
         in_specs=[smem] + [vmem] * (11 + peers // 2),

time: 48 us -> 48.6 us (1.012)
  Pallas kernels: 12.4 us -> 12.9 us
    pallas_call x0 -> x1, Pallas kernels: none -> 1.02 us  [body(): pl.pallas_call(value_kernel, in_specs=[vmem] * 2, out_specs=vmem, out_sha...]
  transfers between devices with their start and end apart: 19 -> 19, of which waited for: 10 -> 10; matrix products, arithmetic and copies ran while one was open for 0% -> 0% of each run, Pallas kernels for 10% -> 11%
where the time goes in v5:
time: 48.6 us; the launch traced here: 48.4 us
  starting transfers between devices  21.9 us (45%)
  waiting for transfers between devices  13.5 us (28%)
  Pallas kernels  12.9 us (27%)
    ppermute x19, starting transfers between devices, swap(): lax.ppermute(value, axis, [(i, i ^ mask) for i in range(lax.axis_size(axi...  21.9 us
    ppermute x19, waiting for transfers between devices, swap(): lax.ppermute(value, axis, [(i, i ^ mask) for i in range(lax.axis_size(axi...  13.5 us
    pallas_call x1, Pallas kernels, body(): pl.pallas_call(functools.partial(backward_kernel, **sizes), in_specs=[sme...  5.06 us
    pallas_call x1, Pallas kernels, body(): pl.pallas_call(functools.partial(forward_kernel, **sizes), in_specs=[smem...  3.46 us
    pallas_call x1, Pallas kernels, body(): pl.pallas_call(functools.partial(pack_kernel, peers=peers), in_specs=[sme...  1.58 us
    pallas_call x2, Pallas kernels, body(): pl.pallas_call(functools.partial(place_kernel, masks=masks), in_specs=[sm...  1.5 us
    pallas_call x1, Pallas kernels, body(): pl.pallas_call(value_kernel, in_specs=[vmem] * 2, out_specs=vmem, out_sha...  1.02 us
  transfers between devices with their start and end apart: 19, of which 10 were waited for; matrix products, arithmetic and copies ran while one was open for 0% of the time, Pallas kernels for 11%

profile of v5, /device:TPU:0, one launch (start us, length us, event | category | flops | bytes accessed | tf_op | source)
XLA Modules:
  0.0 48.4 jit_solution(18338996008363267879)
XLA Ops:
  0.0 1.6 %pack.1 = (bf16[2,4,8,1280]{3,2,1,0:T(8,128)(2,1)S(1)}, bf16[2,4,8,1280]{3,2,1,0:T(8,128)(2,1)S(1)}, bf16[2,4,8,1280]{3,2,1,0:T(8,128)(2,1)S(1)}, bf16[2,4,8,128...) custom-call(s32[1]{0:T(128)} %bitcast.me_ref, bf16[4,8,8,1280]{3,2,1,0:T(8,128)(2,1)} %bitcast.46, ...), custom_call_target="tpu_custom_call" | custom-call | tf_op jit(solution)/shard_map/pack/pallas_call | solution.py:344
  1.6 3.1 %collective-permute-start.5 = (f32[4,128]{1,0:T(4,128)S(1)}, f32[4,128]{1,0:T(4,128)S(1)}, u32[]{:S(2)}, u32[]{:S(2)}) collective-permute-start(f32[4,128]{1,0:T(4,128)S(1)} %get-tuple-element.36), channel_id=1, source_target_pairs={{0,1},{1,0},{2,3},{3,2},{4,5},{5,4},{6,7},{7,6},{8,9},{9,8},{10,11... | collective-permute-start | bytes 6152 | tf_op jit(solution)/shard_map/ppermute | solution.py:270
  4.7 1.6 %collective-permute-done.5 = f32[4,128]{1,0:T(4,128)S(1)} collective-permute-done((f32[4,128]{1,0:T(4,128)S(1)}, f32[4,128]{1,0:T(4,128)S(1)}, u32[]{:S(2)}, u32[]{:S(2)}) %collective-permute-start.5) | collective-permute-done | bytes 2080 | tf_op jit(solution)/shard_map/ppermute | solution.py:270
  6.3 3.0 %collective-permute-start.6 = (f32[4,128]{1,0:T(4,128)S(1)}, f32[4,128]{1,0:T(4,128)S(1)}, u32[]{:S(2)}, u32[]{:S(2)}) collective-permute-start(f32[4,128]{1,0:T(4,128)S(1)} %add.3.refs_0_), channel_id=1, source_target_pairs={{0,2},{1,3},{2,0},{3,1},{4,6},{5,7},{6,4},{7,5},{8,10},{9,11},{10,... | collective-permute-start | bytes 6152 | tf_op jit(solution)/shard_map/ppermute | solution.py:270
  9.3 1.5 %collective-permute-start = (bf16[2,4,8,1280]{3,2,1,0:T(8,128)(2,1)S(1)}, bf16[2,4,8,1280]{3,2,1,0:T(8,128)(2,1)S(1)}, u32[]{:S(2)}, u32[]{:S(2)}) collective-permute-start(bf16[2,4,8,1280]{3,2,1,0:T(8,128)(2,1)S(1)} %get-tuple-element.28), channel_id=1, source_target_pairs={{0,8},{4,12},{8,0},{12,4},{16,24},{20,28},{24,16},{28,20},{1,9},{5... | collective-permute-start | bytes 491528 | tf_op jit(solution)/shard_map/ppermute | solution.py:270
  10.8 1.5 %collective-permute-start.1 = (bf16[2,4,8,1280]{3,2,1,0:T(8,128)(2,1)S(1)}, bf16[2,4,8,1280]{3,2,1,0:T(8,128)(2,1)S(1)}, u32[]{:S(2)}, u32[]{:S(2)}) collective-permute-start(bf16[2,4,8,1280]{3,2,1,0:T(8,128)(2,1)S(1)} %get-tuple-element.29), channel_id=1, source_target_pairs={{0,16},{4,20},{8,24},{12,28},{16,0},{20,4},{24,8},{28,12},{1,17},{... | collective-permute-start | bytes 491528 | tf_op jit(solution)/shard_map/ppermute | solution.py:270
  12.3 0.5 collective-permute-start.2
  12.8 0.2 scale.1
  13.0 1.6 %collective-permute-start.7 = (bf16[2,4,8,1280]{3,2,1,0:T(8,128)(2,1)S(1)}, bf16[2,4,8,1280]{3,2,1,0:T(8,128)(2,1)S(1)}, u32[]{:S(2)}, u32[]{:S(2)}) collective-permute-start(bf16[2,4,8,1280]{3,2,1,0:T(8,128)(2,1)S(1)} %get-tuple-element.38), channel_id=1, source_target_pairs={{0,8},{4,12},{8,0},{12,4},{16,24},{20,28},{24,16},{28,20},{1,9},{5... | collective-permute-start | bytes 491528 | tf_op jit(solution)/shard_map/ppermute | solution.py:270
  14.6 1.5 %collective-permute-start.8 = (bf16[2,4,8,1280]{3,2,1,0:T(8,128)(2,1)S(1)}, bf16[2,4,8,1280]{3,2,1,0:T(8,128)(2,1)S(1)}, u32[]{:S(2)}, u32[]{:S(2)}) collective-permute-start(bf16[2,4,8,1280]{3,2,1,0:T(8,128)(2,1)S(1)} %get-tuple-element.39), channel_id=1, source_target_pairs={{0,16},{4,20},{8,24},{12,28},{16,0},{20,4},{24,8},{28,12},{1,17},{... | collective-permute-start | bytes 491528 | tf_op jit(solution)/shard_map/ppermute | solution.py:270
  16.1 0.3 collective-permute-done
  16.4 2.4 %collective-permute-start.9 = (bf16[2,4,8,1280]{3,2,1,0:T(8,128)(2,1)S(1)}, bf16[2,4,8,1280]{3,2,1,0:T(8,128)(2,1)S(1)}, u32[]{:S(2)}, u32[]{:S(2)}) collective-permute-start(bf16[2,4,8,1280]{3,2,1,0:T(8,128)(2,1)S(1)} %get-tuple-element.40), channel_id=1, source_target_pairs={{0,24},{4,28},{8,16},{12,20},{16,8},{20,12},{24,0},{28,4},{1,25},{... | collective-permute-start | bytes 491528 | tf_op jit(solution)/shard_map/ppermute | solution.py:270
  18.8 2.5 %collective-permute-done.1 = bf16[2,4,8,1280]{3,2,1,0:T(8,128)(2,1)S(1)} collective-permute-done((bf16[2,4,8,1280]{3,2,1,0:T(8,128)(2,1)S(1)}, bf16[2,4,8,1280]{3,2,1,0:T(8,128)(2,1)S(1)}, u32[]{:S(2)}, u32[]{:S(2)}) %collective-permute-start.1) | collective-permute-done | bytes 163872 | tf_op jit(solution)/shard_map/ppermute | solution.py:270
  21.3 0.6 %collective-permute-start.4 = (bf16[3,32,1280]{2,1,0:T(8,128)(2,1)S(1)}, bf16[3,32,1280]{2,1,0:T(8,128)(2,1)S(1)}, u32[]{:S(2)}, u32[]{:S(2)}) collective-permute-start(bf16[3,32,1280]{2,1,0:T(8,128)(2,1)S(1)} %join.2), channel_id=1, source_target_pairs={{0,4},{4,0},{8,12},{12,8},{16,20},{20,16},{24,28},{28,24},{1,5},{5... | collective-permute-start | bytes 737288 | tf_op jit(solution)/shard_map/ppermute | solution.py:270
  21.9 1.3 %collective-permute-done.7 = bf16[2,4,8,1280]{3,2,1,0:T(8,128)(2,1)S(1)} collective-permute-done((bf16[2,4,8,1280]{3,2,1,0:T(8,128)(2,1)S(1)}, bf16[2,4,8,1280]{3,2,1,0:T(8,128)(2,1)S(1)}, u32[]{:S(2)}, u32[]{:S(2)}) %collective-permute-start.7) | collective-permute-done | bytes 163872 | tf_op jit(solution)/shard_map/ppermute | solution.py:270
  23.2 3.0 %collective-permute-done.8 = bf16[2,4,8,1280]{3,2,1,0:T(8,128)(2,1)S(1)} collective-permute-done((bf16[2,4,8,1280]{3,2,1,0:T(8,128)(2,1)S(1)}, bf16[2,4,8,1280]{3,2,1,0:T(8,128)(2,1)S(1)}, u32[]{:S(2)}, u32[]{:S(2)}) %collective-permute-start.8) | collective-permute-done | bytes 163872 | tf_op jit(solution)/shard_map/ppermute | solution.py:270
  26.3 0.5 %collective-permute-start.10 = (bf16[32,1280]{1,0:T(8,128)(2,1)S(1)}, bf16[32,1280]{1,0:T(8,128)(2,1)S(1)}, u32[]{:S(2)}, u32[]{:S(2)}) collective-permute-start(bf16[32,1280]{1,0:T(8,128)(2,1)S(1)} %slice_bitcast_fusion), channel_id=1, source_target_pairs={{0,4},{4,0},{8,12},{12,8},{16,20},{20,16},{24,28},{28,24},{1,5},{5... | collective-permute-start | bytes 245768 | tf_op jit(solution)/shard_map/ppermute | solution.py:270
  27.0 3.5 %forward.1 = (bf16[256,1280]{1,0:T(8,128)(2,1)S(1)}, bf16[256,1280]{1,0:T(8,128)(2,1)S(1)}, f32[20,32,256]{2,1,0:T(8,128)S(1)}, bf16[256,1280]{1,0:T(8,128)(2,1)S(1)}) custom-call(s32[1]{0:T(128)} %bitcast.me_ref, bf16[2,256,256]{2,1,0:T(8,128)(2,1)S(1)} %order.1.order_ref, f32[3,1280]{1,0:T(4,128)S(1)} %copy-done.3, f32[1280]{0:T(1024)S(1)} %copy-done.4, ...), custom_call_target="tpu_custom_call" | custom-call | tf_op jit(solution)/shard_map/forward/pallas_call | solution.py:376
  30.5 1.0 %value.1.v_ref = bf16[256,1280]{1,0:T(8,128)(2,1)S(1)} custom-call(bf16[256,1280]{1,0:T(8,128)(2,1)S(1)} %get-tuple-element.33.hidden_ref, bf16[1280,1280]{1,0:T(8,128)(2,1)S(1)} %copy-done.2), custom_call_target="tpu_custom_call" | custom-call | tf_op jit(solution)/shard_map/value/pallas_call | solution.py:386
  31.5 5.1 %backward.1 = (bf16[32,1280]{1,0:T(8,128)(2,1)S(1)}, bf16[32,1280]{1,0:T(8,128)(2,1)S(1)}, bf16[32,1280]{1,0:T(8,128)(2,1)S(1)}, bf16[32,1280]{1,0:T(8,128)(2,1)...) custom-call(s32[1]{0:T(128)} %bitcast.me_ref, ...), custom_call_target="tpu_custom_call" | custom-call | tf_op jit(solution)/shard_map/backward/pallas_call | solution.py:394
  36.7 0.8 %collective-permute-start.17 = (bf16[32,1280]{1,0:T(8,128)(2,1)S(1)}, bf16[32,1280]{1,0:T(8,128)(2,1)S(1)}, u32[]{:S(2)}, u32[]{:S(2)}) collective-permute-start(bf16[32,1280]{1,0:T(8,128)(2,1)S(1)} %get-tuple-element.47), channel_id=1, source_target_pairs={{0,24},{4,28},{8,16},{12,20},{16,8},{20,12},{24,0},{28,4},{1,25},{... | collective-permute-start | bytes 245768 | tf_op jit(solution)/shard_map/ppermute | solution.py:270
  37.6 1.8 %collective-permute-start.18 = (bf16[32,1280]{1,0:T(8,128)(2,1)S(1)}, bf16[32,1280]{1,0:T(8,128)(2,1)S(1)}, u32[]{:S(2)}, u32[]{:S(2)}) collective-permute-start(bf16[32,1280]{1,0:T(8,128)(2,1)S(1)} %get-tuple-element.48), channel_id=1, source_target_pairs={{0,28},{4,24},{8,20},{12,16},{16,12},{20,8},{24,4},{28,0},{1,29},{... | collective-permute-start | bytes 245768 | tf_op jit(solution)/shard_map/ppermute | solution.py:270
  39.4 0.6 %collective-permute-start.12 = (bf16[32,1280]{1,0:T(8,128)(2,1)S(1)}, bf16[32,1280]{1,0:T(8,128)(2,1)S(1)}, u32[]{:S(2)}, u32[]{:S(2)}) collective-permute-start(bf16[32,1280]{1,0:T(8,128)(2,1)S(1)} %get-tuple-element.41), channel_id=1, source_target_pairs={{0,8},{4,12},{8,0},{12,4},{16,24},{20,28},{24,16},{28,20},{1,9},{5... | collective-permute-start | bytes 245768 | tf_op jit(solution)/shard_map/ppermute | solution.py:270
  40.0 1.1 %collective-permute-start.13 = (bf16[32,1280]{1,0:T(8,128)(2,1)S(1)}, bf16[32,1280]{1,0:T(8,128)(2,1)S(1)}, u32[]{:S(2)}, u32[]{:S(2)}) collective-permute-start(bf16[32,1280]{1,0:T(8,128)(2,1)S(1)} %get-tuple-element.42), channel_id=1, source_target_pairs={{0,12},{4,8},{8,4},{12,0},{16,28},{20,24},{24,20},{28,16},{1,13},{... | collective-permute-start | bytes 245768 | tf_op jit(solution)/shard_map/ppermute | solution.py:270
  41.1 1.0 %collective-permute-start.14 = (bf16[32,1280]{1,0:T(8,128)(2,1)S(1)}, bf16[32,1280]{1,0:T(8,128)(2,1)S(1)}, u32[]{:S(2)}, u32[]{:S(2)}) collective-permute-start(bf16[32,1280]{1,0:T(8,128)(2,1)S(1)} %get-tuple-element.43), channel_id=1, source_target_pairs={{0,16},{4,20},{8,24},{12,28},{16,0},{20,4},{24,8},{28,12},{1,17},{... | collective-permute-start | bytes 245768 | tf_op jit(solution)/shard_map/ppermute | solution.py:270
  42.1 0.8 %collective-permute-done.17 = bf16[32,1280]{1,0:T(8,128)(2,1)S(1)} collective-permute-done((bf16[32,1280]{1,0:T(8,128)(2,1)S(1)}, bf16[32,1280]{1,0:T(8,128)(2,1)S(1)}, u32[]{:S(2)}, u32[]{:S(2)}) %collective-permute-start.17) | collective-permute-done | bytes 81952 | tf_op jit(solution)/shard_map/ppermute | solution.py:270
  43.0 0.7 %collective-permute-done.18 = bf16[32,1280]{1,0:T(8,128)(2,1)S(1)} collective-permute-done((bf16[32,1280]{1,0:T(8,128)(2,1)S(1)}, bf16[32,1280]{1,0:T(8,128)(2,1)S(1)}, u32[]{:S(2)}, u32[]{:S(2)}) %collective-permute-start.18) | collective-permute-done | bytes 81952 | tf_op jit(solution)/shard_map/ppermute | solution.py:270
  43.6 0.8 %place.2.refs_4_ = bf16[4,8,8,1280]{3,2,1,0:T(8,128)(2,1)} custom-call(s32[1]{0:T(128)} %bitcast.me_ref, bf16[4,8,1280]{2,1,0:T(8,128)(2,1)S(1)} %bitcast.38, bf16[4,8,1280]{2,1,0:T(8,128)(2,1)S(1)} %bitcast.41, bf16[4,8,1280]{2,1,0:T(8,128)(2,1)S(1)} %bitcast.43, bf16[4,8,1280]{2,1,0:T(8,128)(2,1)S(1)} %bitcast.44), custom_call_target="tpu_custom_call" | custom-call | tf_op jit(solution)/shard_map/place/pallas_call | solution.py:413
  44.4 1.6 %collective-permute-done.12 = bf16[32,1280]{1,0:T(8,128)(2,1)S(1)} collective-permute-done((bf16[32,1280]{1,0:T(8,128)(2,1)S(1)}, bf16[32,1280]{1,0:T(8,128)(2,1)S(1)}, u32[]{:S(2)}, u32[]{:S(2)}) %collective-permute-start.12) | collective-permute-done | bytes 81952 | tf_op jit(solution)/shard_map/ppermute | solution.py:270
  46.0 0.7 %collective-permute-done.13 = bf16[32,1280]{1,0:T(8,128)(2,1)S(1)} collective-permute-done((bf16[32,1280]{1,0:T(8,128)(2,1)S(1)}, bf16[32,1280]{1,0:T(8,128)(2,1)S(1)}, u32[]{:S(2)}, u32[]{:S(2)}) %collective-permute-start.13) | collective-permute-done | bytes 81952 | tf_op jit(solution)/shard_map/ppermute | solution.py:270
  46.7 1.0 %collective-permute-done.15 = bf16[32,1280]{1,0:T(8,128)(2,1)S(1)} collective-permute-done((bf16[32,1280]{1,0:T(8,128)(2,1)S(1)}, bf16[32,1280]{1,0:T(8,128)(2,1)S(1)}, u32[]{:S(2)}, u32[]{:S(2)}) %collective-permute-start.15) | collective-permute-done | bytes 81952 | tf_op jit(solution)/shard_map/ppermute | solution.py:270
  47.7 0.8 %place.3 = bf16[4,8,8,1280]{3,2,1,0:T(8,128)(2,1)} custom-call(s32[1]{0:T(128)} %bitcast.me_ref, bf16[4,8,1280]{2,1,0:T(8,128)(2,1)S(1)} %bitcast.39, bf16[4,8,1280]{2,1,0:T(8,128)(2,1)S(1)} %bitcast.40, bf16[4,8,1280]{2,1,0:T(8,128)(2,1)S(1)} %bitcast.42, bf16[4,8,1280]{2,1,0:T(8,128)(2,1)S(1)} %bitcast.45, ...), custom_call_target="tpu_custom_call", output_to_operand_aliasing={{}: (5, {})} | custom-call | tf_op jit(solution)/shard_map/place/pallas_call | solution.py:413
  (29 shorter events, 0.4 us)
Async XLA Ops:
  1.6 4.7 %collective-permute-start.5 = (f32[4,128]{1,0:T(4,128)S(1)}, f32[4,128]{1,0:T(4,128)S(1)}, u32[]{:S(2)}, u32[]{:S(2)}) collective-permute-start(f32[4,128]{1,0:T(4,128)S(1)} %get-tuple-element.36), channel_id=1, source_target_pairs={{0,1},{1,0},{2,3},{3,2},{4,5},{5,4},{6,7},{7,6},{8,9},{9,8},{10,11... | collective-permute-start | bytes 6152 | tf_op jit(solution)/shard_map/ppermute | solution.py:270
  6.3 6.5 %collective-permute-start.6 = (f32[4,128]{1,0:T(4,128)S(1)}, f32[4,128]{1,0:T(4,128)S(1)}, u32[]{:S(2)}, u32[]{:S(2)}) collective-permute-start(f32[4,128]{1,0:T(4,128)S(1)} %add.3.refs_0_), channel_id=1, source_target_pairs={{0,2},{1,3},{2,0},{3,1},{4,6},{5,7},{6,4},{7,5},{8,10},{9,11},{10,... | collective-permute-start | bytes 6152 | tf_op jit(solution)/shard_map/ppermute | solution.py:270
  9.3 7.1 %collective-permute-start = (bf16[2,4,8,1280]{3,2,1,0:T(8,128)(2,1)S(1)}, bf16[2,4,8,1280]{3,2,1,0:T(8,128)(2,1)S(1)}, u32[]{:S(2)}, u32[]{:S(2)}) collective-permute-start(bf16[2,4,8,1280]{3,2,1,0:T(8,128)(2,1)S(1)} %get-tuple-element.28), channel_id=1, source_target_pairs={{0,8},{4,12},{8,0},{12,4},{16,24},{20,28},{24,16},{28,20},{1,9},{5... | collective-permute-start | bytes 491528 | tf_op jit(solution)/shard_map/ppermute | solution.py:270
  10.8 10.5 %collective-permute-start.1 = (bf16[2,4,8,1280]{3,2,1,0:T(8,128)(2,1)S(1)}, bf16[2,4,8,1280]{3,2,1,0:T(8,128)(2,1)S(1)}, u32[]{:S(2)}, u32[]{:S(2)}) collective-permute-start(bf16[2,4,8,1280]{3,2,1,0:T(8,128)(2,1)S(1)} %get-tuple-element.29), channel_id=1, source_target_pairs={{0,16},{4,20},{8,24},{12,28},{16,0},{20,4},{24,8},{28,12},{1,17},{... | collective-permute-start | bytes 491528 | tf_op jit(solution)/shard_map/ppermute | solution.py:270
  12.3 9.0 %collective-permute-start.2 = (bf16[2,4,8,1280]{3,2,1,0:T(8,128)(2,1)S(1)}, bf16[2,4,8,1280]{3,2,1,0:T(8,128)(2,1)S(1)}, u32[]{:S(2)}, u32[]{:S(2)}) collective-permute-start(bf16[2,4,8,1280]{3,2,1,0:T(8,128)(2,1)S(1)} %get-tuple-element.30), channel_id=1, source_target_pairs={{0,24},{4,28},{8,16},{12,20},{16,8},{20,12},{24,0},{28,4},{1,25},{... | collective-permute-start | bytes 491528 | tf_op jit(solution)/shard_map/ppermute | solution.py:270
  12.8 14.1 %copy-start = (bf16[1280,1280]{1,0:T(8,128)(2,1)S(1)}, bf16[1280,1280]{1,0:T(8,128)(2,1)}, u32[]{:S(2)}) copy-start(bf16[1280,1280]{1,0:T(8,128)(2,1)} %wq_ref.3) | copy-start | bytes 9830404
  12.8 14.1 %copy-start.1 = (bf16[1280,1280]{1,0:T(8,128)(2,1)S(1)}, bf16[1280,1280]{1,0:T(8,128)(2,1)}, u32[]{:S(2)}) copy-start(bf16[1280,1280]{1,0:T(8,128)(2,1)} %wk_ref.3) | copy-start | bytes 9830404
  12.8 14.2 %copy-start.3 = (f32[3,1280]{1,0:T(4,128)S(1)}, f32[3,1280]{1,0:T(4,128)}, u32[]{:S(2)}) copy-start(f32[3,1280]{1,0:T(4,128)} %taps_ref.3) | copy-start | bytes 46084
  12.8 14.2 %copy-start.4 = (f32[1280]{0:T(1024)S(1)}, f32[1280]{0:T(1024)}, u32[]{:S(2)}) copy-start(f32[1280]{0:T(1024)} %bias_ref.1) | copy-start | bytes 15364
  13.0 10.2 %collective-permute-start.7 = (bf16[2,4,8,1280]{3,2,1,0:T(8,128)(2,1)S(1)}, bf16[2,4,8,1280]{3,2,1,0:T(8,128)(2,1)S(1)}, u32[]{:S(2)}, u32[]{:S(2)}) collective-permute-start(bf16[2,4,8,1280]{3,2,1,0:T(8,128)(2,1)S(1)} %get-tuple-element.38), channel_id=1, source_target_pairs={{0,8},{4,12},{8,0},{12,4},{16,24},{20,28},{24,16},{28,20},{1,9},{5... | collective-permute-start | bytes 491528 | tf_op jit(solution)/shard_map/ppermute | solution.py:270
  14.6 11.7 %collective-permute-start.8 = (bf16[2,4,8,1280]{3,2,1,0:T(8,128)(2,1)S(1)}, bf16[2,4,8,1280]{3,2,1,0:T(8,128)(2,1)S(1)}, u32[]{:S(2)}, u32[]{:S(2)}) collective-permute-start(bf16[2,4,8,1280]{3,2,1,0:T(8,128)(2,1)S(1)} %get-tuple-element.39), channel_id=1, source_target_pairs={{0,16},{4,20},{8,24},{12,28},{16,0},{20,4},{24,8},{28,12},{1,17},{... | collective-permute-start | bytes 491528 | tf_op jit(solution)/shard_map/ppermute | solution.py:270
  16.4 9.8 %collective-permute-start.9 = (bf16[2,4,8,1280]{3,2,1,0:T(8,128)(2,1)S(1)}, bf16[2,4,8,1280]{3,2,1,0:T(8,128)(2,1)S(1)}, u32[]{:S(2)}, u32[]{:S(2)}) collective-permute-start(bf16[2,4,8,1280]{3,2,1,0:T(8,128)(2,1)S(1)} %get-tuple-element.40), channel_id=1, source_target_pairs={{0,24},{4,28},{8,16},{12,20},{16,8},{20,12},{24,0},{28,4},{1,25},{... | collective-permute-start | bytes 491528 | tf_op jit(solution)/shard_map/ppermute | solution.py:270
  21.3 5.6 %collective-permute-start.3 = (bf16[32,1280]{1,0:T(8,128)(2,1)S(1)}, bf16[32,1280]{1,0:T(8,128)(2,1)S(1)}, u32[]{:S(2)}, u32[]{:S(2)}) collective-permute-start(bf16[32,1280]{1,0:T(8,128)(2,1)S(1)} %slice_bitcast_fusion.1), channel_id=1, source_target_pairs={{0,4},{4,0},{8,12},{12,8},{16,20},{20,16},{24,28},{28,24},{1,5},{5... | collective-permute-start | bytes 245768 | tf_op jit(solution)/shard_map/ppermute | solution.py:270
  21.3 5.6 %collective-permute-start.4 = (bf16[3,32,1280]{2,1,0:T(8,128)(2,1)S(1)}, bf16[3,32,1280]{2,1,0:T(8,128)(2,1)S(1)}, u32[]{:S(2)}, u32[]{:S(2)}) collective-permute-start(bf16[3,32,1280]{2,1,0:T(8,128)(2,1)S(1)} %join.2), channel_id=1, source_target_pairs={{0,4},{4,0},{8,12},{12,8},{16,20},{20,16},{24,28},{28,24},{1,5},{5... | collective-permute-start | bytes 737288 | tf_op jit(solution)/shard_map/ppermute | solution.py:270
  26.2 5.3 %collective-permute-start.11 = (bf16[3,32,1280]{2,1,0:T(8,128)(2,1)S(1)}, bf16[3,32,1280]{2,1,0:T(8,128)(2,1)S(1)}, u32[]{:S(2)}, u32[]{:S(2)}) collective-permute-start(bf16[3,32,1280]{2,1,0:T(8,128)(2,1)S(1)} %join.3), channel_id=1, source_target_pairs={{0,4},{4,0},{8,12},{12,8},{16,20},{20,16},{24,28},{28,24},{1,5},{5... | collective-permute-start | bytes 737288 | tf_op jit(solution)/shard_map/ppermute | solution.py:270
  26.3 5.2 %collective-permute-start.10 = (bf16[32,1280]{1,0:T(8,128)(2,1)S(1)}, bf16[32,1280]{1,0:T(8,128)(2,1)S(1)}, u32[]{:S(2)}, u32[]{:S(2)}) collective-permute-start(bf16[32,1280]{1,0:T(8,128)(2,1)S(1)} %slice_bitcast_fusion), channel_id=1, source_target_pairs={{0,4},{4,0},{8,12},{12,8},{16,20},{20,16},{24,28},{28,24},{1,5},{5... | collective-permute-start | bytes 245768 | tf_op jit(solution)/shard_map/ppermute | solution.py:270
  27.0 3.5 %copy-start.2 = (bf16[1280,1280]{1,0:T(8,128)(2,1)S(1)}, bf16[1280,1280]{1,0:T(8,128)(2,1)}, u32[]{:S(2)}) copy-start(bf16[1280,1280]{1,0:T(8,128)(2,1)} %wv_ref.3) | copy-start | bytes 9830404
  36.6 4.5 %collective-permute-start.16 = (bf16[32,1280]{1,0:T(8,128)(2,1)S(1)}, bf16[32,1280]{1,0:T(8,128)(2,1)S(1)}, u32[]{:S(2)}, u32[]{:S(2)}) collective-permute-start(bf16[32,1280]{1,0:T(8,128)(2,1)S(1)} %get-tuple-element.46), channel_id=1, source_target_pairs={{0,4},{4,0},{8,12},{12,8},{16,20},{20,16},{24,28},{28,24},{1,5},{5... | collective-permute-start | bytes 245768 | tf_op jit(solution)/shard_map/ppermute | solution.py:270
  36.7 6.2 %collective-permute-start.17 = (bf16[32,1280]{1,0:T(8,128)(2,1)S(1)}, bf16[32,1280]{1,0:T(8,128)(2,1)S(1)}, u32[]{:S(2)}, u32[]{:S(2)}) collective-permute-start(bf16[32,1280]{1,0:T(8,128)(2,1)S(1)} %get-tuple-element.47), channel_id=1, source_target_pairs={{0,24},{4,28},{8,16},{12,20},{16,8},{20,12},{24,0},{28,4},{1,25},{... | collective-permute-start | bytes 245768 | tf_op jit(solution)/shard_map/ppermute | solution.py:270
  37.6 6.0 %collective-permute-start.18 = (bf16[32,1280]{1,0:T(8,128)(2,1)S(1)}, bf16[32,1280]{1,0:T(8,128)(2,1)S(1)}, u32[]{:S(2)}, u32[]{:S(2)}) collective-permute-start(bf16[32,1280]{1,0:T(8,128)(2,1)S(1)} %get-tuple-element.48), channel_id=1, source_target_pairs={{0,28},{4,24},{8,20},{12,16},{16,12},{20,8},{24,4},{28,0},{1,29},{... | collective-permute-start | bytes 245768 | tf_op jit(solution)/shard_map/ppermute | solution.py:270
  39.4 6.6 %collective-permute-start.12 = (bf16[32,1280]{1,0:T(8,128)(2,1)S(1)}, bf16[32,1280]{1,0:T(8,128)(2,1)S(1)}, u32[]{:S(2)}, u32[]{:S(2)}) collective-permute-start(bf16[32,1280]{1,0:T(8,128)(2,1)S(1)} %get-tuple-element.41), channel_id=1, source_target_pairs={{0,8},{4,12},{8,0},{12,4},{16,24},{20,28},{24,16},{28,20},{1,9},{5... | collective-permute-start | bytes 245768 | tf_op jit(solution)/shard_map/ppermute | solution.py:270
  40.0 6.6 %collective-permute-start.13 = (bf16[32,1280]{1,0:T(8,128)(2,1)S(1)}, bf16[32,1280]{1,0:T(8,128)(2,1)S(1)}, u32[]{:S(2)}, u32[]{:S(2)}) collective-permute-start(bf16[32,1280]{1,0:T(8,128)(2,1)S(1)} %get-tuple-element.42), channel_id=1, source_target_pairs={{0,12},{4,8},{8,4},{12,0},{16,28},{20,24},{24,20},{28,16},{1,13},{... | collective-permute-start | bytes 245768 | tf_op jit(solution)/shard_map/ppermute | solution.py:270
  41.1 5.5 %collective-permute-start.14 = (bf16[32,1280]{1,0:T(8,128)(2,1)S(1)}, bf16[32,1280]{1,0:T(8,128)(2,1)S(1)}, u32[]{:S(2)}, u32[]{:S(2)}) collective-permute-start(bf16[32,1280]{1,0:T(8,128)(2,1)S(1)} %get-tuple-element.43), channel_id=1, source_target_pairs={{0,16},{4,20},{8,24},{12,28},{16,0},{20,4},{24,8},{28,12},{1,17},{... | collective-permute-start | bytes 245768 | tf_op jit(solution)/shard_map/ppermute | solution.py:270
  42.9 4.7 %collective-permute-start.15 = (bf16[32,1280]{1,0:T(8,128)(2,1)S(1)}, bf16[32,1280]{1,0:T(8,128)(2,1)S(1)}, u32[]{:S(2)}, u32[]{:S(2)}) collective-permute-start(bf16[32,1280]{1,0:T(8,128)(2,1)S(1)} %get-tuple-element.44), channel_id=1, source_target_pairs={{0,20},{4,16},{8,28},{12,24},{16,4},{20,0},{24,12},{28,8},{1,21},{... | collective-permute-start | bytes 245768 | tf_op jit(solution)/shard_map/ppermute | solution.py:270

commit v6 on v5

--- a/solution.py
+++ b/solution.py
@@ -52,25 +52,28 @@
     return jnp.concatenate([kept * mask for mask in token_masks], axis=0)
 
 
+def pieces(tokens_ref, outs, me, masks, sems):
+    return [
+        pltpu.make_async_copy(
+            tokens_ref.at[:, me ^ mask], outs[index // 2].at[mask % 2], sems.at[index]
+        )
+        for index, mask in enumerate(masks)
+    ]
+
+
 def pack_kernel(me_ref, tokens_ref, cotangent_ref, *refs, peers):
-    outs = refs[:peers // 2]
-    energy_ref, held_ref, sems = refs[peers // 2:]
-    me = me_ref[0]
+    outs = refs[:peers // 2 - 1]
+    energy_ref, held_ref, sems = refs[peers // 2 - 1:]
     frame_rows = held_ref.shape[0]
-    frame_copies = [
+    held = [
         pltpu.make_async_copy(cotangent_ref.at[frame], held_ref.at[frame], sems.at[peers + frame])
         for frame in range(frame_rows)
     ]
-    copies = [
-        pltpu.make_async_copy(
-            tokens_ref.at[:, me ^ mask], outs[mask // 2].at[mask % 2], sems.at[mask]
-        )
-        for mask in range(peers)
-    ]
-    for copy in frame_copies + copies:
+    copies = pieces(tokens_ref, outs, me_ref[0], range(2, peers), sems)
+    for copy in held + copies:
         copy.start()
     for frame in range(frame_rows):
-        frame_copies[frame].wait()
+        held[frame].wait()
         total = jnp.zeros(held_ref.shape[2:], jnp.float32)
         for group in range(peers):
             grad = held_ref[frame, group].astype(jnp.float32)
@@ -78,6 +81,16 @@
         energy_ref[frame:frame + 1, :] = jnp.broadcast_to(
             jnp.sum(total, keepdims=True), (1, LANES)
         )
+    for copy in copies:
+        copy.wait()
+
+
+def prepare_kernel(me_ref, tokens_ref, sent_ref, order_ref, sems, *, frames, toks):
+    copies = pieces(tokens_ref, [sent_ref], me_ref[0], range(2), sems)
+    for copy in copies:
+        copy.start()
+    order_ref[0] = reorder_matrix(frames, toks, True)
+    order_ref[1] = reorder_matrix(frames, toks, False)
     for copy in copies:
         copy.wait()
 
@@ -118,11 +131,6 @@
     if mask % 2 == 0:
         return blocks[chip][0]
     return blocks[-1][chip - 1] if chip else blocks[-2][...]
-
-
-def order_kernel(order_ref, *, frames, toks):
-    order_ref[0] = reorder_matrix(frames, toks, True)
-    order_ref[1] = reorder_matrix(frames, toks, False)
 
 
 def forward_kernel(me_ref, order_ref, taps_ref, bias_ref, wq_ref, wk_ref, *refs,
@@ -247,9 +255,10 @@
         if 0 <= index - 2:
             contract(wides.pop(index - 2), *places[index - 2])
 
-    total = sum(
-        lax.dot_general(weight_ref[...], left_ref[index], NT, preferred_element_type=jnp.float32)
-        for index, weight_ref in enumerate((wq_ref, wk_ref, wv_ref))
+    total = lax.dot_general(
+        jnp.concatenate([wq_ref[...], wk_ref[...], wv_ref[...]], axis=1),
+        jnp.concatenate([left_ref[0], left_ref[1], left_ref[2]], axis=1),
+        NT, preferred_element_type=jnp.float32,
     ).astype(jnp.bfloat16)
     for col in range(0, channels, BLOCK):
         cols = slice(col, col + BLOCK)
@@ -341,18 +350,30 @@
     sent_shape = low((2, frame_rows, toks, channels))
     split = (frame_rows, peers, toks, channels)
 
+    tokens, cotangent = (off_chip(array.reshape(split)) for array in (tokens, cotangent))
     *sent_tokens, energy, held = pl.pallas_call(
         functools.partial(pack_kernel, peers=peers),
         in_specs=[smem, hbm, hbm],
-        out_specs=[vmem] * (peers // 2 + 2),
-        out_shape=[sent_shape] * (peers // 2)
+        out_specs=[vmem] * (peers // 2 + 1),
+        out_shape=[sent_shape] * (peers // 2 - 1)
         + [pltpu.VMEM((frame_rows, LANES), jnp.float32), low(split)],
         scratch_shapes=[pltpu.SemaphoreType.DMA((peers + frame_rows,))],
         compiler_params=grant(8),
         name="pack",
-    )(me_arg, off_chip(tokens.reshape(split)), off_chip(cotangent.reshape(split)))
+    )(me_arg, tokens, cotangent)
+    sent_here, order = pl.pallas_call(
+        functools.partial(prepare_kernel, frames=frames, toks=toks),
+        in_specs=[smem, hbm],
+        out_specs=[vmem] * 2,
+        out_shape=[sent_shape, low((2, rows, rows))],
+        scratch_shapes=[pltpu.SemaphoreType.DMA((2,))],
+        compiler_params=grant(4),
+        name="prepare",
+    )(me_arg, tokens)
+    order = on_chip(order)
+    sent_tokens = [sent_here, *sent_tokens]
+    terms = tile_terms(energy)
     token_blocks = gather_tokens(sent_tokens)
-    terms = tile_terms(energy)
     sent_grads = pl.pallas_call(
         functools.partial(scale_kernel, peers=peers, count=spatial_all * channels),
         in_specs=[smem] + [vmem] * (1 + len(terms)),
@@ -366,13 +387,6 @@
 
     weights = (w_query, w_key, w_value)
     sizes = dict(frames=frames, toks=toks, peers=peers)
-    order = on_chip(pl.pallas_call(
-        functools.partial(order_kernel, frames=frames, toks=toks),
-        out_specs=vmem,
-        out_shape=low((2, rows, rows)),
-        compiler_params=grant(4),
-        name="order",
-    )())
     query, key, prob, hidden = pl.pallas_call(
         functools.partial(forward_kernel, **sizes),
         in_specs=[smem] + [vmem] * (7 + peers // 2),

time: 48.6 us -> 48.5 us (level)
  starting transfers between devices: 21.9 us -> 20.7 us
  Pallas kernels: 12.9 us -> 13.7 us
    ppermute x19, starting transfers between devices: 21.9 us -> 20.7 us  [swap(): lax.ppermute(value, axis, [(i, i ^ mask) for i in range(lax.axis_size(axi...]
    pallas_call x1, Pallas kernels: 0.09 us -> 0.94 us  [body(): pl.pallas_call(functools.partial(prepare_kernel, frames=frames, toks=toks...]
  transfers between devices with their start and end apart: 19 -> 19, of which waited for: 10 -> 10; matrix products, arithmetic and copies ran while one was open for 0% -> 0% of each run, Pallas kernels for 11% -> 13%
where the time goes in v6:
time: 48.5 us; the launch traced here: 48.3 us
  starting transfers between devices  20.7 us (43%)
  Pallas kernels  13.7 us (28%)
  waiting for transfers between devices  13.6 us (28%)
    ppermute x19, starting transfers between devices, swap(): lax.ppermute(value, axis, [(i, i ^ mask) for i in range(lax.axis_size(axi...  20.7 us
    ppermute x19, waiting for transfers between devices, swap(): lax.ppermute(value, axis, [(i, i ^ mask) for i in range(lax.axis_size(axi...  13.6 us
    pallas_call x1, Pallas kernels, body(): pl.pallas_call(functools.partial(backward_kernel, **sizes), in_specs=[sme...  5.05 us
    pallas_call x1, Pallas kernels, body(): pl.pallas_call(functools.partial(forward_kernel, **sizes), in_specs=[smem...  3.46 us
    pallas_call x1, Pallas kernels, body(): pl.pallas_call(functools.partial(pack_kernel, peers=peers), in_specs=[sme...  1.58 us
    pallas_call x2, Pallas kernels, body(): pl.pallas_call(functools.partial(place_kernel, masks=masks), in_specs=[sm...  1.5 us
    pallas_call x1, Pallas kernels, body(): pl.pallas_call(value_kernel, in_specs=[vmem] * 2, out_specs=vmem, out_sha...  1.02 us
  transfers between devices with their start and end apart: 19, of which 10 were waited for; matrix products, arithmetic and copies ran while one was open for 0% of the time, Pallas kernels for 13%

profile of v6, /device:TPU:0, one launch (start us, length us, event | category | flops | bytes accessed | tf_op | source)
XLA Modules:
  0.0 48.3 jit_solution(4657615070364227844)
XLA Ops:
  0.0 1.6 %pack.1 = (bf16[2,4,8,1280]{3,2,1,0:T(8,128)(2,1)S(1)}, bf16[2,4,8,1280]{3,2,1,0:T(8,128)(2,1)S(1)}, bf16[2,4,8,1280]{3,2,1,0:T(8,128)(2,1)S(1)}, f32[4,128]{1,0:T(4,128)S(1)}, bf16[4,8,8,1280]{3,2,1,0:T(8,128)(2,1)S(1)}) custom-call(s32[1]{0:T(128)} %bitcast.me_ref, bf16[4,8,8,1280]{3,2,1,0:T(8,128)(2,1)} %bitcast.46, bf16[4,8,8,1280]{3,2,1,0:T(8,128)(2,1)} %bitcast.48), custom_call_target="tpu_custom_call" | custom-call | tf_op jit(solution)/shard_map/pack/pallas_call | solution.py:354
  1.6 3.1 %collective-permute-start.5 = (f32[4,128]{1,0:T(4,128)S(1)}, f32[4,128]{1,0:T(4,128)S(1)}, u32[]{:S(2)}, u32[]{:S(2)}) collective-permute-start(f32[4,128]{1,0:T(4,128)S(1)} %get-tuple-element.38), channel_id=1, source_target_pairs={{0,1},{1,0},{2,3},{3,2},{4,5},{5,4},{6,7},{7,6},{8,9},{9,8},{10,11... | collective-permute-start | bytes 6152 | tf_op jit(solution)/shard_map/ppermute | solution.py:279
  4.7 1.6 %collective-permute-done.5 = f32[4,128]{1,0:T(4,128)S(1)} collective-permute-done((f32[4,128]{1,0:T(4,128)S(1)}, f32[4,128]{1,0:T(4,128)S(1)}, u32[]{:S(2)}, u32[]{:S(2)}) %collective-permute-start.5) | collective-permute-done | bytes 2080 | tf_op jit(solution)/shard_map/ppermute | solution.py:279
  6.3 3.0 %collective-permute-start.6 = (f32[4,128]{1,0:T(4,128)S(1)}, f32[4,128]{1,0:T(4,128)S(1)}, u32[]{:S(2)}, u32[]{:S(2)}) collective-permute-start(f32[4,128]{1,0:T(4,128)S(1)} %add.3.refs_0_), channel_id=1, source_target_pairs={{0,2},{1,3},{2,0},{3,1},{4,6},{5,7},{6,4},{7,5},{8,10},{9,11},{10,... | collective-permute-start | bytes 6152 | tf_op jit(solution)/shard_map/ppermute | solution.py:279
  9.3 1.5 %collective-permute-start = (bf16[2,4,8,1280]{3,2,1,0:T(8,128)(2,1)S(1)}, bf16[2,4,8,1280]{3,2,1,0:T(8,128)(2,1)S(1)}, u32[]{:S(2)}, u32[]{:S(2)}) collective-permute-start(bf16[2,4,8,1280]{3,2,1,0:T(8,128)(2,1)S(1)} %get-tuple-element.30), channel_id=1, source_target_pairs={{0,8},{4,12},{8,0},{12,4},{16,24},{20,28},{24,16},{28,20},{1,9},{5... | collective-permute-start | bytes 491528 | tf_op jit(solution)/shard_map/ppermute | solution.py:279
  10.8 1.5 %collective-permute-start.1 = (bf16[2,4,8,1280]{3,2,1,0:T(8,128)(2,1)S(1)}, bf16[2,4,8,1280]{3,2,1,0:T(8,128)(2,1)S(1)}, u32[]{:S(2)}, u32[]{:S(2)}) collective-permute-start(bf16[2,4,8,1280]{3,2,1,0:T(8,128)(2,1)S(1)} %get-tuple-element.31), channel_id=1, source_target_pairs={{0,16},{4,20},{8,24},{12,28},{16,0},{20,4},{24,8},{28,12},{1,17},{... | collective-permute-start | bytes 491528 | tf_op jit(solution)/shard_map/ppermute | solution.py:279
  12.3 0.5 collective-permute-start.2
  12.8 0.9 %prepare.1 = (bf16[2,4,8,1280]{3,2,1,0:T(8,128)(2,1)S(1)}, bf16[2,256,256]{2,1,0:T(8,128)(2,1)S(1)}) custom-call(s32[1]{0:T(128)} %bitcast.me_ref, bf16[4,8,8,1280]{3,2,1,0:T(8,128)(2,1)} %bitcast.47), custom_call_target="tpu_custom_call" | custom-call | tf_op jit(solution)/shard_map/prepare/pallas_call | solution.py:364
  13.8 0.2 scale.1
  14.0 1.6 %collective-permute-start.7 = (bf16[2,4,8,1280]{3,2,1,0:T(8,128)(2,1)S(1)}, bf16[2,4,8,1280]{3,2,1,0:T(8,128)(2,1)S(1)}, u32[]{:S(2)}, u32[]{:S(2)}) collective-permute-start(bf16[2,4,8,1280]{3,2,1,0:T(8,128)(2,1)S(1)} %get-tuple-element.40), channel_id=1, source_target_pairs={{0,8},{4,12},{8,0},{12,4},{16,24},{20,28},{24,16},{28,20},{1,9},{5... | collective-permute-start | bytes 491528 | tf_op jit(solution)/shard_map/ppermute | solution.py:279
  15.5 1.5 %collective-permute-start.8 = (bf16[2,4,8,1280]{3,2,1,0:T(8,128)(2,1)S(1)}, bf16[2,4,8,1280]{3,2,1,0:T(8,128)(2,1)S(1)}, u32[]{:S(2)}, u32[]{:S(2)}) collective-permute-start(bf16[2,4,8,1280]{3,2,1,0:T(8,128)(2,1)S(1)} %get-tuple-element.41), channel_id=1, source_target_pairs={{0,16},{4,20},{8,24},{12,28},{16,0},{20,4},{24,8},{28,12},{1,17},{... | collective-permute-start | bytes 491528 | tf_op jit(solution)/shard_map/ppermute | solution.py:279
  17.1 1.8 %collective-permute-start.9 = (bf16[2,4,8,1280]{3,2,1,0:T(8,128)(2,1)S(1)}, bf16[2,4,8,1280]{3,2,1,0:T(8,128)(2,1)S(1)}, u32[]{:S(2)}, u32[]{:S(2)}) collective-permute-start(bf16[2,4,8,1280]{3,2,1,0:T(8,128)(2,1)S(1)} %get-tuple-element.42), channel_id=1, source_target_pairs={{0,24},{4,28},{8,16},{12,20},{16,8},{20,12},{24,0},{28,4},{1,25},{... | collective-permute-start | bytes 491528 | tf_op jit(solution)/shard_map/ppermute | solution.py:279
  18.8 1.2 %collective-permute-done.1 = bf16[2,4,8,1280]{3,2,1,0:T(8,128)(2,1)S(1)} collective-permute-done((bf16[2,4,8,1280]{3,2,1,0:T(8,128)(2,1)S(1)}, bf16[2,4,8,1280]{3,2,1,0:T(8,128)(2,1)S(1)}, u32[]{:S(2)}, u32[]{:S(2)}) %collective-permute-start.1) | collective-permute-done | bytes 163872 | tf_op jit(solution)/shard_map/ppermute | solution.py:279
  20.0 0.9 %collective-permute-done.2 = bf16[2,4,8,1280]{3,2,1,0:T(8,128)(2,1)S(1)} collective-permute-done((bf16[2,4,8,1280]{3,2,1,0:T(8,128)(2,1)S(1)}, bf16[2,4,8,1280]{3,2,1,0:T(8,128)(2,1)S(1)}, u32[]{:S(2)}, u32[]{:S(2)}) %collective-permute-start.2) | collective-permute-done | bytes 163872 | tf_op jit(solution)/shard_map/ppermute | solution.py:279
  21.0 2.2 %collective-permute-done.7 = bf16[2,4,8,1280]{3,2,1,0:T(8,128)(2,1)S(1)} collective-permute-done((bf16[2,4,8,1280]{3,2,1,0:T(8,128)(2,1)S(1)}, bf16[2,4,8,1280]{3,2,1,0:T(8,128)(2,1)S(1)}, u32[]{:S(2)}, u32[]{:S(2)}) %collective-permute-start.7) | collective-permute-done | bytes 163872 | tf_op jit(solution)/shard_map/ppermute | solution.py:279
  23.2 3.0 %collective-permute-done.8 = bf16[2,4,8,1280]{3,2,1,0:T(8,128)(2,1)S(1)} collective-permute-done((bf16[2,4,8,1280]{3,2,1,0:T(8,128)(2,1)S(1)}, bf16[2,4,8,1280]{3,2,1,0:T(8,128)(2,1)S(1)}, u32[]{:S(2)}, u32[]{:S(2)}) %collective-permute-start.8) | collective-permute-done | bytes 163872 | tf_op jit(solution)/shard_map/ppermute | solution.py:279
  26.3 0.5 %collective-permute-start.10 = (bf16[32,1280]{1,0:T(8,128)(2,1)S(1)}, bf16[32,1280]{1,0:T(8,128)(2,1)S(1)}, u32[]{:S(2)}, u32[]{:S(2)}) collective-permute-start(bf16[32,1280]{1,0:T(8,128)(2,1)S(1)} %slice_bitcast_fusion), channel_id=1, source_target_pairs={{0,4},{4,0},{8,12},{12,8},{16,20},{20,16},{24,28},{28,24},{1,5},{5... | collective-permute-start | bytes 245768 | tf_op jit(solution)/shard_map/ppermute | solution.py:279
  26.9 3.5 %forward.1 = (bf16[256,1280]{1,0:T(8,128)(2,1)S(1)}, bf16[256,1280]{1,0:T(8,128)(2,1)S(1)}, f32[20,32,256]{2,1,0:T(8,128)S(1)}, bf16[256,1280]{1,0:T(8,128)(2,1)S(1)}) custom-call(s32[1]{0:T(128)} %bitcast.me_ref, bf16[2,256,256]{2,1,0:T(8,128)(2,1)S(1)} %get-tuple-element.28.order_ref, f32[3,1280]{1,0:T(4,128)S(1)} %copy-done.3, f32[1280]{0:T(1024)S(1)} %copy-done.4, ...), custom_call_target="tpu_custom_call" | custom-call | tf_op jit(solution)/shard_map/forward/pallas_call | solution.py:390
  30.4 1.0 %value.1.v_ref = bf16[256,1280]{1,0:T(8,128)(2,1)S(1)} custom-call(bf16[256,1280]{1,0:T(8,128)(2,1)S(1)} %get-tuple-element.35.hidden_ref, bf16[1280,1280]{1,0:T(8,128)(2,1)S(1)} %copy-done.2), custom_call_target="tpu_custom_call" | custom-call | tf_op jit(solution)/shard_map/value/pallas_call | solution.py:400
  31.4 5.1 %backward.1 = (bf16[32,1280]{1,0:T(8,128)(2,1)S(1)}, bf16[32,1280]{1,0:T(8,128)(2,1)S(1)}, bf16[32,1280]{1,0:T(8,128)(2,1)S(1)}, bf16[32,1280]{1,0:T(8,128)(2,1)...) custom-call(s32[1]{0:T(128)} %bitcast.me_ref, ...), custom_call_target="tpu_custom_call" | custom-call | tf_op jit(solution)/shard_map/backward/pallas_call | solution.py:408
  36.6 0.8 %collective-permute-start.17 = (bf16[32,1280]{1,0:T(8,128)(2,1)S(1)}, bf16[32,1280]{1,0:T(8,128)(2,1)S(1)}, u32[]{:S(2)}, u32[]{:S(2)}) collective-permute-start(bf16[32,1280]{1,0:T(8,128)(2,1)S(1)} %get-tuple-element.49), channel_id=1, source_target_pairs={{0,24},{4,28},{8,16},{12,20},{16,8},{20,12},{24,0},{28,4},{1,25},{... | collective-permute-start | bytes 245768 | tf_op jit(solution)/shard_map/ppermute | solution.py:279
  37.5 1.8 %collective-permute-start.18 = (bf16[32,1280]{1,0:T(8,128)(2,1)S(1)}, bf16[32,1280]{1,0:T(8,128)(2,1)S(1)}, u32[]{:S(2)}, u32[]{:S(2)}) collective-permute-start(bf16[32,1280]{1,0:T(8,128)(2,1)S(1)} %get-tuple-element.50), channel_id=1, source_target_pairs={{0,28},{4,24},{8,20},{12,16},{16,12},{20,8},{24,4},{28,0},{1,29},{... | collective-permute-start | bytes 245768 | tf_op jit(solution)/shard_map/ppermute | solution.py:279
  39.3 0.6 %collective-permute-start.12 = (bf16[32,1280]{1,0:T(8,128)(2,1)S(1)}, bf16[32,1280]{1,0:T(8,128)(2,1)S(1)}, u32[]{:S(2)}, u32[]{:S(2)}) collective-permute-start(bf16[32,1280]{1,0:T(8,128)(2,1)S(1)} %get-tuple-element.43), channel_id=1, source_target_pairs={{0,8},{4,12},{8,0},{12,4},{16,24},{20,28},{24,16},{28,20},{1,9},{5... | collective-permute-start | bytes 245768 | tf_op jit(solution)/shard_map/ppermute | solution.py:279
  39.9 1.1 %collective-permute-start.13 = (bf16[32,1280]{1,0:T(8,128)(2,1)S(1)}, bf16[32,1280]{1,0:T(8,128)(2,1)S(1)}, u32[]{:S(2)}, u32[]{:S(2)}) collective-permute-start(bf16[32,1280]{1,0:T(8,128)(2,1)S(1)} %get-tuple-element.44), channel_id=1, source_target_pairs={{0,12},{4,8},{8,4},{12,0},{16,28},{20,24},{24,20},{28,16},{1,13},{... | collective-permute-start | bytes 245768 | tf_op jit(solution)/shard_map/ppermute | solution.py:279
  41.0 1.0 %collective-permute-start.14 = (bf16[32,1280]{1,0:T(8,128)(2,1)S(1)}, bf16[32,1280]{1,0:T(8,128)(2,1)S(1)}, u32[]{:S(2)}, u32[]{:S(2)}) collective-permute-start(bf16[32,1280]{1,0:T(8,128)(2,1)S(1)} %get-tuple-element.45), channel_id=1, source_target_pairs={{0,16},{4,20},{8,24},{12,28},{16,0},{20,4},{24,8},{28,12},{1,17},{... | collective-permute-start | bytes 245768 | tf_op jit(solution)/shard_map/ppermute | solution.py:279
  42.0 0.8 %collective-permute-done.17 = bf16[32,1280]{1,0:T(8,128)(2,1)S(1)} collective-permute-done((bf16[32,1280]{1,0:T(8,128)(2,1)S(1)}, bf16[32,1280]{1,0:T(8,128)(2,1)S(1)}, u32[]{:S(2)}, u32[]{:S(2)}) %collective-permute-start.17) | collective-permute-done | bytes 81952 | tf_op jit(solution)/shard_map/ppermute | solution.py:279
  42.8 0.7 %collective-permute-done.18 = bf16[32,1280]{1,0:T(8,128)(2,1)S(1)} collective-permute-done((bf16[32,1280]{1,0:T(8,128)(2,1)S(1)}, bf16[32,1280]{1,0:T(8,128)(2,1)S(1)}, u32[]{:S(2)}, u32[]{:S(2)}) %collective-permute-start.18) | collective-permute-done | bytes 81952 | tf_op jit(solution)/shard_map/ppermute | solution.py:279
  43.5 0.8 %place.2.refs_4_ = bf16[4,8,8,1280]{3,2,1,0:T(8,128)(2,1)} custom-call(s32[1]{0:T(128)} %bitcast.me_ref, bf16[4,8,1280]{2,1,0:T(8,128)(2,1)S(1)} %bitcast.38, bf16[4,8,1280]{2,1,0:T(8,128)(2,1)S(1)} %bitcast.41, bf16[4,8,1280]{2,1,0:T(8,128)(2,1)S(1)} %bitcast.43, bf16[4,8,1280]{2,1,0:T(8,128)(2,1)S(1)} %bitcast.44), custom_call_target="tpu_custom_call" | custom-call | tf_op jit(solution)/shard_map/place/pallas_call | solution.py:427
  44.3 1.6 %collective-permute-done.12 = bf16[32,1280]{1,0:T(8,128)(2,1)S(1)} collective-permute-done((bf16[32,1280]{1,0:T(8,128)(2,1)S(1)}, bf16[32,1280]{1,0:T(8,128)(2,1)S(1)}, u32[]{:S(2)}, u32[]{:S(2)}) %collective-permute-start.12) | collective-permute-done | bytes 81952 | tf_op jit(solution)/shard_map/ppermute | solution.py:279
  45.9 0.7 %collective-permute-done.13 = bf16[32,1280]{1,0:T(8,128)(2,1)S(1)} collective-permute-done((bf16[32,1280]{1,0:T(8,128)(2,1)S(1)}, bf16[32,1280]{1,0:T(8,128)(2,1)S(1)}, u32[]{:S(2)}, u32[]{:S(2)}) %collective-permute-start.13) | collective-permute-done | bytes 81952 | tf_op jit(solution)/shard_map/ppermute | solution.py:279
  46.5 1.0 %collective-permute-done.15 = bf16[32,1280]{1,0:T(8,128)(2,1)S(1)} collective-permute-done((bf16[32,1280]{1,0:T(8,128)(2,1)S(1)}, bf16[32,1280]{1,0:T(8,128)(2,1)S(1)}, u32[]{:S(2)}, u32[]{:S(2)}) %collective-permute-start.15) | collective-permute-done | bytes 81952 | tf_op jit(solution)/shard_map/ppermute | solution.py:279
  47.6 0.8 %place.3 = bf16[4,8,8,1280]{3,2,1,0:T(8,128)(2,1)} custom-call(s32[1]{0:T(128)} %bitcast.me_ref, bf16[4,8,1280]{2,1,0:T(8,128)(2,1)S(1)} %bitcast.39, bf16[4,8,1280]{2,1,0:T(8,128)(2,1)S(1)} %bitcast.40, bf16[4,8,1280]{2,1,0:T(8,128)(2,1)S(1)} %bitcast.42, bf16[4,8,1280]{2,1,0:T(8,128)(2,1)S(1)} %bitcast.45, ...), custom_call_target="tpu_custom_call", output_to_operand_aliasing={{}: (5, {})} | custom-call | tf_op jit(solution)/shard_map/place/pallas_call | solution.py:427
  (29 shorter events, 0.4 us)
Async XLA Ops:
  1.6 4.7 %collective-permute-start.5 = (f32[4,128]{1,0:T(4,128)S(1)}, f32[4,128]{1,0:T(4,128)S(1)}, u32[]{:S(2)}, u32[]{:S(2)}) collective-permute-start(f32[4,128]{1,0:T(4,128)S(1)} %get-tuple-element.38), channel_id=1, source_target_pairs={{0,1},{1,0},{2,3},{3,2},{4,5},{5,4},{6,7},{7,6},{8,9},{9,8},{10,11... | collective-permute-start | bytes 6152 | tf_op jit(solution)/shard_map/ppermute | solution.py:279
  6.3 7.5 %collective-permute-start.6 = (f32[4,128]{1,0:T(4,128)S(1)}, f32[4,128]{1,0:T(4,128)S(1)}, u32[]{:S(2)}, u32[]{:S(2)}) collective-permute-start(f32[4,128]{1,0:T(4,128)S(1)} %add.3.refs_0_), channel_id=1, source_target_pairs={{0,2},{1,3},{2,0},{3,1},{4,6},{5,7},{6,4},{7,5},{8,10},{9,11},{10,... | collective-permute-start | bytes 6152 | tf_op jit(solution)/shard_map/ppermute | solution.py:279
  9.3 7.7 %collective-permute-start = (bf16[2,4,8,1280]{3,2,1,0:T(8,128)(2,1)S(1)}, bf16[2,4,8,1280]{3,2,1,0:T(8,128)(2,1)S(1)}, u32[]{:S(2)}, u32[]{:S(2)}) collective-permute-start(bf16[2,4,8,1280]{3,2,1,0:T(8,128)(2,1)S(1)} %get-tuple-element.30), channel_id=1, source_target_pairs={{0,8},{4,12},{8,0},{12,4},{16,24},{20,28},{24,16},{28,20},{1,9},{5... | collective-permute-start | bytes 491528 | tf_op jit(solution)/shard_map/ppermute | solution.py:279
  10.8 9.2 %collective-permute-start.1 = (bf16[2,4,8,1280]{3,2,1,0:T(8,128)(2,1)S(1)}, bf16[2,4,8,1280]{3,2,1,0:T(8,128)(2,1)S(1)}, u32[]{:S(2)}, u32[]{:S(2)}) collective-permute-start(bf16[2,4,8,1280]{3,2,1,0:T(8,128)(2,1)S(1)} %get-tuple-element.31), channel_id=1, source_target_pairs={{0,16},{4,20},{8,24},{12,28},{16,0},{20,4},{24,8},{28,12},{1,17},{... | collective-permute-start | bytes 491528 | tf_op jit(solution)/shard_map/ppermute | solution.py:279
  12.3 8.6 %collective-permute-start.2 = (bf16[2,4,8,1280]{3,2,1,0:T(8,128)(2,1)S(1)}, bf16[2,4,8,1280]{3,2,1,0:T(8,128)(2,1)S(1)}, u32[]{:S(2)}, u32[]{:S(2)}) collective-permute-start(bf16[2,4,8,1280]{3,2,1,0:T(8,128)(2,1)S(1)} %get-tuple-element.32), channel_id=1, source_target_pairs={{0,24},{4,28},{8,16},{12,20},{16,8},{20,12},{24,0},{28,4},{1,25},{... | collective-permute-start | bytes 491528 | tf_op jit(solution)/shard_map/ppermute | solution.py:279
  13.8 13.1 %copy-start = (bf16[1280,1280]{1,0:T(8,128)(2,1)S(1)}, bf16[1280,1280]{1,0:T(8,128)(2,1)}, u32[]{:S(2)}) copy-start(bf16[1280,1280]{1,0:T(8,128)(2,1)} %wq_ref.3) | copy-start | bytes 9830404
  13.8 13.1 %copy-start.1 = (bf16[1280,1280]{1,0:T(8,128)(2,1)S(1)}, bf16[1280,1280]{1,0:T(8,128)(2,1)}, u32[]{:S(2)}) copy-start(bf16[1280,1280]{1,0:T(8,128)(2,1)} %wk_ref.3) | copy-start | bytes 9830404
  13.8 13.1 %copy-start.3 = (f32[3,1280]{1,0:T(4,128)S(1)}, f32[3,1280]{1,0:T(4,128)}, u32[]{:S(2)}) copy-start(f32[3,1280]{1,0:T(4,128)} %taps_ref.3) | copy-start | bytes 46084
  13.8 13.1 %copy-start.4 = (f32[1280]{0:T(1024)S(1)}, f32[1280]{0:T(1024)}, u32[]{:S(2)}) copy-start(f32[1280]{0:T(1024)} %bias_ref.1) | copy-start | bytes 15364
  14.0 9.3 %collective-permute-start.7 = (bf16[2,4,8,1280]{3,2,1,0:T(8,128)(2,1)S(1)}, bf16[2,4,8,1280]{3,2,1,0:T(8,128)(2,1)S(1)}, u32[]{:S(2)}, u32[]{:S(2)}) collective-permute-start(bf16[2,4,8,1280]{3,2,1,0:T(8,128)(2,1)S(1)} %get-tuple-element.40), channel_id=1, source_target_pairs={{0,8},{4,12},{8,0},{12,4},{16,24},{20,28},{24,16},{28,20},{1,9},{5... | collective-permute-start | bytes 491528 | tf_op jit(solution)/shard_map/ppermute | solution.py:279
  15.5 10.7 %collective-permute-start.8 = (bf16[2,4,8,1280]{3,2,1,0:T(8,128)(2,1)S(1)}, bf16[2,4,8,1280]{3,2,1,0:T(8,128)(2,1)S(1)}, u32[]{:S(2)}, u32[]{:S(2)}) collective-permute-start(bf16[2,4,8,1280]{3,2,1,0:T(8,128)(2,1)S(1)} %get-tuple-element.41), channel_id=1, source_target_pairs={{0,16},{4,20},{8,24},{12,28},{16,0},{20,4},{24,8},{28,12},{1,17},{... | collective-permute-start | bytes 491528 | tf_op jit(solution)/shard_map/ppermute | solution.py:279
  17.1 9.2 %collective-permute-start.9 = (bf16[2,4,8,1280]{3,2,1,0:T(8,128)(2,1)S(1)}, bf16[2,4,8,1280]{3,2,1,0:T(8,128)(2,1)S(1)}, u32[]{:S(2)}, u32[]{:S(2)}) collective-permute-start(bf16[2,4,8,1280]{3,2,1,0:T(8,128)(2,1)S(1)} %get-tuple-element.42), channel_id=1, source_target_pairs={{0,24},{4,28},{8,16},{12,20},{16,8},{20,12},{24,0},{28,4},{1,25},{... | collective-permute-start | bytes 491528 | tf_op jit(solution)/shard_map/ppermute | solution.py:279
  20.0 6.8 %collective-permute-start.3 = (bf16[32,1280]{1,0:T(8,128)(2,1)S(1)}, bf16[32,1280]{1,0:T(8,128)(2,1)S(1)}, u32[]{:S(2)}, u32[]{:S(2)}) collective-permute-start(bf16[32,1280]{1,0:T(8,128)(2,1)S(1)} %slice_bitcast_fusion.1), channel_id=1, source_target_pairs={{0,4},{4,0},{8,12},{12,8},{16,20},{20,16},{24,28},{28,24},{1,5},{5... | collective-permute-start | bytes 245768 | tf_op jit(solution)/shard_map/ppermute | solution.py:279
  21.0 5.9 %collective-permute-start.4 = (bf16[3,32,1280]{2,1,0:T(8,128)(2,1)S(1)}, bf16[3,32,1280]{2,1,0:T(8,128)(2,1)S(1)}, u32[]{:S(2)}, u32[]{:S(2)}) collective-permute-start(bf16[3,32,1280]{2,1,0:T(8,128)(2,1)S(1)} %join.2), channel_id=1, source_target_pairs={{0,4},{4,0},{8,12},{12,8},{16,20},{20,16},{24,28},{28,24},{1,5},{5... | collective-permute-start | bytes 737288 | tf_op jit(solution)/shard_map/ppermute | solution.py:279
  26.2 5.2 %collective-permute-start.11 = (bf16[3,32,1280]{2,1,0:T(8,128)(2,1)S(1)}, bf16[3,32,1280]{2,1,0:T(8,128)(2,1)S(1)}, u32[]{:S(2)}, u32[]{:S(2)}) collective-permute-start(bf16[3,32,1280]{2,1,0:T(8,128)(2,1)S(1)} %join.3), channel_id=1, source_target_pairs={{0,4},{4,0},{8,12},{12,8},{16,20},{20,16},{24,28},{28,24},{1,5},{5... | collective-permute-start | bytes 737288 | tf_op jit(solution)/shard_map/ppermute | solution.py:279
  26.3 5.0 %collective-permute-start.10 = (bf16[32,1280]{1,0:T(8,128)(2,1)S(1)}, bf16[32,1280]{1,0:T(8,128)(2,1)S(1)}, u32[]{:S(2)}, u32[]{:S(2)}) collective-permute-start(bf16[32,1280]{1,0:T(8,128)(2,1)S(1)} %slice_bitcast_fusion), channel_id=1, source_target_pairs={{0,4},{4,0},{8,12},{12,8},{16,20},{20,16},{24,28},{28,24},{1,5},{5... | collective-permute-start | bytes 245768 | tf_op jit(solution)/shard_map/ppermute | solution.py:279
  26.9 3.5 %copy-start.2 = (bf16[1280,1280]{1,0:T(8,128)(2,1)S(1)}, bf16[1280,1280]{1,0:T(8,128)(2,1)}, u32[]{:S(2)}) copy-start(bf16[1280,1280]{1,0:T(8,128)(2,1)} %wv_ref.3) | copy-start | bytes 9830404
  36.5 4.5 %collective-permute-start.16 = (bf16[32,1280]{1,0:T(8,128)(2,1)S(1)}, bf16[32,1280]{1,0:T(8,128)(2,1)S(1)}, u32[]{:S(2)}, u32[]{:S(2)}) collective-permute-start(bf16[32,1280]{1,0:T(8,128)(2,1)S(1)} %get-tuple-element.48), channel_id=1, source_target_pairs={{0,4},{4,0},{8,12},{12,8},{16,20},{20,16},{24,28},{28,24},{1,5},{5... | collective-permute-start | bytes 245768 | tf_op jit(solution)/shard_map/ppermute | solution.py:279
  36.6 6.2 %collective-permute-start.17 = (bf16[32,1280]{1,0:T(8,128)(2,1)S(1)}, bf16[32,1280]{1,0:T(8,128)(2,1)S(1)}, u32[]{:S(2)}, u32[]{:S(2)}) collective-permute-start(bf16[32,1280]{1,0:T(8,128)(2,1)S(1)} %get-tuple-element.49), channel_id=1, source_target_pairs={{0,24},{4,28},{8,16},{12,20},{16,8},{20,12},{24,0},{28,4},{1,25},{... | collective-permute-start | bytes 245768 | tf_op jit(solution)/shard_map/ppermute | solution.py:279
  37.5 6.0 %collective-permute-start.18 = (bf16[32,1280]{1,0:T(8,128)(2,1)S(1)}, bf16[32,1280]{1,0:T(8,128)(2,1)S(1)}, u32[]{:S(2)}, u32[]{:S(2)}) collective-permute-start(bf16[32,1280]{1,0:T(8,128)(2,1)S(1)} %get-tuple-element.50), channel_id=1, source_target_pairs={{0,28},{4,24},{8,20},{12,16},{16,12},{20,8},{24,4},{28,0},{1,29},{... | collective-permute-start | bytes 245768 | tf_op jit(solution)/shard_map/ppermute | solution.py:279
  39.3 6.6 %collective-permute-start.12 = (bf16[32,1280]{1,0:T(8,128)(2,1)S(1)}, bf16[32,1280]{1,0:T(8,128)(2,1)S(1)}, u32[]{:S(2)}, u32[]{:S(2)}) collective-permute-start(bf16[32,1280]{1,0:T(8,128)(2,1)S(1)} %get-tuple-element.43), channel_id=1, source_target_pairs={{0,8},{4,12},{8,0},{12,4},{16,24},{20,28},{24,16},{28,20},{1,9},{5... | collective-permute-start | bytes 245768 | tf_op jit(solution)/shard_map/ppermute | solution.py:279
  39.9 6.6 %collective-permute-start.13 = (bf16[32,1280]{1,0:T(8,128)(2,1)S(1)}, bf16[32,1280]{1,0:T(8,128)(2,1)S(1)}, u32[]{:S(2)}, u32[]{:S(2)}) collective-permute-start(bf16[32,1280]{1,0:T(8,128)(2,1)S(1)} %get-tuple-element.44), channel_id=1, source_target_pairs={{0,12},{4,8},{8,4},{12,0},{16,28},{20,24},{24,20},{28,16},{1,13},{... | collective-permute-start | bytes 245768 | tf_op jit(solution)/shard_map/ppermute | solution.py:279
  41.0 5.5 %collective-permute-start.14 = (bf16[32,1280]{1,0:T(8,128)(2,1)S(1)}, bf16[32,1280]{1,0:T(8,128)(2,1)S(1)}, u32[]{:S(2)}, u32[]{:S(2)}) collective-permute-start(bf16[32,1280]{1,0:T(8,128)(2,1)S(1)} %get-tuple-element.45), channel_id=1, source_target_pairs={{0,16},{4,20},{8,24},{12,28},{16,0},{20,4},{24,8},{28,12},{1,17},{... | collective-permute-start | bytes 245768 | tf_op jit(solution)/shard_map/ppermute | solution.py:279
  42.8 4.7 %collective-permute-start.15 = (bf16[32,1280]{1,0:T(8,128)(2,1)S(1)}, bf16[32,1280]{1,0:T(8,128)(2,1)S(1)}, u32[]{:S(2)}, u32[]{:S(2)}) collective-permute-start(bf16[32,1280]{1,0:T(8,128)(2,1)S(1)} %get-tuple-element.46), channel_id=1, source_target_pairs={{0,20},{4,16},{8,28},{12,24},{16,4},{20,0},{24,12},{28,8},{1,21},{... | collective-permute-start | bytes 245768 | tf_op jit(solution)/shard_map/ppermute | solution.py:279

commit v7 on v6

--- a/solution.py
+++ b/solution.py
@@ -65,22 +65,22 @@
     outs = refs[:peers // 2 - 1]
     energy_ref, held_ref, sems = refs[peers // 2 - 1:]
     frame_rows = held_ref.shape[0]
-    held = [
-        pltpu.make_async_copy(cotangent_ref.at[frame], held_ref.at[frame], sems.at[peers + frame])
-        for frame in range(frame_rows)
-    ]
+    held = pltpu.make_async_copy(cotangent_ref, held_ref, sems.at[peers])
     copies = pieces(tokens_ref, outs, me_ref[0], range(2, peers), sems)
-    for copy in held + copies:
+    for copy in [held] + copies:
         copy.start()
+    held.wait()
+    partial = []
     for frame in range(frame_rows):
-        held[frame].wait()
         total = jnp.zeros(held_ref.shape[2:], jnp.float32)
         for group in range(peers):
             grad = held_ref[frame, group].astype(jnp.float32)
             total += grad * grad
-        energy_ref[frame:frame + 1, :] = jnp.broadcast_to(
-            jnp.sum(total, keepdims=True), (1, LANES)
-        )
+        lanes = sum(total[:, col:col + LANES] for col in range(0, total.shape[1], LANES))
+        partial.append(jnp.sum(lanes, axis=0, keepdims=True))
+    energy_ref[...] = jnp.broadcast_to(
+        jnp.sum(jnp.concatenate(partial, axis=0), axis=1, keepdims=True), energy_ref.shape
+    )
     for copy in copies:
         copy.wait()
 
@@ -357,7 +357,7 @@
         out_specs=[vmem] * (peers // 2 + 1),
         out_shape=[sent_shape] * (peers // 2 - 1)
         + [pltpu.VMEM((frame_rows, LANES), jnp.float32), low(split)],
-        scratch_shapes=[pltpu.SemaphoreType.DMA((peers + frame_rows,))],
+        scratch_shapes=[pltpu.SemaphoreType.DMA((peers + 1,))],
         compiler_params=grant(8),
         name="pack",
     )(me_arg, tokens, cotangent)

time: 48.5 us -> 48.2 us (level)
  no operation moved by 1% of the time
where the time goes in v7:
time: 48.2 us; the launch traced here: 48.1 us
  starting transfers between devices  20.7 us (43%)
  waiting for transfers between devices  13.6 us (28%)
  Pallas kernels  13.5 us (28%)
    ppermute x19, starting transfers between devices, swap(): lax.ppermute(value, axis, [(i, i ^ mask) for i in range(lax.axis_size(axi...  20.7 us
    ppermute x19, waiting for transfers between devices, swap(): lax.ppermute(value, axis, [(i, i ^ mask) for i in range(lax.axis_size(axi...  13.6 us
    pallas_call x1, Pallas kernels, body(): pl.pallas_call(functools.partial(backward_kernel, **sizes), in_specs=[sme...  5.05 us
    pallas_call x1, Pallas kernels, body(): pl.pallas_call(functools.partial(forward_kernel, **sizes), in_specs=[smem...  3.46 us
    pallas_call x2, Pallas kernels, body(): pl.pallas_call(functools.partial(place_kernel, masks=masks), in_specs=[sm...  1.5 us
    pallas_call x1, Pallas kernels, body(): pl.pallas_call(functools.partial(pack_kernel, peers=peers), in_specs=[sme...  1.32 us
    pallas_call x1, Pallas kernels, body(): pl.pallas_call(value_kernel, in_specs=[vmem] * 2, out_specs=vmem, out_sha...  1.02 us
  transfers between devices with their start and end apart: 19, of which 10 were waited for; matrix products, arithmetic and copies ran while one was open for 0% of the time, Pallas kernels for 13%

profile of v7, /device:TPU:0, one launch (start us, length us, event | category | flops | bytes accessed | tf_op | source)
XLA Modules:
  0.0 48.1 jit_solution(11362563083890592120)
XLA Ops:
  0.0 1.3 %pack.1 = (bf16[2,4,8,1280]{3,2,1,0:T(8,128)(2,1)S(1)}, bf16[2,4,8,1280]{3,2,1,0:T(8,128)(2,1)S(1)}, bf16[2,4,8,1280]{3,2,1,0:T(8,128)(2,1)S(1)}, f32[4,128]{1,0:T(4,128)S(1)}, bf16[4,8,8,1280]{3,2,1,0:T(8,128)(2,1)S(1)}) custom-call(s32[1]{0:T(128)} %bitcast.me_ref, bf16[4,8,8,1280]{3,2,1,0:T(8,128)(2,1)} %bitcast.46, bf16[4,8,8,1280]{3,2,1,0:T(8,128)(2,1)} %bitcast.48), custom_call_target="tpu_custom_call" | custom-call | tf_op jit(solution)/shard_map/pack/pallas_call | solution.py:354
  1.3 3.1 %collective-permute-start.5 = (f32[4,128]{1,0:T(4,128)S(1)}, f32[4,128]{1,0:T(4,128)S(1)}, u32[]{:S(2)}, u32[]{:S(2)}) collective-permute-start(f32[4,128]{1,0:T(4,128)S(1)} %get-tuple-element.38), channel_id=1, source_target_pairs={{0,1},{1,0},{2,3},{3,2},{4,5},{5,4},{6,7},{7,6},{8,9},{9,8},{10,11... | collective-permute-start | bytes 6152 | tf_op jit(solution)/shard_map/ppermute | solution.py:279
  4.5 1.6 %collective-permute-done.5 = f32[4,128]{1,0:T(4,128)S(1)} collective-permute-done((f32[4,128]{1,0:T(4,128)S(1)}, f32[4,128]{1,0:T(4,128)S(1)}, u32[]{:S(2)}, u32[]{:S(2)}) %collective-permute-start.5) | collective-permute-done | bytes 2080 | tf_op jit(solution)/shard_map/ppermute | solution.py:279
  6.0 3.0 %collective-permute-start.6 = (f32[4,128]{1,0:T(4,128)S(1)}, f32[4,128]{1,0:T(4,128)S(1)}, u32[]{:S(2)}, u32[]{:S(2)}) collective-permute-start(f32[4,128]{1,0:T(4,128)S(1)} %add.3.refs_0_), channel_id=1, source_target_pairs={{0,2},{1,3},{2,0},{3,1},{4,6},{5,7},{6,4},{7,5},{8,10},{9,11},{10,... | collective-permute-start | bytes 6152 | tf_op jit(solution)/shard_map/ppermute | solution.py:279
  9.1 1.5 %collective-permute-start = (bf16[2,4,8,1280]{3,2,1,0:T(8,128)(2,1)S(1)}, bf16[2,4,8,1280]{3,2,1,0:T(8,128)(2,1)S(1)}, u32[]{:S(2)}, u32[]{:S(2)}) collective-permute-start(bf16[2,4,8,1280]{3,2,1,0:T(8,128)(2,1)S(1)} %get-tuple-element.30), channel_id=1, source_target_pairs={{0,8},{4,12},{8,0},{12,4},{16,24},{20,28},{24,16},{28,20},{1,9},{5... | collective-permute-start | bytes 491528 | tf_op jit(solution)/shard_map/ppermute | solution.py:279
  10.5 1.5 %collective-permute-start.1 = (bf16[2,4,8,1280]{3,2,1,0:T(8,128)(2,1)S(1)}, bf16[2,4,8,1280]{3,2,1,0:T(8,128)(2,1)S(1)}, u32[]{:S(2)}, u32[]{:S(2)}) collective-permute-start(bf16[2,4,8,1280]{3,2,1,0:T(8,128)(2,1)S(1)} %get-tuple-element.31), channel_id=1, source_target_pairs={{0,16},{4,20},{8,24},{12,28},{16,0},{20,4},{24,8},{28,12},{1,17},{... | collective-permute-start | bytes 491528 | tf_op jit(solution)/shard_map/ppermute | solution.py:279
  12.1 0.5 collective-permute-start.2
  12.5 0.9 %prepare.1 = (bf16[2,4,8,1280]{3,2,1,0:T(8,128)(2,1)S(1)}, bf16[2,256,256]{2,1,0:T(8,128)(2,1)S(1)}) custom-call(s32[1]{0:T(128)} %bitcast.me_ref, bf16[4,8,8,1280]{3,2,1,0:T(8,128)(2,1)} %bitcast.47), custom_call_target="tpu_custom_call" | custom-call | tf_op jit(solution)/shard_map/prepare/pallas_call | solution.py:364
  13.6 0.2 scale.1
  13.7 1.6 %collective-permute-start.7 = (bf16[2,4,8,1280]{3,2,1,0:T(8,128)(2,1)S(1)}, bf16[2,4,8,1280]{3,2,1,0:T(8,128)(2,1)S(1)}, u32[]{:S(2)}, u32[]{:S(2)}) collective-permute-start(bf16[2,4,8,1280]{3,2,1,0:T(8,128)(2,1)S(1)} %get-tuple-element.40), channel_id=1, source_target_pairs={{0,8},{4,12},{8,0},{12,4},{16,24},{20,28},{24,16},{28,20},{1,9},{5... | collective-permute-start | bytes 491528 | tf_op jit(solution)/shard_map/ppermute | solution.py:279
  15.3 1.5 %collective-permute-start.8 = (bf16[2,4,8,1280]{3,2,1,0:T(8,128)(2,1)S(1)}, bf16[2,4,8,1280]{3,2,1,0:T(8,128)(2,1)S(1)}, u32[]{:S(2)}, u32[]{:S(2)}) collective-permute-start(bf16[2,4,8,1280]{3,2,1,0:T(8,128)(2,1)S(1)} %get-tuple-element.41), channel_id=1, source_target_pairs={{0,16},{4,20},{8,24},{12,28},{16,0},{20,4},{24,8},{28,12},{1,17},{... | collective-permute-start | bytes 491528 | tf_op jit(solution)/shard_map/ppermute | solution.py:279
  16.8 1.8 %collective-permute-start.9 = (bf16[2,4,8,1280]{3,2,1,0:T(8,128)(2,1)S(1)}, bf16[2,4,8,1280]{3,2,1,0:T(8,128)(2,1)S(1)}, u32[]{:S(2)}, u32[]{:S(2)}) collective-permute-start(bf16[2,4,8,1280]{3,2,1,0:T(8,128)(2,1)S(1)} %get-tuple-element.42), channel_id=1, source_target_pairs={{0,24},{4,28},{8,16},{12,20},{16,8},{20,12},{24,0},{28,4},{1,25},{... | collective-permute-start | bytes 491528 | tf_op jit(solution)/shard_map/ppermute | solution.py:279
  18.6 1.2 %collective-permute-done.1 = bf16[2,4,8,1280]{3,2,1,0:T(8,128)(2,1)S(1)} collective-permute-done((bf16[2,4,8,1280]{3,2,1,0:T(8,128)(2,1)S(1)}, bf16[2,4,8,1280]{3,2,1,0:T(8,128)(2,1)S(1)}, u32[]{:S(2)}, u32[]{:S(2)}) %collective-permute-start.1) | collective-permute-done | bytes 163872 | tf_op jit(solution)/shard_map/ppermute | solution.py:279
  19.7 0.9 %collective-permute-done.2 = bf16[2,4,8,1280]{3,2,1,0:T(8,128)(2,1)S(1)} collective-permute-done((bf16[2,4,8,1280]{3,2,1,0:T(8,128)(2,1)S(1)}, bf16[2,4,8,1280]{3,2,1,0:T(8,128)(2,1)S(1)}, u32[]{:S(2)}, u32[]{:S(2)}) %collective-permute-start.2) | collective-permute-done | bytes 163872 | tf_op jit(solution)/shard_map/ppermute | solution.py:279
  20.8 2.2 %collective-permute-done.7 = bf16[2,4,8,1280]{3,2,1,0:T(8,128)(2,1)S(1)} collective-permute-done((bf16[2,4,8,1280]{3,2,1,0:T(8,128)(2,1)S(1)}, bf16[2,4,8,1280]{3,2,1,0:T(8,128)(2,1)S(1)}, u32[]{:S(2)}, u32[]{:S(2)}) %collective-permute-start.7) | collective-permute-done | bytes 163872 | tf_op jit(solution)/shard_map/ppermute | solution.py:279
  23.0 3.0 %collective-permute-done.8 = bf16[2,4,8,1280]{3,2,1,0:T(8,128)(2,1)S(1)} collective-permute-done((bf16[2,4,8,1280]{3,2,1,0:T(8,128)(2,1)S(1)}, bf16[2,4,8,1280]{3,2,1,0:T(8,128)(2,1)S(1)}, u32[]{:S(2)}, u32[]{:S(2)}) %collective-permute-start.8) | collective-permute-done | bytes 163872 | tf_op jit(solution)/shard_map/ppermute | solution.py:279
  26.1 0.5 %collective-permute-start.10 = (bf16[32,1280]{1,0:T(8,128)(2,1)S(1)}, bf16[32,1280]{1,0:T(8,128)(2,1)S(1)}, u32[]{:S(2)}, u32[]{:S(2)}) collective-permute-start(bf16[32,1280]{1,0:T(8,128)(2,1)S(1)} %slice_bitcast_fusion), channel_id=1, source_target_pairs={{0,4},{4,0},{8,12},{12,8},{16,20},{20,16},{24,28},{28,24},{1,5},{5... | collective-permute-start | bytes 245768 | tf_op jit(solution)/shard_map/ppermute | solution.py:279
  26.6 3.5 %forward.1 = (bf16[256,1280]{1,0:T(8,128)(2,1)S(1)}, bf16[256,1280]{1,0:T(8,128)(2,1)S(1)}, f32[20,32,256]{2,1,0:T(8,128)S(1)}, bf16[256,1280]{1,0:T(8,128)(2,1)S(1)}) custom-call(s32[1]{0:T(128)} %bitcast.me_ref, bf16[2,256,256]{2,1,0:T(8,128)(2,1)S(1)} %get-tuple-element.28.order_ref, f32[3,1280]{1,0:T(4,128)S(1)} %copy-done.3, f32[1280]{0:T(1024)S(1)} %copy-done.4, ...), custom_call_target="tpu_custom_call" | custom-call | tf_op jit(solution)/shard_map/forward/pallas_call | solution.py:390
  30.1 1.0 %value.1.v_ref = bf16[256,1280]{1,0:T(8,128)(2,1)S(1)} custom-call(bf16[256,1280]{1,0:T(8,128)(2,1)S(1)} %get-tuple-element.35.hidden_ref, bf16[1280,1280]{1,0:T(8,128)(2,1)S(1)} %copy-done.2), custom_call_target="tpu_custom_call" | custom-call | tf_op jit(solution)/shard_map/value/pallas_call | solution.py:400
  31.1 5.1 %backward.1 = (bf16[32,1280]{1,0:T(8,128)(2,1)S(1)}, bf16[32,1280]{1,0:T(8,128)(2,1)S(1)}, bf16[32,1280]{1,0:T(8,128)(2,1)S(1)}, bf16[32,1280]{1,0:T(8,128)(2,1)...) custom-call(s32[1]{0:T(128)} %bitcast.me_ref, ...), custom_call_target="tpu_custom_call" | custom-call | tf_op jit(solution)/shard_map/backward/pallas_call | solution.py:408
  36.4 0.8 %collective-permute-start.17 = (bf16[32,1280]{1,0:T(8,128)(2,1)S(1)}, bf16[32,1280]{1,0:T(8,128)(2,1)S(1)}, u32[]{:S(2)}, u32[]{:S(2)}) collective-permute-start(bf16[32,1280]{1,0:T(8,128)(2,1)S(1)} %get-tuple-element.49), channel_id=1, source_target_pairs={{0,24},{4,28},{8,16},{12,20},{16,8},{20,12},{24,0},{28,4},{1,25},{... | collective-permute-start | bytes 245768 | tf_op jit(solution)/shard_map/ppermute | solution.py:279
  37.2 1.8 %collective-permute-start.18 = (bf16[32,1280]{1,0:T(8,128)(2,1)S(1)}, bf16[32,1280]{1,0:T(8,128)(2,1)S(1)}, u32[]{:S(2)}, u32[]{:S(2)}) collective-permute-start(bf16[32,1280]{1,0:T(8,128)(2,1)S(1)} %get-tuple-element.50), channel_id=1, source_target_pairs={{0,28},{4,24},{8,20},{12,16},{16,12},{20,8},{24,4},{28,0},{1,29},{... | collective-permute-start | bytes 245768 | tf_op jit(solution)/shard_map/ppermute | solution.py:279
  39.0 0.6 %collective-permute-start.12 = (bf16[32,1280]{1,0:T(8,128)(2,1)S(1)}, bf16[32,1280]{1,0:T(8,128)(2,1)S(1)}, u32[]{:S(2)}, u32[]{:S(2)}) collective-permute-start(bf16[32,1280]{1,0:T(8,128)(2,1)S(1)} %get-tuple-element.43), channel_id=1, source_target_pairs={{0,8},{4,12},{8,0},{12,4},{16,24},{20,28},{24,16},{28,20},{1,9},{5... | collective-permute-start | bytes 245768 | tf_op jit(solution)/shard_map/ppermute | solution.py:279
  39.6 1.1 %collective-permute-start.13 = (bf16[32,1280]{1,0:T(8,128)(2,1)S(1)}, bf16[32,1280]{1,0:T(8,128)(2,1)S(1)}, u32[]{:S(2)}, u32[]{:S(2)}) collective-permute-start(bf16[32,1280]{1,0:T(8,128)(2,1)S(1)} %get-tuple-element.44), channel_id=1, source_target_pairs={{0,12},{4,8},{8,4},{12,0},{16,28},{20,24},{24,20},{28,16},{1,13},{... | collective-permute-start | bytes 245768 | tf_op jit(solution)/shard_map/ppermute | solution.py:279
  40.7 1.0 %collective-permute-start.14 = (bf16[32,1280]{1,0:T(8,128)(2,1)S(1)}, bf16[32,1280]{1,0:T(8,128)(2,1)S(1)}, u32[]{:S(2)}, u32[]{:S(2)}) collective-permute-start(bf16[32,1280]{1,0:T(8,128)(2,1)S(1)} %get-tuple-element.45), channel_id=1, source_target_pairs={{0,16},{4,20},{8,24},{12,28},{16,0},{20,4},{24,8},{28,12},{1,17},{... | collective-permute-start | bytes 245768 | tf_op jit(solution)/shard_map/ppermute | solution.py:279
  41.8 0.8 %collective-permute-done.17 = bf16[32,1280]{1,0:T(8,128)(2,1)S(1)} collective-permute-done((bf16[32,1280]{1,0:T(8,128)(2,1)S(1)}, bf16[32,1280]{1,0:T(8,128)(2,1)S(1)}, u32[]{:S(2)}, u32[]{:S(2)}) %collective-permute-start.17) | collective-permute-done | bytes 81952 | tf_op jit(solution)/shard_map/ppermute | solution.py:279
  42.6 0.7 %collective-permute-done.18 = bf16[32,1280]{1,0:T(8,128)(2,1)S(1)} collective-permute-done((bf16[32,1280]{1,0:T(8,128)(2,1)S(1)}, bf16[32,1280]{1,0:T(8,128)(2,1)S(1)}, u32[]{:S(2)}, u32[]{:S(2)}) %collective-permute-start.18) | collective-permute-done | bytes 81952 | tf_op jit(solution)/shard_map/ppermute | solution.py:279
  43.2 0.8 %place.2.refs_4_ = bf16[4,8,8,1280]{3,2,1,0:T(8,128)(2,1)} custom-call(s32[1]{0:T(128)} %bitcast.me_ref, bf16[4,8,1280]{2,1,0:T(8,128)(2,1)S(1)} %bitcast.38, bf16[4,8,1280]{2,1,0:T(8,128)(2,1)S(1)} %bitcast.41, bf16[4,8,1280]{2,1,0:T(8,128)(2,1)S(1)} %bitcast.43, bf16[4,8,1280]{2,1,0:T(8,128)(2,1)S(1)} %bitcast.44), custom_call_target="tpu_custom_call" | custom-call | tf_op jit(solution)/shard_map/place/pallas_call | solution.py:427
  44.0 1.6 %collective-permute-done.12 = bf16[32,1280]{1,0:T(8,128)(2,1)S(1)} collective-permute-done((bf16[32,1280]{1,0:T(8,128)(2,1)S(1)}, bf16[32,1280]{1,0:T(8,128)(2,1)S(1)}, u32[]{:S(2)}, u32[]{:S(2)}) %collective-permute-start.12) | collective-permute-done | bytes 81952 | tf_op jit(solution)/shard_map/ppermute | solution.py:279
  45.6 0.7 %collective-permute-done.13 = bf16[32,1280]{1,0:T(8,128)(2,1)S(1)} collective-permute-done((bf16[32,1280]{1,0:T(8,128)(2,1)S(1)}, bf16[32,1280]{1,0:T(8,128)(2,1)S(1)}, u32[]{:S(2)}, u32[]{:S(2)}) %collective-permute-start.13) | collective-permute-done | bytes 81952 | tf_op jit(solution)/shard_map/ppermute | solution.py:279
  46.3 1.0 %collective-permute-done.15 = bf16[32,1280]{1,0:T(8,128)(2,1)S(1)} collective-permute-done((bf16[32,1280]{1,0:T(8,128)(2,1)S(1)}, bf16[32,1280]{1,0:T(8,128)(2,1)S(1)}, u32[]{:S(2)}, u32[]{:S(2)}) %collective-permute-start.15) | collective-permute-done | bytes 81952 | tf_op jit(solution)/shard_map/ppermute | solution.py:279
  47.3 0.8 %place.3 = bf16[4,8,8,1280]{3,2,1,0:T(8,128)(2,1)} custom-call(s32[1]{0:T(128)} %bitcast.me_ref, bf16[4,8,1280]{2,1,0:T(8,128)(2,1)S(1)} %bitcast.39, bf16[4,8,1280]{2,1,0:T(8,128)(2,1)S(1)} %bitcast.40, bf16[4,8,1280]{2,1,0:T(8,128)(2,1)S(1)} %bitcast.42, bf16[4,8,1280]{2,1,0:T(8,128)(2,1)S(1)} %bitcast.45, ...), custom_call_target="tpu_custom_call", output_to_operand_aliasing={{}: (5, {})} | custom-call | tf_op jit(solution)/shard_map/place/pallas_call | solution.py:427
  (29 shorter events, 0.4 us)
Async XLA Ops:
  1.3 4.7 %collective-permute-start.5 = (f32[4,128]{1,0:T(4,128)S(1)}, f32[4,128]{1,0:T(4,128)S(1)}, u32[]{:S(2)}, u32[]{:S(2)}) collective-permute-start(f32[4,128]{1,0:T(4,128)S(1)} %get-tuple-element.38), channel_id=1, source_target_pairs={{0,1},{1,0},{2,3},{3,2},{4,5},{5,4},{6,7},{7,6},{8,9},{9,8},{10,11... | collective-permute-start | bytes 6152 | tf_op jit(solution)/shard_map/ppermute | solution.py:279
  6.0 7.5 %collective-permute-start.6 = (f32[4,128]{1,0:T(4,128)S(1)}, f32[4,128]{1,0:T(4,128)S(1)}, u32[]{:S(2)}, u32[]{:S(2)}) collective-permute-start(f32[4,128]{1,0:T(4,128)S(1)} %add.3.refs_0_), channel_id=1, source_target_pairs={{0,2},{1,3},{2,0},{3,1},{4,6},{5,7},{6,4},{7,5},{8,10},{9,11},{10,... | collective-permute-start | bytes 6152 | tf_op jit(solution)/shard_map/ppermute | solution.py:279
  9.1 7.7 %collective-permute-start = (bf16[2,4,8,1280]{3,2,1,0:T(8,128)(2,1)S(1)}, bf16[2,4,8,1280]{3,2,1,0:T(8,128)(2,1)S(1)}, u32[]{:S(2)}, u32[]{:S(2)}) collective-permute-start(bf16[2,4,8,1280]{3,2,1,0:T(8,128)(2,1)S(1)} %get-tuple-element.30), channel_id=1, source_target_pairs={{0,8},{4,12},{8,0},{12,4},{16,24},{20,28},{24,16},{28,20},{1,9},{5... | collective-permute-start | bytes 491528 | tf_op jit(solution)/shard_map/ppermute | solution.py:279
  10.5 9.2 %collective-permute-start.1 = (bf16[2,4,8,1280]{3,2,1,0:T(8,128)(2,1)S(1)}, bf16[2,4,8,1280]{3,2,1,0:T(8,128)(2,1)S(1)}, u32[]{:S(2)}, u32[]{:S(2)}) collective-permute-start(bf16[2,4,8,1280]{3,2,1,0:T(8,128)(2,1)S(1)} %get-tuple-element.31), channel_id=1, source_target_pairs={{0,16},{4,20},{8,24},{12,28},{16,0},{20,4},{24,8},{28,12},{1,17},{... | collective-permute-start | bytes 491528 | tf_op jit(solution)/shard_map/ppermute | solution.py:279
  12.1 8.6 %collective-permute-start.2 = (bf16[2,4,8,1280]{3,2,1,0:T(8,128)(2,1)S(1)}, bf16[2,4,8,1280]{3,2,1,0:T(8,128)(2,1)S(1)}, u32[]{:S(2)}, u32[]{:S(2)}) collective-permute-start(bf16[2,4,8,1280]{3,2,1,0:T(8,128)(2,1)S(1)} %get-tuple-element.32), channel_id=1, source_target_pairs={{0,24},{4,28},{8,16},{12,20},{16,8},{20,12},{24,0},{28,4},{1,25},{... | collective-permute-start | bytes 491528 | tf_op jit(solution)/shard_map/ppermute | solution.py:279
  13.5 13.1 %copy-start = (bf16[1280,1280]{1,0:T(8,128)(2,1)S(1)}, bf16[1280,1280]{1,0:T(8,128)(2,1)}, u32[]{:S(2)}) copy-start(bf16[1280,1280]{1,0:T(8,128)(2,1)} %wq_ref.3) | copy-start | bytes 9830404
  13.5 13.1 %copy-start.1 = (bf16[1280,1280]{1,0:T(8,128)(2,1)S(1)}, bf16[1280,1280]{1,0:T(8,128)(2,1)}, u32[]{:S(2)}) copy-start(bf16[1280,1280]{1,0:T(8,128)(2,1)} %wk_ref.3) | copy-start | bytes 9830404
  13.5 13.1 %copy-start.3 = (f32[3,1280]{1,0:T(4,128)S(1)}, f32[3,1280]{1,0:T(4,128)}, u32[]{:S(2)}) copy-start(f32[3,1280]{1,0:T(4,128)} %taps_ref.3) | copy-start | bytes 46084
  13.5 13.1 %copy-start.4 = (f32[1280]{0:T(1024)S(1)}, f32[1280]{0:T(1024)}, u32[]{:S(2)}) copy-start(f32[1280]{0:T(1024)} %bias_ref.1) | copy-start | bytes 15364
  13.7 9.3 %collective-permute-start.7 = (bf16[2,4,8,1280]{3,2,1,0:T(8,128)(2,1)S(1)}, bf16[2,4,8,1280]{3,2,1,0:T(8,128)(2,1)S(1)}, u32[]{:S(2)}, u32[]{:S(2)}) collective-permute-start(bf16[2,4,8,1280]{3,2,1,0:T(8,128)(2,1)S(1)} %get-tuple-element.40), channel_id=1, source_target_pairs={{0,8},{4,12},{8,0},{12,4},{16,24},{20,28},{24,16},{28,20},{1,9},{5... | collective-permute-start | bytes 491528 | tf_op jit(solution)/shard_map/ppermute | solution.py:279
  15.3 10.7 %collective-permute-start.8 = (bf16[2,4,8,1280]{3,2,1,0:T(8,128)(2,1)S(1)}, bf16[2,4,8,1280]{3,2,1,0:T(8,128)(2,1)S(1)}, u32[]{:S(2)}, u32[]{:S(2)}) collective-permute-start(bf16[2,4,8,1280]{3,2,1,0:T(8,128)(2,1)S(1)} %get-tuple-element.41), channel_id=1, source_target_pairs={{0,16},{4,20},{8,24},{12,28},{16,0},{20,4},{24,8},{28,12},{1,17},{... | collective-permute-start | bytes 491528 | tf_op jit(solution)/shard_map/ppermute | solution.py:279
  16.8 9.2 %collective-permute-start.9 = (bf16[2,4,8,1280]{3,2,1,0:T(8,128)(2,1)S(1)}, bf16[2,4,8,1280]{3,2,1,0:T(8,128)(2,1)S(1)}, u32[]{:S(2)}, u32[]{:S(2)}) collective-permute-start(bf16[2,4,8,1280]{3,2,1,0:T(8,128)(2,1)S(1)} %get-tuple-element.42), channel_id=1, source_target_pairs={{0,24},{4,28},{8,16},{12,20},{16,8},{20,12},{24,0},{28,4},{1,25},{... | collective-permute-start | bytes 491528 | tf_op jit(solution)/shard_map/ppermute | solution.py:279
  19.7 6.8 %collective-permute-start.3 = (bf16[32,1280]{1,0:T(8,128)(2,1)S(1)}, bf16[32,1280]{1,0:T(8,128)(2,1)S(1)}, u32[]{:S(2)}, u32[]{:S(2)}) collective-permute-start(bf16[32,1280]{1,0:T(8,128)(2,1)S(1)} %slice_bitcast_fusion.1), channel_id=1, source_target_pairs={{0,4},{4,0},{8,12},{12,8},{16,20},{20,16},{24,28},{28,24},{1,5},{5... | collective-permute-start | bytes 245768 | tf_op jit(solution)/shard_map/ppermute | solution.py:279
  20.7 5.9 %collective-permute-start.4 = (bf16[3,32,1280]{2,1,0:T(8,128)(2,1)S(1)}, bf16[3,32,1280]{2,1,0:T(8,128)(2,1)S(1)}, u32[]{:S(2)}, u32[]{:S(2)}) collective-permute-start(bf16[3,32,1280]{2,1,0:T(8,128)(2,1)S(1)} %join.2), channel_id=1, source_target_pairs={{0,4},{4,0},{8,12},{12,8},{16,20},{20,16},{24,28},{28,24},{1,5},{5... | collective-permute-start | bytes 737288 | tf_op jit(solution)/shard_map/ppermute | solution.py:279
  26.0 5.1 %collective-permute-start.11 = (bf16[3,32,1280]{2,1,0:T(8,128)(2,1)S(1)}, bf16[3,32,1280]{2,1,0:T(8,128)(2,1)S(1)}, u32[]{:S(2)}, u32[]{:S(2)}) collective-permute-start(bf16[3,32,1280]{2,1,0:T(8,128)(2,1)S(1)} %join.3), channel_id=1, source_target_pairs={{0,4},{4,0},{8,12},{12,8},{16,20},{20,16},{24,28},{28,24},{1,5},{5... | collective-permute-start | bytes 737288 | tf_op jit(solution)/shard_map/ppermute | solution.py:279
  26.1 5.0 %collective-permute-start.10 = (bf16[32,1280]{1,0:T(8,128)(2,1)S(1)}, bf16[32,1280]{1,0:T(8,128)(2,1)S(1)}, u32[]{:S(2)}, u32[]{:S(2)}) collective-permute-start(bf16[32,1280]{1,0:T(8,128)(2,1)S(1)} %slice_bitcast_fusion), channel_id=1, source_target_pairs={{0,4},{4,0},{8,12},{12,8},{16,20},{20,16},{24,28},{28,24},{1,5},{5... | collective-permute-start | bytes 245768 | tf_op jit(solution)/shard_map/ppermute | solution.py:279
  26.6 3.5 %copy-start.2 = (bf16[1280,1280]{1,0:T(8,128)(2,1)S(1)}, bf16[1280,1280]{1,0:T(8,128)(2,1)}, u32[]{:S(2)}) copy-start(bf16[1280,1280]{1,0:T(8,128)(2,1)} %wv_ref.3) | copy-start | bytes 9830404
  36.2 4.5 %collective-permute-start.16 = (bf16[32,1280]{1,0:T(8,128)(2,1)S(1)}, bf16[32,1280]{1,0:T(8,128)(2,1)S(1)}, u32[]{:S(2)}, u32[]{:S(2)}) collective-permute-start(bf16[32,1280]{1,0:T(8,128)(2,1)S(1)} %get-tuple-element.48), channel_id=1, source_target_pairs={{0,4},{4,0},{8,12},{12,8},{16,20},{20,16},{24,28},{28,24},{1,5},{5... | collective-permute-start | bytes 245768 | tf_op jit(solution)/shard_map/ppermute | solution.py:279
  36.4 6.2 %collective-permute-start.17 = (bf16[32,1280]{1,0:T(8,128)(2,1)S(1)}, bf16[32,1280]{1,0:T(8,128)(2,1)S(1)}, u32[]{:S(2)}, u32[]{:S(2)}) collective-permute-start(bf16[32,1280]{1,0:T(8,128)(2,1)S(1)} %get-tuple-element.49), channel_id=1, source_target_pairs={{0,24},{4,28},{8,16},{12,20},{16,8},{20,12},{24,0},{28,4},{1,25},{... | collective-permute-start | bytes 245768 | tf_op jit(solution)/shard_map/ppermute | solution.py:279
  37.2 6.0 %collective-permute-start.18 = (bf16[32,1280]{1,0:T(8,128)(2,1)S(1)}, bf16[32,1280]{1,0:T(8,128)(2,1)S(1)}, u32[]{:S(2)}, u32[]{:S(2)}) collective-permute-start(bf16[32,1280]{1,0:T(8,128)(2,1)S(1)} %get-tuple-element.50), channel_id=1, source_target_pairs={{0,28},{4,24},{8,20},{12,16},{16,12},{20,8},{24,4},{28,0},{1,29},{... | collective-permute-start | bytes 245768 | tf_op jit(solution)/shard_map/ppermute | solution.py:279
  39.0 6.6 %collective-permute-start.12 = (bf16[32,1280]{1,0:T(8,128)(2,1)S(1)}, bf16[32,1280]{1,0:T(8,128)(2,1)S(1)}, u32[]{:S(2)}, u32[]{:S(2)}) collective-permute-start(bf16[32,1280]{1,0:T(8,128)(2,1)S(1)} %get-tuple-element.43), channel_id=1, source_target_pairs={{0,8},{4,12},{8,0},{12,4},{16,24},{20,28},{24,16},{28,20},{1,9},{5... | collective-permute-start | bytes 245768 | tf_op jit(solution)/shard_map/ppermute | solution.py:279
  39.6 6.7 %collective-permute-start.13 = (bf16[32,1280]{1,0:T(8,128)(2,1)S(1)}, bf16[32,1280]{1,0:T(8,128)(2,1)S(1)}, u32[]{:S(2)}, u32[]{:S(2)}) collective-permute-start(bf16[32,1280]{1,0:T(8,128)(2,1)S(1)} %get-tuple-element.44), channel_id=1, source_target_pairs={{0,12},{4,8},{8,4},{12,0},{16,28},{20,24},{24,20},{28,16},{1,13},{... | collective-permute-start | bytes 245768 | tf_op jit(solution)/shard_map/ppermute | solution.py:279
  40.7 5.6 %collective-permute-start.14 = (bf16[32,1280]{1,0:T(8,128)(2,1)S(1)}, bf16[32,1280]{1,0:T(8,128)(2,1)S(1)}, u32[]{:S(2)}, u32[]{:S(2)}) collective-permute-start(bf16[32,1280]{1,0:T(8,128)(2,1)S(1)} %get-tuple-element.45), channel_id=1, source_target_pairs={{0,16},{4,20},{8,24},{12,28},{16,0},{20,4},{24,8},{28,12},{1,17},{... | collective-permute-start | bytes 245768 | tf_op jit(solution)/shard_map/ppermute | solution.py:279
  42.6 4.7 %collective-permute-start.15 = (bf16[32,1280]{1,0:T(8,128)(2,1)S(1)}, bf16[32,1280]{1,0:T(8,128)(2,1)S(1)}, u32[]{:S(2)}, u32[]{:S(2)}) collective-permute-start(bf16[32,1280]{1,0:T(8,128)(2,1)S(1)} %get-tuple-element.46), channel_id=1, source_target_pairs={{0,20},{4,16},{8,28},{12,24},{16,4},{20,0},{24,12},{28,8},{1,21},{... | collective-permute-start | bytes 245768 | tf_op jit(solution)/shard_map/ppermute | solution.py:279

commit v8 on v7

--- a/solution.py
+++ b/solution.py
@@ -394,7 +394,7 @@
         out_shape=[low((rows, channels))] * 2
         + [pltpu.VMEM((heads, frames, rows), jnp.float32), low((rows, channels))],
         scratch_shapes=[pltpu.VMEM((rows, channels), jnp.float32)],
-        compiler_params=grant(20),
+        compiler_params=pltpu.CompilerParams(vmem_limit_bytes=20 << 20),
         name="forward",
     )(me_arg, order, conv_taps, conv_bias, *weights[:2], *map(on_chip, token_blocks))
     value = pl.pallas_call(
@@ -419,8 +419,8 @@
         name="backward",
     )(me_arg, order, conv_taps, *weights, *map(on_chip, (query, key, value, prob)), *map(on_chip, grad_blocks))
     received = [block.reshape(frame_rows, toks, channels) for block in spread_frames(results)]
-    early = [mask for mask in range(peers) if bin(mask >> 1).count("1") != 1]
-    late = [mask for mask in range(peers) if mask not in early]
+    late = far_first(peers)[-3:-1]
+    early = [mask for mask in range(peers) if mask not in late]
     output = None
     for masks in (early, late):
         blocks = [on_chip(received[mask]) for mask in masks]

time: 48.2 us -> 47.5 us (0.985)
  waiting for transfers between devices: 13.6 us -> 12.5 us
  starting transfers between devices: 20.7 us -> 21.2 us
    ppermute x19, waiting for transfers between devices: 13.6 us -> 12.5 us  [swap(): lax.ppermute(value, axis, [(i, i ^ mask) for i in range(lax.axis_size(axi...]
  transfers between devices with their start and end apart: 19 -> 19, of which waited for: 10 -> 8; matrix products, arithmetic and copies ran while one was open for 0% -> 0% of each run, Pallas kernels for 13% -> 14%
where the time goes in v8:
time: 47.5 us; the launch traced here: 47.4 us
  starting transfers between devices  21.2 us (45%)
  Pallas kernels  13.5 us (28%)
  waiting for transfers between devices  12.5 us (26%)
    ppermute x19, starting transfers between devices, swap(): lax.ppermute(value, axis, [(i, i ^ mask) for i in range(lax.axis_size(axi...  21.2 us
    ppermute x19, waiting for transfers between devices, swap(): lax.ppermute(value, axis, [(i, i ^ mask) for i in range(lax.axis_size(axi...  12.5 us
    pallas_call x1, Pallas kernels, body(): pl.pallas_call(functools.partial(backward_kernel, **sizes), in_specs=[sme...  5.05 us
    pallas_call x1, Pallas kernels, body(): pl.pallas_call(functools.partial(forward_kernel, **sizes), in_specs=[smem...  3.46 us
    pallas_call x2, Pallas kernels, body(): pl.pallas_call(functools.partial(place_kernel, masks=masks), in_specs=[sm...  1.5 us
    pallas_call x1, Pallas kernels, body(): pl.pallas_call(functools.partial(pack_kernel, peers=peers), in_specs=[sme...  1.32 us
    pallas_call x1, Pallas kernels, body(): pl.pallas_call(value_kernel, in_specs=[vmem] * 2, out_specs=vmem, out_sha...  1.02 us
  transfers between devices with their start and end apart: 19, of which 8 were waited for; matrix products, arithmetic and copies ran while one was open for 0% of the time, Pallas kernels for 14%

profile of v8, /device:TPU:0, one launch (start us, length us, event | category | flops | bytes accessed | tf_op | source)
XLA Modules:
  0.0 47.4 jit_solution(17248361742211948576)
XLA Ops:
  0.0 1.3 %pack.1 = (bf16[2,4,8,1280]{3,2,1,0:T(8,128)(2,1)S(1)}, bf16[2,4,8,1280]{3,2,1,0:T(8,128)(2,1)S(1)}, bf16[2,4,8,1280]{3,2,1,0:T(8,128)(2,1)S(1)}, f32[4,128]{1,0:T(4,128)S(1)}, bf16[4,8,8,1280]{3,2,1,0:T(8,128)(2,1)S(1)}) custom-call(s32[1]{0:T(128)} %bitcast.me_ref, bf16[4,8,8,1280]{3,2,1,0:T(8,128)(2,1)} %bitcast.46, bf16[4,8,8,1280]{3,2,1,0:T(8,128)(2,1)} %bitcast.48), custom_call_target="tpu_custom_call" | custom-call | tf_op jit(solution)/shard_map/pack/pallas_call | solution.py:354
  1.3 3.1 %collective-permute-start.5 = (f32[4,128]{1,0:T(4,128)S(1)}, f32[4,128]{1,0:T(4,128)S(1)}, u32[]{:S(2)}, u32[]{:S(2)}) collective-permute-start(f32[4,128]{1,0:T(4,128)S(1)} %get-tuple-element.38), channel_id=1, source_target_pairs={{0,1},{1,0},{2,3},{3,2},{4,5},{5,4},{6,7},{7,6},{8,9},{9,8},{10,11... | collective-permute-start | bytes 6152 | tf_op jit(solution)/shard_map/ppermute | solution.py:279
  4.5 1.6 %collective-permute-done.5 = f32[4,128]{1,0:T(4,128)S(1)} collective-permute-done((f32[4,128]{1,0:T(4,128)S(1)}, f32[4,128]{1,0:T(4,128)S(1)}, u32[]{:S(2)}, u32[]{:S(2)}) %collective-permute-start.5) | collective-permute-done | bytes 2080 | tf_op jit(solution)/shard_map/ppermute | solution.py:279
  6.0 3.0 %collective-permute-start.6 = (f32[4,128]{1,0:T(4,128)S(1)}, f32[4,128]{1,0:T(4,128)S(1)}, u32[]{:S(2)}, u32[]{:S(2)}) collective-permute-start(f32[4,128]{1,0:T(4,128)S(1)} %add.3.refs_0_), channel_id=1, source_target_pairs={{0,2},{1,3},{2,0},{3,1},{4,6},{5,7},{6,4},{7,5},{8,10},{9,11},{10,... | collective-permute-start | bytes 6152 | tf_op jit(solution)/shard_map/ppermute | solution.py:279
  9.1 1.5 %collective-permute-start = (bf16[2,4,8,1280]{3,2,1,0:T(8,128)(2,1)S(1)}, bf16[2,4,8,1280]{3,2,1,0:T(8,128)(2,1)S(1)}, u32[]{:S(2)}, u32[]{:S(2)}) collective-permute-start(bf16[2,4,8,1280]{3,2,1,0:T(8,128)(2,1)S(1)} %get-tuple-element.30), channel_id=1, source_target_pairs={{0,8},{4,12},{8,0},{12,4},{16,24},{20,28},{24,16},{28,20},{1,9},{5... | collective-permute-start | bytes 491528 | tf_op jit(solution)/shard_map/ppermute | solution.py:279
  10.5 1.5 %collective-permute-start.1 = (bf16[2,4,8,1280]{3,2,1,0:T(8,128)(2,1)S(1)}, bf16[2,4,8,1280]{3,2,1,0:T(8,128)(2,1)S(1)}, u32[]{:S(2)}, u32[]{:S(2)}) collective-permute-start(bf16[2,4,8,1280]{3,2,1,0:T(8,128)(2,1)S(1)} %get-tuple-element.31), channel_id=1, source_target_pairs={{0,16},{4,20},{8,24},{12,28},{16,0},{20,4},{24,8},{28,12},{1,17},{... | collective-permute-start | bytes 491528 | tf_op jit(solution)/shard_map/ppermute | solution.py:279
  12.1 0.5 %collective-permute-start.2 = (bf16[2,4,8,1280]{3,2,1,0:T(8,128)(2,1)S(1)}, bf16[2,4,8,1280]{3,2,1,0:T(8,128)(2,1)S(1)}, u32[]{:S(2)}, u32[]{:S(2)}) collective-permute-start(bf16[2,4,8,1280]{3,2,1,0:T(8,128)(2,1)S(1)} %get-tuple-element.32), channel_id=1, source_target_pairs={{0,24},{4,28},{8,16},{12,20},{16,8},{20,12},{24,0},{28,4},{1,25},{... | collective-permute-start | bytes 491528 | tf_op jit(solution)/shard_map/ppermute | solution.py:279
  12.5 0.9 %prepare.1 = (bf16[2,4,8,1280]{3,2,1,0:T(8,128)(2,1)S(1)}, bf16[2,256,256]{2,1,0:T(8,128)(2,1)S(1)}) custom-call(s32[1]{0:T(128)} %bitcast.me_ref, bf16[4,8,8,1280]{3,2,1,0:T(8,128)(2,1)} %bitcast.47), custom_call_target="tpu_custom_call" | custom-call | tf_op jit(solution)/shard_map/prepare/pallas_call | solution.py:364
  13.6 0.2 scale.1
  13.7 1.6 %collective-permute-start.7 = (bf16[2,4,8,1280]{3,2,1,0:T(8,128)(2,1)S(1)}, bf16[2,4,8,1280]{3,2,1,0:T(8,128)(2,1)S(1)}, u32[]{:S(2)}, u32[]{:S(2)}) collective-permute-start(bf16[2,4,8,1280]{3,2,1,0:T(8,128)(2,1)S(1)} %get-tuple-element.40), channel_id=1, source_target_pairs={{0,8},{4,12},{8,0},{12,4},{16,24},{20,28},{24,16},{28,20},{1,9},{5... | collective-permute-start | bytes 491528 | tf_op jit(solution)/shard_map/ppermute | solution.py:279
  15.3 1.5 %collective-permute-start.8 = (bf16[2,4,8,1280]{3,2,1,0:T(8,128)(2,1)S(1)}, bf16[2,4,8,1280]{3,2,1,0:T(8,128)(2,1)S(1)}, u32[]{:S(2)}, u32[]{:S(2)}) collective-permute-start(bf16[2,4,8,1280]{3,2,1,0:T(8,128)(2,1)S(1)} %get-tuple-element.41), channel_id=1, source_target_pairs={{0,16},{4,20},{8,24},{12,28},{16,0},{20,4},{24,8},{28,12},{1,17},{... | collective-permute-start | bytes 491528 | tf_op jit(solution)/shard_map/ppermute | solution.py:279
  16.8 1.8 %collective-permute-start.9 = (bf16[2,4,8,1280]{3,2,1,0:T(8,128)(2,1)S(1)}, bf16[2,4,8,1280]{3,2,1,0:T(8,128)(2,1)S(1)}, u32[]{:S(2)}, u32[]{:S(2)}) collective-permute-start(bf16[2,4,8,1280]{3,2,1,0:T(8,128)(2,1)S(1)} %get-tuple-element.42), channel_id=1, source_target_pairs={{0,24},{4,28},{8,16},{12,20},{16,8},{20,12},{24,0},{28,4},{1,25},{... | collective-permute-start | bytes 491528 | tf_op jit(solution)/shard_map/ppermute | solution.py:279
  18.6 1.2 %collective-permute-done.1 = bf16[2,4,8,1280]{3,2,1,0:T(8,128)(2,1)S(1)} collective-permute-done((bf16[2,4,8,1280]{3,2,1,0:T(8,128)(2,1)S(1)}, bf16[2,4,8,1280]{3,2,1,0:T(8,128)(2,1)S(1)}, u32[]{:S(2)}, u32[]{:S(2)}) %collective-permute-start.1) | collective-permute-done | bytes 163872 | tf_op jit(solution)/shard_map/ppermute | solution.py:279
  19.7 0.9 %collective-permute-done.2 = bf16[2,4,8,1280]{3,2,1,0:T(8,128)(2,1)S(1)} collective-permute-done((bf16[2,4,8,1280]{3,2,1,0:T(8,128)(2,1)S(1)}, bf16[2,4,8,1280]{3,2,1,0:T(8,128)(2,1)S(1)}, u32[]{:S(2)}, u32[]{:S(2)}) %collective-permute-start.2) | collective-permute-done | bytes 163872 | tf_op jit(solution)/shard_map/ppermute | solution.py:279
  20.7 0.1 collective-permute-start.4
  20.8 2.2 %collective-permute-done.7 = bf16[2,4,8,1280]{3,2,1,0:T(8,128)(2,1)S(1)} collective-permute-done((bf16[2,4,8,1280]{3,2,1,0:T(8,128)(2,1)S(1)}, bf16[2,4,8,1280]{3,2,1,0:T(8,128)(2,1)S(1)}, u32[]{:S(2)}, u32[]{:S(2)}) %collective-permute-start.7) | collective-permute-done | bytes 163872 | tf_op jit(solution)/shard_map/ppermute | solution.py:279
  23.0 3.0 %collective-permute-done.8 = bf16[2,4,8,1280]{3,2,1,0:T(8,128)(2,1)S(1)} collective-permute-done((bf16[2,4,8,1280]{3,2,1,0:T(8,128)(2,1)S(1)}, bf16[2,4,8,1280]{3,2,1,0:T(8,128)(2,1)S(1)}, u32[]{:S(2)}, u32[]{:S(2)}) %collective-permute-start.8) | collective-permute-done | bytes 163872 | tf_op jit(solution)/shard_map/ppermute | solution.py:279
  26.1 0.5 %collective-permute-start.10 = (bf16[32,1280]{1,0:T(8,128)(2,1)S(1)}, bf16[32,1280]{1,0:T(8,128)(2,1)S(1)}, u32[]{:S(2)}, u32[]{:S(2)}) collective-permute-start(bf16[32,1280]{1,0:T(8,128)(2,1)S(1)} %slice_bitcast_fusion), channel_id=1, source_target_pairs={{0,4},{4,0},{8,12},{12,8},{16,20},{20,16},{24,28},{28,24},{1,5},{5... | collective-permute-start | bytes 245768 | tf_op jit(solution)/shard_map/ppermute | solution.py:279
  26.6 3.5 %forward.1 = (bf16[256,1280]{1,0:T(8,128)(2,1)S(1)}, bf16[256,1280]{1,0:T(8,128)(2,1)S(1)}, f32[20,32,256]{2,1,0:T(8,128)S(1)}, bf16[256,1280]{1,0:T(8,128)(2,1)S(1)}) custom-call(s32[1]{0:T(128)} %bitcast.me_ref, bf16[2,256,256]{2,1,0:T(8,128)(2,1)S(1)} %get-tuple-element.28.order_ref, f32[3,1280]{1,0:T(4,128)S(1)} %copy-done.3, f32[1280]{0:T(1024)S(1)} %copy-done.4, ...), custom_call_target="tpu_custom_call" | custom-call | tf_op jit(solution)/shard_map/forward/pallas_call | solution.py:390
  30.1 1.0 %value.1.v_ref = bf16[256,1280]{1,0:T(8,128)(2,1)S(1)} custom-call(bf16[256,1280]{1,0:T(8,128)(2,1)S(1)} %get-tuple-element.35.hidden_ref, bf16[1280,1280]{1,0:T(8,128)(2,1)S(1)} %copy-done.2), custom_call_target="tpu_custom_call" | custom-call | tf_op jit(solution)/shard_map/value/pallas_call | solution.py:400
  31.1 5.1 %backward.1 = (bf16[32,1280]{1,0:T(8,128)(2,1)S(1)}, bf16[32,1280]{1,0:T(8,128)(2,1)S(1)}, bf16[32,1280]{1,0:T(8,128)(2,1)S(1)}, bf16[32,1280]{1,0:T(8,128)(2,1)...) custom-call(s32[1]{0:T(128)} %bitcast.me_ref, ...), custom_call_target="tpu_custom_call" | custom-call | tf_op jit(solution)/shard_map/backward/pallas_call | solution.py:408
  36.2 0.1 collective-permute-start.14
  36.4 0.6 %collective-permute-start.15 = (bf16[32,1280]{1,0:T(8,128)(2,1)S(1)}, bf16[32,1280]{1,0:T(8,128)(2,1)S(1)}, u32[]{:S(2)}, u32[]{:S(2)}) collective-permute-start(bf16[32,1280]{1,0:T(8,128)(2,1)S(1)} %get-tuple-element.47), channel_id=1, source_target_pairs={{0,8},{4,12},{8,0},{12,4},{16,24},{20,28},{24,16},{28,20},{1,9},{5... | collective-permute-start | bytes 245768 | tf_op jit(solution)/shard_map/ppermute | solution.py:279
  37.0 0.8 %collective-permute-start.16 = (bf16[32,1280]{1,0:T(8,128)(2,1)S(1)}, bf16[32,1280]{1,0:T(8,128)(2,1)S(1)}, u32[]{:S(2)}, u32[]{:S(2)}) collective-permute-start(bf16[32,1280]{1,0:T(8,128)(2,1)S(1)} %get-tuple-element.48), channel_id=1, source_target_pairs={{0,16},{4,20},{8,24},{12,28},{16,0},{20,4},{24,8},{28,12},{1,17},{... | collective-permute-start | bytes 245768 | tf_op jit(solution)/shard_map/ppermute | solution.py:279
  37.8 2.1 %collective-permute-start.17 = (bf16[32,1280]{1,0:T(8,128)(2,1)S(1)}, bf16[32,1280]{1,0:T(8,128)(2,1)S(1)}, u32[]{:S(2)}, u32[]{:S(2)}) collective-permute-start(bf16[32,1280]{1,0:T(8,128)(2,1)S(1)} %get-tuple-element.49), channel_id=1, source_target_pairs={{0,24},{4,28},{8,16},{12,20},{16,8},{20,12},{24,0},{28,4},{1,25},{... | collective-permute-start | bytes 245768 | tf_op jit(solution)/shard_map/ppermute | solution.py:279
  39.9 1.8 %collective-permute-start.12 = (bf16[32,1280]{1,0:T(8,128)(2,1)S(1)}, bf16[32,1280]{1,0:T(8,128)(2,1)S(1)}, u32[]{:S(2)}, u32[]{:S(2)}) collective-permute-start(bf16[32,1280]{1,0:T(8,128)(2,1)S(1)} %get-tuple-element.43), channel_id=1, source_target_pairs={{0,20},{4,16},{8,28},{12,24},{16,4},{20,0},{24,12},{28,8},{1,21},{... | collective-permute-start | bytes 245768 | tf_op jit(solution)/shard_map/ppermute | solution.py:279
  41.7 0.6 %collective-permute-start.13 = (bf16[32,1280]{1,0:T(8,128)(2,1)S(1)}, bf16[32,1280]{1,0:T(8,128)(2,1)S(1)}, u32[]{:S(2)}, u32[]{:S(2)}) collective-permute-start(bf16[32,1280]{1,0:T(8,128)(2,1)S(1)} %get-tuple-element.44), channel_id=1, source_target_pairs={{0,12},{4,8},{8,4},{12,0},{16,28},{20,24},{24,20},{28,16},{1,13},{... | collective-permute-start | bytes 245768 | tf_op jit(solution)/shard_map/ppermute | solution.py:279
  42.3 1.1 %collective-permute-done.17 = bf16[32,1280]{1,0:T(8,128)(2,1)S(1)} collective-permute-done((bf16[32,1280]{1,0:T(8,128)(2,1)S(1)}, bf16[32,1280]{1,0:T(8,128)(2,1)S(1)}, u32[]{:S(2)}, u32[]{:S(2)}) %collective-permute-start.17) | collective-permute-done | bytes 81952 | tf_op jit(solution)/shard_map/ppermute | solution.py:279
  43.4 2.1 %collective-permute-done.18 = bf16[32,1280]{1,0:T(8,128)(2,1)S(1)} collective-permute-done((bf16[32,1280]{1,0:T(8,128)(2,1)S(1)}, bf16[32,1280]{1,0:T(8,128)(2,1)S(1)}, u32[]{:S(2)}, u32[]{:S(2)}) %collective-permute-start.18) | collective-permute-done | bytes 81952 | tf_op jit(solution)/shard_map/ppermute | solution.py:279
  45.4 0.8 %place.2.refs_2_ = bf16[4,8,8,1280]{3,2,1,0:T(8,128)(2,1)} custom-call(s32[1]{0:T(128)} %bitcast.me_ref, bf16[4,8,1280]{2,1,0:T(8,128)(2,1)S(1)} %bitcast.38, bf16[4,8,1280]{2,1,0:T(8,128)(2,1)S(1)} %bitcast.39, bf16[4,8,1280]{2,1,0:T(8,128)(2,1)S(1)} %bitcast.40, bf16[4,8,1280]{2,1,0:T(8,128)(2,1)S(1)} %bitcast.41, bf16[4,8,1280]{2,1,0:T(8,128)(2,1)S(1)} %bitcast.42, ...), custom_call_target="tpu_custom_call" | custom-call | tf_op jit(solution)/shard_map/place/pallas_call | solution.py:427
  46.3 0.4 collective-permute-done.12
  46.7 0.7 %place.3 = bf16[4,8,8,1280]{3,2,1,0:T(8,128)(2,1)} custom-call(s32[1]{0:T(128)} %bitcast.me_ref, bf16[4,8,1280]{2,1,0:T(8,128)(2,1)S(1)} %bitcast.44, bf16[4,8,1280]{2,1,0:T(8,128)(2,1)S(1)} %bitcast.45, bf16[4,8,8,1280]{3,2,1,0:T(8,128)(2,1)} %place.2.refs_2_), custom_call_target="tpu_custom_call", output_to_operand_aliasing={{}: (3, {})} | custom-call | tf_op jit(solution)/shard_map/place/pallas_call | solution.py:427
  (29 shorter events, 0.2 us)
Async XLA Ops:
  1.3 4.7 %collective-permute-start.5 = (f32[4,128]{1,0:T(4,128)S(1)}, f32[4,128]{1,0:T(4,128)S(1)}, u32[]{:S(2)}, u32[]{:S(2)}) collective-permute-start(f32[4,128]{1,0:T(4,128)S(1)} %get-tuple-element.38), channel_id=1, source_target_pairs={{0,1},{1,0},{2,3},{3,2},{4,5},{5,4},{6,7},{7,6},{8,9},{9,8},{10,11... | collective-permute-start | bytes 6152 | tf_op jit(solution)/shard_map/ppermute | solution.py:279
  6.0 7.5 %collective-permute-start.6 = (f32[4,128]{1,0:T(4,128)S(1)}, f32[4,128]{1,0:T(4,128)S(1)}, u32[]{:S(2)}, u32[]{:S(2)}) collective-permute-start(f32[4,128]{1,0:T(4,128)S(1)} %add.3.refs_0_), channel_id=1, source_target_pairs={{0,2},{1,3},{2,0},{3,1},{4,6},{5,7},{6,4},{7,5},{8,10},{9,11},{10,... | collective-permute-start | bytes 6152 | tf_op jit(solution)/shard_map/ppermute | solution.py:279
  9.1 7.7 %collective-permute-start = (bf16[2,4,8,1280]{3,2,1,0:T(8,128)(2,1)S(1)}, bf16[2,4,8,1280]{3,2,1,0:T(8,128)(2,1)S(1)}, u32[]{:S(2)}, u32[]{:S(2)}) collective-permute-start(bf16[2,4,8,1280]{3,2,1,0:T(8,128)(2,1)S(1)} %get-tuple-element.30), channel_id=1, source_target_pairs={{0,8},{4,12},{8,0},{12,4},{16,24},{20,28},{24,16},{28,20},{1,9},{5... | collective-permute-start | bytes 491528 | tf_op jit(solution)/shard_map/ppermute | solution.py:279
  10.5 9.2 %collective-permute-start.1 = (bf16[2,4,8,1280]{3,2,1,0:T(8,128)(2,1)S(1)}, bf16[2,4,8,1280]{3,2,1,0:T(8,128)(2,1)S(1)}, u32[]{:S(2)}, u32[]{:S(2)}) collective-permute-start(bf16[2,4,8,1280]{3,2,1,0:T(8,128)(2,1)S(1)} %get-tuple-element.31), channel_id=1, source_target_pairs={{0,16},{4,20},{8,24},{12,28},{16,0},{20,4},{24,8},{28,12},{1,17},{... | collective-permute-start | bytes 491528 | tf_op jit(solution)/shard_map/ppermute | solution.py:279
  12.1 8.6 %collective-permute-start.2 = (bf16[2,4,8,1280]{3,2,1,0:T(8,128)(2,1)S(1)}, bf16[2,4,8,1280]{3,2,1,0:T(8,128)(2,1)S(1)}, u32[]{:S(2)}, u32[]{:S(2)}) collective-permute-start(bf16[2,4,8,1280]{3,2,1,0:T(8,128)(2,1)S(1)} %get-tuple-element.32), channel_id=1, source_target_pairs={{0,24},{4,28},{8,16},{12,20},{16,8},{20,12},{24,0},{28,4},{1,25},{... | collective-permute-start | bytes 491528 | tf_op jit(solution)/shard_map/ppermute | solution.py:279
  13.5 13.1 %copy-start = (bf16[1280,1280]{1,0:T(8,128)(2,1)S(1)}, bf16[1280,1280]{1,0:T(8,128)(2,1)}, u32[]{:S(2)}) copy-start(bf16[1280,1280]{1,0:T(8,128)(2,1)} %wq_ref.3) | copy-start | bytes 9830404
  13.5 13.1 %copy-start.1 = (bf16[1280,1280]{1,0:T(8,128)(2,1)S(1)}, bf16[1280,1280]{1,0:T(8,128)(2,1)}, u32[]{:S(2)}) copy-start(bf16[1280,1280]{1,0:T(8,128)(2,1)} %wk_ref.3) | copy-start | bytes 9830404
  13.5 13.1 %copy-start.3 = (f32[3,1280]{1,0:T(4,128)S(1)}, f32[3,1280]{1,0:T(4,128)}, u32[]{:S(2)}) copy-start(f32[3,1280]{1,0:T(4,128)} %taps_ref.3) | copy-start | bytes 46084
  13.5 13.1 %copy-start.4 = (f32[1280]{0:T(1024)S(1)}, f32[1280]{0:T(1024)}, u32[]{:S(2)}) copy-start(f32[1280]{0:T(1024)} %bias_ref.1) | copy-start | bytes 15364
  13.7 9.3 %collective-permute-start.7 = (bf16[2,4,8,1280]{3,2,1,0:T(8,128)(2,1)S(1)}, bf16[2,4,8,1280]{3,2,1,0:T(8,128)(2,1)S(1)}, u32[]{:S(2)}, u32[]{:S(2)}) collective-permute-start(bf16[2,4,8,1280]{3,2,1,0:T(8,128)(2,1)S(1)} %get-tuple-element.40), channel_id=1, source_target_pairs={{0,8},{4,12},{8,0},{12,4},{16,24},{20,28},{24,16},{28,20},{1,9},{5... | collective-permute-start | bytes 491528 | tf_op jit(solution)/shard_map/ppermute | solution.py:279
  15.3 10.7 %collective-permute-start.8 = (bf16[2,4,8,1280]{3,2,1,0:T(8,128)(2,1)S(1)}, bf16[2,4,8,1280]{3,2,1,0:T(8,128)(2,1)S(1)}, u32[]{:S(2)}, u32[]{:S(2)}) collective-permute-start(bf16[2,4,8,1280]{3,2,1,0:T(8,128)(2,1)S(1)} %get-tuple-element.41), channel_id=1, source_target_pairs={{0,16},{4,20},{8,24},{12,28},{16,0},{20,4},{24,8},{28,12},{1,17},{... | collective-permute-start | bytes 491528 | tf_op jit(solution)/shard_map/ppermute | solution.py:279
  16.8 9.2 %collective-permute-start.9 = (bf16[2,4,8,1280]{3,2,1,0:T(8,128)(2,1)S(1)}, bf16[2,4,8,1280]{3,2,1,0:T(8,128)(2,1)S(1)}, u32[]{:S(2)}, u32[]{:S(2)}) collective-permute-start(bf16[2,4,8,1280]{3,2,1,0:T(8,128)(2,1)S(1)} %get-tuple-element.42), channel_id=1, source_target_pairs={{0,24},{4,28},{8,16},{12,20},{16,8},{20,12},{24,0},{28,4},{1,25},{... | collective-permute-start | bytes 491528 | tf_op jit(solution)/shard_map/ppermute | solution.py:279
  19.7 6.8 %collective-permute-start.3 = (bf16[32,1280]{1,0:T(8,128)(2,1)S(1)}, bf16[32,1280]{1,0:T(8,128)(2,1)S(1)}, u32[]{:S(2)}, u32[]{:S(2)}) collective-permute-start(bf16[32,1280]{1,0:T(8,128)(2,1)S(1)} %slice_bitcast_fusion.1), channel_id=1, source_target_pairs={{0,4},{4,0},{8,12},{12,8},{16,20},{20,16},{24,28},{28,24},{1,5},{5... | collective-permute-start | bytes 245768 | tf_op jit(solution)/shard_map/ppermute | solution.py:279
  20.7 5.9 %collective-permute-start.4 = (bf16[3,32,1280]{2,1,0:T(8,128)(2,1)S(1)}, bf16[3,32,1280]{2,1,0:T(8,128)(2,1)S(1)}, u32[]{:S(2)}, u32[]{:S(2)}) collective-permute-start(bf16[3,32,1280]{2,1,0:T(8,128)(2,1)S(1)} %join.2), channel_id=1, source_target_pairs={{0,4},{4,0},{8,12},{12,8},{16,20},{20,16},{24,28},{28,24},{1,5},{5... | collective-permute-start | bytes 737288 | tf_op jit(solution)/shard_map/ppermute | solution.py:279
  26.0 5.1 %collective-permute-start.11 = (bf16[3,32,1280]{2,1,0:T(8,128)(2,1)S(1)}, bf16[3,32,1280]{2,1,0:T(8,128)(2,1)S(1)}, u32[]{:S(2)}, u32[]{:S(2)}) collective-permute-start(bf16[3,32,1280]{2,1,0:T(8,128)(2,1)S(1)} %join.3), channel_id=1, source_target_pairs={{0,4},{4,0},{8,12},{12,8},{16,20},{20,16},{24,28},{28,24},{1,5},{5... | collective-permute-start | bytes 737288 | tf_op jit(solution)/shard_map/ppermute | solution.py:279
  26.1 5.0 %collective-permute-start.10 = (bf16[32,1280]{1,0:T(8,128)(2,1)S(1)}, bf16[32,1280]{1,0:T(8,128)(2,1)S(1)}, u32[]{:S(2)}, u32[]{:S(2)}) collective-permute-start(bf16[32,1280]{1,0:T(8,128)(2,1)S(1)} %slice_bitcast_fusion), channel_id=1, source_target_pairs={{0,4},{4,0},{8,12},{12,8},{16,20},{20,16},{24,28},{28,24},{1,5},{5... | collective-permute-start | bytes 245768 | tf_op jit(solution)/shard_map/ppermute | solution.py:279
  26.6 3.5 %copy-start.2 = (bf16[1280,1280]{1,0:T(8,128)(2,1)S(1)}, bf16[1280,1280]{1,0:T(8,128)(2,1)}, u32[]{:S(2)}) copy-start(bf16[1280,1280]{1,0:T(8,128)(2,1)} %wv_ref.3) | copy-start | bytes 9830404
  36.2 3.7 %collective-permute-start.14 = (bf16[32,1280]{1,0:T(8,128)(2,1)S(1)}, bf16[32,1280]{1,0:T(8,128)(2,1)S(1)}, u32[]{:S(2)}, u32[]{:S(2)}) collective-permute-start(bf16[32,1280]{1,0:T(8,128)(2,1)S(1)} %get-tuple-element.46), channel_id=1, source_target_pairs={{0,4},{4,0},{8,12},{12,8},{16,20},{20,16},{24,28},{28,24},{1,5},{5... | collective-permute-start | bytes 245768 | tf_op jit(solution)/shard_map/ppermute | solution.py:279
  36.4 5.3 %collective-permute-start.15 = (bf16[32,1280]{1,0:T(8,128)(2,1)S(1)}, bf16[32,1280]{1,0:T(8,128)(2,1)S(1)}, u32[]{:S(2)}, u32[]{:S(2)}) collective-permute-start(bf16[32,1280]{1,0:T(8,128)(2,1)S(1)} %get-tuple-element.47), channel_id=1, source_target_pairs={{0,8},{4,12},{8,0},{12,4},{16,24},{20,28},{24,16},{28,20},{1,9},{5... | collective-permute-start | bytes 245768 | tf_op jit(solution)/shard_map/ppermute | solution.py:279
  37.0 5.3 %collective-permute-start.16 = (bf16[32,1280]{1,0:T(8,128)(2,1)S(1)}, bf16[32,1280]{1,0:T(8,128)(2,1)S(1)}, u32[]{:S(2)}, u32[]{:S(2)}) collective-permute-start(bf16[32,1280]{1,0:T(8,128)(2,1)S(1)} %get-tuple-element.48), channel_id=1, source_target_pairs={{0,16},{4,20},{8,24},{12,28},{16,0},{20,4},{24,8},{28,12},{1,17},{... | collective-permute-start | bytes 245768 | tf_op jit(solution)/shard_map/ppermute | solution.py:279
  37.8 5.6 %collective-permute-start.17 = (bf16[32,1280]{1,0:T(8,128)(2,1)S(1)}, bf16[32,1280]{1,0:T(8,128)(2,1)S(1)}, u32[]{:S(2)}, u32[]{:S(2)}) collective-permute-start(bf16[32,1280]{1,0:T(8,128)(2,1)S(1)} %get-tuple-element.49), channel_id=1, source_target_pairs={{0,24},{4,28},{8,16},{12,20},{16,8},{20,12},{24,0},{28,4},{1,25},{... | collective-permute-start | bytes 245768 | tf_op jit(solution)/shard_map/ppermute | solution.py:279
  39.8 5.6 %collective-permute-start.18 = (bf16[32,1280]{1,0:T(8,128)(2,1)S(1)}, bf16[32,1280]{1,0:T(8,128)(2,1)S(1)}, u32[]{:S(2)}, u32[]{:S(2)}) collective-permute-start(bf16[32,1280]{1,0:T(8,128)(2,1)S(1)} %get-tuple-element.50), channel_id=1, source_target_pairs={{0,28},{4,24},{8,20},{12,16},{16,12},{20,8},{24,4},{28,0},{1,29},{... | collective-permute-start | bytes 245768 | tf_op jit(solution)/shard_map/ppermute | solution.py:279
  39.9 6.8 %collective-permute-start.12 = (bf16[32,1280]{1,0:T(8,128)(2,1)S(1)}, bf16[32,1280]{1,0:T(8,128)(2,1)S(1)}, u32[]{:S(2)}, u32[]{:S(2)}) collective-permute-start(bf16[32,1280]{1,0:T(8,128)(2,1)S(1)} %get-tuple-element.43), channel_id=1, source_target_pairs={{0,20},{4,16},{8,28},{12,24},{16,4},{20,0},{24,12},{28,8},{1,21},{... | collective-permute-start | bytes 245768 | tf_op jit(solution)/shard_map/ppermute | solution.py:279
  41.7 5.0 %collective-permute-start.13 = (bf16[32,1280]{1,0:T(8,128)(2,1)S(1)}, bf16[32,1280]{1,0:T(8,128)(2,1)S(1)}, u32[]{:S(2)}, u32[]{:S(2)}) collective-permute-start(bf16[32,1280]{1,0:T(8,128)(2,1)S(1)} %get-tuple-element.44), channel_id=1, source_target_pairs={{0,12},{4,8},{8,4},{12,0},{16,28},{20,24},{24,20},{28,16},{1,13},{... | collective-permute-start | bytes 245768 | tf_op jit(solution)/shard_map/ppermute | solution.py:279
